TPU v7x, 32 devices: a whole 2x2x4 slice. The times are simulated.
32 devices in a mesh: seq: 8 (over y, x, core), fsdp: 4 (over z).
Axes of the slice: x: 2, y: 2, z: 4, core: 2. Of those that a mesh axis runs over, the one named last changes fastest.
Arguments:
- block_in: bfloat16 [4096, 1536], P(('seq', 'fsdp')), may hold values from -6 to 6
- norm_gain: float32 [1536], replicated, may hold values from 0.5 to 1.5
- in_weight: bfloat16 [1536, 6448], P('fsdp'), may hold values from -0.15625 to 0.15625
- conv_inner_weight: float32 [4, 48, 64], P(None, 'seq', 'fsdp'), may hold values from -3 to 3
- conv_inner_bias: float32 [48, 64], P('seq', 'fsdp'), may hold values from -3 to 3
- conv_pair_weight: float32 [4, 256], replicated, may hold values from -3 to 3
- conv_pair_bias: float32 [256], replicated, may hold values from -3 to 3
- step_bias: float32 [48], P('seq'), may hold values from -6 to -1
- decay_log: float32 [48], P('seq'), may hold values from 0 to 2.77
- skip_gain: float32 [48], P('seq'), may hold values from 0.5 to 1.5
- gate_gain: float32 [48, 64], P('seq', 'fsdp'), may hold values from 0.5 to 1.5
- out_weight: bfloat16 [3072, 1536], P(None, 'fsdp'), may hold values from -0.109375 to 0.109375
- cotangent: bfloat16 [4096, 1536], P(('seq', 'fsdp')), may hold values from -6 to 6
Outputs:
- block_out: bfloat16 [4096, 1536], P(('seq', 'fsdp'))
- grad_input: bfloat16 [4096, 1536], P(('seq', 'fsdp'))
- grad_norm_gain: float32 [1536], replicated
- grad_in_weight: float32 [1536, 6448], P('fsdp')
- grad_conv_inner_weight: float32 [4, 48, 64], P(None, 'seq', 'fsdp')
- grad_conv_inner_bias: float32 [48, 64], P('seq', 'fsdp')
- grad_conv_pair_weight: float32 [4, 256], replicated
- grad_conv_pair_bias: float32 [256], replicated
- grad_step_bias: float32 [48], P('seq')
- grad_decay_log: float32 [48], P('seq')
- grad_skip_gain: float32 [48], P('seq')
- grad_gate_gain: float32 [48, 64], P('seq', 'fsdp')
- grad_out_weight: float32 [3072, 1536], P(None, 'fsdp')
All inputs are finite; a program needn't handle non-finite values.
Results may differ from a plain program's by a relative error of at most 0.015.
The roundings to bfloat16 on the way count: a program that leaves them out, or rounds other values in their place, can miss the bound.
Values may be sent and summed in bfloat16 or wider, within the bound.
No kernel may reach another device: no remote copies, remote signals or barrier semaphores. Data moves between devices by JAX's collectives and lax.ppermute only.
A program may use at most 384 MiB of HBM per device.

v0:
```python
import functools

import jax
import jax.numpy as jnp
from jax import lax
from jax.experimental import pallas as pl
from jax.experimental.pallas import tpu as pltpu
from jax.sharding import PartitionSpec as P


H = 48
P_SIZE = 64
N = 128
KW = 4
Q = 256

norm_epsilon = 1e-05
far_below = -1e30
highest = lax.Precision.HIGHEST
f32 = jnp.float32
bf16 = jnp.bfloat16
everyone = ("seq", "fsdp")


def spread(value, axis, count):
    copies = jnp.broadcast_to(value[None], (count,) + value.shape)
    return lax.all_to_all(copies, axis, 0, 0, tiled=True)


def dot_f32(left, right, dims, batch=((), ())):
    return lax.dot_general(left, right, (dims, batch), preferred_element_type=f32)


def mm(left, right, dims, precision=None):
    return lax.dot_general(
        left, right, (dims, ((), ())), preferred_element_type=f32, precision=precision
    )


def split3(value):
    first = value.astype(bf16)
    rest = value - first.astype(f32)
    second = rest.astype(bf16)
    return first, second, (rest - second.astype(f32)).astype(bf16)


def mm_ones(ones, value, dims, flip=False):
    ones = ones.astype(bf16)
    parts = [
        mm(part, ones, dims) if flip else mm(ones, part, dims) for part in reversed(split3(value))
    ]
    return sum(parts[1:], parts[0])


def lanes_of(width):
    return [(at, min(2 * P_SIZE, width - at)) for at in range(0, width, 2 * P_SIZE)]


def widen(per_head, width):
    rows = per_head.shape[0]
    out = []
    for at, wide in lanes_of(width):
        h = at // P_SIZE
        first = jnp.broadcast_to(per_head[:, h : h + 1], (rows, wide))
        if wide > P_SIZE:
            second = jnp.broadcast_to(per_head[:, h + 1 : h + 2], (rows, wide))
            lane = lax.broadcasted_iota(jnp.int32, (rows, wide), 1)
            first = jnp.where(lane < P_SIZE, first, second)
        out.append(first)
    return out[0] if len(out) == 1 else jnp.concatenate(out, axis=1)


def pick_heads(width):
    row = lax.broadcasted_iota(jnp.int32, (width, 8), 0)
    col = lax.broadcasted_iota(jnp.int32, (width, 8), 1)
    return ((row >= col * P_SIZE) & (row < (col + 1) * P_SIZE)).astype(f32)


def lower_ones(strict=False):
    row = lax.broadcasted_iota(jnp.int32, (Q, Q), 0)
    col = lax.broadcasted_iota(jnp.int32, (Q, Q), 1)
    return (row > col) if strict else (row >= col)


def upper_ones():
    row = lax.broadcasted_iota(jnp.int32, (Q, Q), 0)
    col = lax.broadcasted_iota(jnp.int32, (Q, Q), 1)
    return row <= col


def split_heads(value):
    if value.shape[1] == P_SIZE:
        return [value]
    lane = lax.broadcasted_iota(jnp.int32, value.shape, 1)
    zero = jnp.zeros_like(value)
    return [jnp.where(lane < P_SIZE, value, zero), jnp.where(lane < P_SIZE, zero, value)]


def soft_plus(value):
    small = jnp.exp(-jnp.abs(value))
    series = small * (1.0 - small * (0.5 - small * (1.0 / 3.0 - 0.25 * small)))
    return jnp.maximum(value, 0.0) + jnp.where(small < 0.01, series, jnp.log(1.0 + small))


def choose_half(spot_ref, mine_ref, other_ref, out_ref):
    half = pl.program_id(0) // (pl.num_programs(0) // 2)
    mine = half == spot_ref[1]

    @pl.when(mine)
    def _():
        out_ref[...] = mine_ref[...]

    @pl.when(jnp.logical_not(mine))
    def _():
        out_ref[...] = other_ref[...]


def to_halves(spot_ref, block, value, away_ref, mine_ref):
    mine = (block // (pl.num_programs(0) // 2)) == spot_ref[1]

    @pl.when(mine)
    def _():
        mine_ref[...] = value

    @pl.when(jnp.logical_not(mine))
    def _():
        away_ref[...] = value


def project_kernel(
    absolute, QW, spot_ref, mine_ref, other_ref, halo0_ref, halo1_ref, *refs
):
    count = (len(refs) - 23) // 2
    pieces = refs[: 2 * count]
    (
        cwx_ref, cwp_ref, heads_ref,
        x_ref, win_ref, wpair_ref, rawx_ref, rawp_ref, actx_ref, actp_ref, slopex_ref,
        slopep_ref, dt_ref, cum_ref, cumt_ref, stepin_ref, local_ref, total_ref, final_ref,
        state, whole, extx, extp,
    ) = refs[2 * count :]
    b = pl.program_id(0)
    GW = rawx_ref.shape[1]
    PH = N // count
    Dl = win_ref.shape[1] // count
    HA = pieces[0].shape[1] - PH

    @pl.when(b == 0)
    def _():
        def place(ref, at, rows, value):
            if absolute:
                ref[at : at + rows.stop - rows.start, cols] = value[far, rows]
            else:
                at = pl.multiple_of(at, 16)
                ref[pl.ds(at, rows.stop - rows.start), cols] = value[far, rows]

        for k in range(count):
            first, second = pieces[2 * k], pieces[2 * k + 1]
            here = k if absolute else spot_ref[0] ^ k
            for src in range(count):
                cols = slice(src * Dl, (src + 1) * Dl)
                far = lax.rem(spot_ref[2] - src + count, count)
                place(win_ref, here * QW, slice(0, HA), first)
                place(wpair_ref, here * 2 * PH, slice(HA, HA + PH), first)
                if HA < QW:
                    place(win_ref, here * QW + HA, slice(0, QW - HA), second)
                place(
                    wpair_ref, here * 2 * PH + PH, slice(QW - HA, QW - HA + PH), second
                )
                if k == 0:
                    win_ref[GW : GW + 8, cols] = second[far, QW - HA + PH : QW - HA + PH + 8]
        state[...] = jnp.zeros_like(state)
        whole[...] = jnp.zeros_like(whole)
        edge = halo0_ref[...] + halo1_ref[...]
        ex = mm(edge, win_ref[0:GW], ((1,), (1,))).astype(bf16).astype(f32)
        ep = mm(edge, wpair_ref[...], ((1,), (1,))).astype(bf16).astype(f32)
        extx[0:8] = ex[8:16]
        extp[0:8] = ep[8:16]

    @pl.when(b > 0)
    def _():
        extx[0:8] = extx[Q : Q + 8]
        extp[0:8] = extp[Q : Q + 8]

    choose_half(spot_ref, mine_ref, other_ref, x_ref)
    x = x_ref[...]
    rx = mm(x, win_ref[0:GW], ((1,), (1,))).astype(bf16)
    rp = mm(x, wpair_ref[...], ((1,), (1,))).astype(bf16)
    st = mm(x, win_ref[GW : GW + 8], ((1,), (1,))).astype(bf16).astype(f32)
    rawx_ref[...] = rx
    rawp_ref[...] = rp
    extx[8 : Q + 8] = rx.astype(f32)
    extp[8 : Q + 8] = rp.astype(f32)

    def conv(ext, cw, act_out, slope_out):
        pre = cw[KW : KW + 1, :]
        for k in range(KW):
            pre = pre + cw[k : k + 1, :] * ext[9 - KW + k : 9 - KW + k + Q]
        sig = jax.nn.sigmoid(pre)
        act_out[...] = (pre * sig).astype(bf16)
        slope_out[...] = (sig * (1.0 + pre * (1.0 - sig))).astype(bf16)

    conv(extx, cwx_ref, actx_ref, slopex_ref)
    conv(extp, cwp_ref, actp_ref, slopep_ref)
    step_in = st + heads_ref[0:1, 0:8]
    dt = soft_plus(step_in)
    ld = -dt * heads_ref[1:2, 0:8]
    cum = mm_ones(lower_ones().astype(f32), ld, ((1,), (0,)))
    dt_ref[...] = dt
    cum_ref[...] = cum
    stepin_ref[...] = step_in
    eye = (
        lax.broadcasted_iota(jnp.int32, (8, 8), 0) == lax.broadcasted_iota(jnp.int32, (8, 8), 1)
    ).astype(f32)
    cumt_ref[...] = mm(eye, cum, ((1,), (1,)), highest)
    total = cum[Q - 1 : Q]
    total_wide = widen(total, GW)
    total_ref[0] = jnp.broadcast_to(total_wide, (8, GW))
    u32 = actx_ref[...].astype(f32) * widen(dt, GW)
    uw = (u32 * widen(jnp.exp(total - cum), GW)).astype(bf16)
    local_ref[0] = state[...]
    state[...] = state[...] * jnp.exp(total_wide) + mm(actp_ref[:, 0:N], uw, ((0,), (0,)))
    whole[...] = whole[...] + total_wide

    @pl.when(b == pl.num_programs(0) - 1)
    def _():
        final_ref[0:N] = state[...]
        final_ref[N : N + 8] = whole[...]


def intra_kernel(spot_ref, actx_ref, actp_ref, dt_ref, cum_ref, cumt_ref, y_ref):
    GW = y_ref.shape[1]
    scores = mm(actp_ref[:, N : 2 * N], actp_ref[:, 0:N], ((1,), (1,)))
    causal = lower_ones()
    for at, wide in lanes_of(GW):
        u = (
            actx_ref[:, at : at + wide].astype(f32)
            * widen(dt_ref[...], GW)[:, at : at + wide]
        ).astype(bf16)
        mixes = []
        for h in range(at // P_SIZE, (at + wide) // P_SIZE):
            gap = cum_ref[:, h : h + 1] - cumt_ref[h : h + 1, :]
            mixes.append((scores * jnp.exp(jnp.where(causal, gap, far_below))).astype(bf16))
        y_ref[:, at : at + wide] = sum(
            mm(m, p, ((1,), (0,))) for m, p in zip(mixes, split_heads(u), strict=True)
        )


def merge_states(spot_ref, states, totals, forward):
    q = spot_ref[0]
    out = jnp.zeros(states[0].shape, f32)
    count = len(states) + 1
    for k in range(1, count):
        p = q ^ k
        between = jnp.zeros(totals[0].shape, f32)
        for j in range(1, count):
            if j != k:
                o = q ^ j
                inside = ((o > p) & (o < q)) if forward else ((o < p) & (o > q))
                between = between + totals[j - 1] * inside.astype(f32)
        reaches = (p < q) if forward else (p > q)
        out = out + states[k - 1] * (jnp.exp(between) * reaches.astype(f32))
    return out


def inter_kernel(
    spot_ref, actx_ref, actp_ref, cum_ref, total_ref, local_ref, y_ref, z_ref, bn_ref, rows_ref,
    *refs,
):
    finals = refs[:-5]
    yx_ref, states_ref, sums_ref, prefix, before_ref = refs[-5:]
    GW = y_ref.shape[1]

    @pl.when(pl.program_id(0) == 0)
    def _():
        prefix[...] = jnp.zeros_like(prefix)
        before_ref[...] = merge_states(
            spot_ref, [r[0:N] for r in finals], [r[N : N + 1] for r in finals], True
        )

    low = (local_ref[0] + jnp.exp(prefix[0:1]) * before_ref[...]).astype(bf16)
    prefix[...] = prefix[...] + total_ref[0]
    states_ref[0] = low
    yx = mm(actp_ref[:, N : 2 * N], low, ((1,), (0,))) * widen(jnp.exp(cum_ref[...]), GW)
    yx_ref[...] = yx
    mixer = y_ref[...] + yx + rows_ref[1:2] * actx_ref[...].astype(f32)
    z = z_ref[...].astype(f32)
    gated = mixer * (z * jax.nn.sigmoid(z))
    row = lax.broadcasted_iota(jnp.int32, (8, GW), 0)
    squares = mm_ones((row == 0).astype(f32), gated * gated, ((1,), (1,)))
    cross = mm_ones(
        (row == 1).astype(f32), bn_ref[...].astype(f32) * rows_ref[0:1] * gated, ((1,), (1,))
    )
    sums_ref[...] = squares + cross


def gate_kernel(
    spot_ref, actx_ref, actp_ref, cum_ref, total_ref, y_ref, yx_ref, z_ref, bn_ref, rows_ref, *refs
):
    sums = sum(r[...] for r in refs[:-10])
    out_rows_ref, gn_ref, bgate_ref, dy_ref, local_ref, first_ref, small_ref = refs[-10:-3]
    away_ref, mine_ref, state = refs[-3:]
    GW = y_ref.shape[1]
    b = pl.program_id(0)

    @pl.when(b == 0)
    def _():
        state[...] = jnp.zeros_like(state)
        small_ref[...] = jnp.zeros_like(small_ref)

    eye = (
        lax.broadcasted_iota(jnp.int32, (8, 8), 0) == lax.broadcasted_iota(jnp.int32, (8, 8), 1)
    ).astype(f32)
    cols = mm(sums, eye, ((0,), (0,)), highest)
    scale = lax.rsqrt(cols[:, 0:1] * rows_ref[2:3, 0:1] + norm_epsilon)
    cross = cols[:, 1:2] * scale * scale * scale * rows_ref[2:3, 0:1]
    x = actx_ref[...].astype(f32)
    mixer = y_ref[...] + yx_ref[...] + rows_ref[1:2] * x
    z = z_ref[...].astype(f32)
    sig = jax.nn.sigmoid(z)
    silu = z * sig
    gated = mixer * silu
    bn = bn_ref[...].astype(f32)
    gain = rows_ref[0:1]
    gn = (gated * scale * gain).astype(bf16)
    gn_ref[...] = gn
    to_halves(
        spot_ref,
        pl.num_programs(0) - 1 - b,
        mm(gn, out_rows_ref[...], ((1,), (0,))).astype(bf16),
        away_ref,
        mine_ref,
    )
    back_gated = scale * (bn * gain) - gated * cross
    dy = (back_gated * silu).astype(bf16)
    dy_ref[...] = dy
    bgate_ref[...] = (back_gated * mixer * sig * (1.0 + z * (1.0 - sig))).astype(bf16)
    dyf = dy.astype(f32)
    small_ref[0:1] += jnp.sum(bn * gated * scale, axis=0, keepdims=True)
    small_ref[1:2] += jnp.sum(dyf * x, axis=0, keepdims=True)
    dyh = (dyf * widen(jnp.exp(cum_ref[...]), GW)).astype(bf16)
    local_ref[0] = state[...]
    state[...] = state[...] * jnp.exp(total_ref[0, 0:1]) + mm(
        actp_ref[:, N : 2 * N], dyh, ((0,), (0,))
    )

    @pl.when(b == pl.num_programs(0) - 1)
    def _():
        first_ref[...] = state[...]


def back_intra_kernel(
    spot_ref, actx_ref, actp_ref, dt_ref, cum_ref, cumt_ref, dy_ref, states_ref,
    du_ref, dbc_ref,
):
    GW = dy_ref.shape[1]
    bs = actp_ref[:, 0:N]
    cs = actp_ref[:, N : 2 * N]
    scores = mm(cs, bs, ((1,), (1,)))
    causal = lower_ones()
    dscores = jnp.zeros((Q, Q), f32)
    dt_wide = widen(dt_ref[...], GW)
    for at, wide in lanes_of(GW):
        u = (actx_ref[:, at : at + wide].astype(f32) * dt_wide[:, at : at + wide]).astype(bf16)
        du = jnp.zeros((Q, wide), f32)
        for k, dyk in enumerate(split_heads(dy_ref[:, at : at + wide])):
            h = at // P_SIZE + k
            gap = cum_ref[:, h : h + 1] - cumt_ref[h : h + 1, :]
            decay = jnp.exp(jnp.where(causal, gap, far_below))
            mix = (scores * decay).astype(bf16)
            dscores = dscores + mm(dyk, u, ((1,), (1,))) * decay
            du = du + mm(mix, dyk, ((0,), (0,)))
        du_ref[:, at : at + wide] = du
    dlow = dscores.astype(bf16)
    dyh = (dy_ref[...].astype(f32) * widen(jnp.exp(cum_ref[...]), GW)).astype(bf16)
    dbc_ref[:, 0:N] = mm(dlow, cs, ((0,), (0,)))
    dbc_ref[:, N : 2 * N] = mm(dlow, bs, ((1,), (0,))) + mm(dyh, states_ref[0], ((1,), (1,)))


def back_inter_kernel(
    spot_ref, actx_ref, actp_ref, slopex_ref, slopep_ref, dt_ref, cum_ref, stepin_ref, total_ref, whole_ref,
    local_ref, states_ref, dy_ref, y_ref, yx_ref, du_ref, dbc_ref, heads_ref, rows_ref, *refs,
):
    others, refs = refs[:-7], refs[-7:]
    dprex_ref, dprep_ref, dstep_ref, hsum_ref, edge_ref, seen, after_ref = refs
    finals, firsts = others[: len(others) // 2], others[len(others) // 2 :]
    GW = dy_ref.shape[1]
    b = pl.program_id(0)

    @pl.when(b == 0)
    def _():
        seen[...] = jnp.zeros_like(seen)
        hsum_ref[...] = jnp.zeros_like(hsum_ref)
        after_ref[...] = merge_states(
            spot_ref, [r[...] for r in firsts], [r[N : N + 1] for r in finals], False
        )

    seen[...] = seen[...] + total_ref[0]
    left = jnp.exp(whole_ref[0:1] - seen[0:1])
    grown = local_ref[0] + left * after_ref[...]
    low = grown.astype(bf16)
    cum = cum_ref[...]
    total = cum[Q - 1 : Q]
    dt = dt_ref[...]
    dt_wide = widen(dt, GW)
    tail = widen(jnp.exp(total - cum), GW)
    x = actx_ref[...].astype(f32)
    u32 = x * dt_wide
    ub = u32.astype(bf16).astype(f32)
    uw = (u32 * tail).astype(bf16)
    bs = actp_ref[:, 0:N]
    du_inter = mm(bs, low, ((1,), (0,))) * tail
    dui = du_ref[...]
    du = dui + du_inter
    dy = dy_ref[...].astype(f32)
    dprex_ref[...] = (du * dt_wide + rows_ref[1:2] * dy) * slopex_ref[...].astype(f32)
    db = dbc_ref[:, 0:N] + mm(uw, low, ((1,), (1,)))
    dprep_ref[:, 0:N] = db * slopep_ref[:, 0:N].astype(f32)
    dprep_ref[:, N : 2 * N] = dbc_ref[:, N : 2 * N] * slopep_ref[:, N : 2 * N].astype(f32)

    @pl.when(b == 0)
    def _():
        edge_ref[:, 0:GW] = dprex_ref[0:8]
        edge_ref[:, GW:] = dprep_ref[0:8]

    sel = pick_heads(GW)
    ddt = mm_ones(sel, x * du, ((1,), (0,)), True)
    later = mm_ones(sel, dy * (y_ref[...] + yx_ref[...]) - ub * dui, ((1,), (0,)), True)
    earlier = mm_ones(sel, u32 * du_inter, ((1,), (0,)), True)
    over = jnp.sum(grown * states_ref[0].astype(f32), axis=0, keepdims=True)
    over = mm(jnp.broadcast_to(over, (8, GW)), sel, ((1,), (0,)), highest)[0:1] * jnp.exp(total)
    dld = (
        mm_ones(upper_ones().astype(f32), later, ((1,), (0,)))
        + mm_ones(lower_ones(True).astype(f32), earlier, ((1,), (0,)))
        + over
    )
    rate = heads_ref[1:2, 0:8]
    dstep = (ddt - rate * dld) * jax.nn.sigmoid(stepin_ref[...])
    dstep_ref[...] = dstep
    hsum_ref[0:1] += jnp.sum(dstep, axis=0, keepdims=True)
    hsum_ref[1:2] += jnp.sum(-dld * dt * rate, axis=0, keepdims=True)


def back_conv_kernel(
    spot_ref, dprex_ref, dprep_ref, nextx_ref, nextp_ref, halo_ref, rawx_ref, rawp_ref,
    cwx_ref, cwp_ref, bgate_ref, step_ref, x_ref, wgate_ref, win_ref,
    backx_ref, pair_away_ref, pair_mine_ref, gradx_ref, gradp_ref, away_ref, mine_ref, gain_ref,
    extx, extp,
):
    b = pl.program_id(0)
    last = b == pl.num_programs(0) - 1

    @pl.when(b == 0)
    def _():
        gradx_ref[...] = jnp.zeros_like(gradx_ref)
        gradp_ref[...] = jnp.zeros_like(gradp_ref)
        gain_ref[...] = jnp.zeros_like(gain_ref)

    def conv(dpre, following, halo, raw, cw, ext, grad):
        ext[0:Q] = dpre[...]
        ext[Q : Q + 8] = jnp.where(last, halo, following[...])
        value = raw[...].astype(f32)
        total = jnp.zeros(dpre.shape, f32)
        for k in range(KW):
            shifted = ext[KW - 1 - k : KW - 1 - k + Q]
            total = total + cw[k : k + 1, :] * shifted
            grad[k : k + 1] += jnp.sum(value * shifted, axis=0, keepdims=True)
        grad[KW : KW + 1] += jnp.sum(dpre[...], axis=0, keepdims=True)
        return total.astype(bf16)

    GW = dprex_ref.shape[1]
    inner = conv(dprex_ref, nextx_ref, halo_ref[:, 0:GW], rawx_ref, cwx_ref, extx, gradx_ref)
    backx_ref[...] = inner
    pair = conv(dprep_ref, nextp_ref, halo_ref[:, GW:], rawp_ref, cwp_ref, extp, gradp_ref)
    to_halves(spot_ref, b, pair, pair_away_ref, pair_mine_ref)
    value = mm(bgate_ref[...], wgate_ref[...], ((1,), (0,)))
    value = value + mm(step_ref[...].astype(bf16), win_ref[GW : GW + 8], ((1,), (0,)))
    value = value + mm(inner, win_ref[0:GW], ((1,), (0,)))
    gain_ref[0:1] += jnp.sum(value * x_ref[...].astype(f32), axis=0, keepdims=True)
    to_halves(spot_ref, b, value.astype(bf16), away_ref, mine_ref)


def cotangent_kernel(absolute, spot_ref, mine_ref, other_ref, x_ref, *refs):
    pieces = refs[:-5]
    cot_ref, gate_rows_ref, rows_ref, z_ref, bn_ref = refs[-5:]
    count = len(pieces)
    QW = rows_ref.shape[0] // count
    Dl = rows_ref.shape[1] // count

    @pl.when(pl.program_id(0) == 0)
    def _():
        for k, piece in enumerate(pieces):
            for src in range(count):
                cols = slice(src * Dl, (src + 1) * Dl)
                far = lax.rem(spot_ref[2] - src + count, count)
                if absolute:
                    gate_rows_ref[k * QW : (k + 1) * QW, cols] = piece[far, 0:QW]
                    rows_ref[k * QW : (k + 1) * QW, cols] = piece[far, QW : 2 * QW]
                else:
                    at = pl.multiple_of((spot_ref[0] ^ k) * QW, 16)
                    gate_rows_ref[pl.ds(at, QW), cols] = piece[far, 0:QW]
                    rows_ref[pl.ds(at, QW), cols] = piece[far, QW : 2 * QW]

    choose_half(spot_ref, mine_ref, other_ref, cot_ref)
    z_ref[...] = mm(x_ref[...], gate_rows_ref[...], ((1,), (1,))).astype(bf16)
    bn_ref[...] = mm(cot_ref[...], rows_ref[...], ((1,), (1,))).astype(bf16)


def partial_blocks_kernel(count, pairs, spot_ref, *refs):
    lefts, rights = refs[:pairs], refs[pairs : 2 * pairs]
    step_ref = refs[2 * pairs] if pairs == 1 else None
    outs, turned, total = refs[-count - 2 : -2], refs[-2], refs[-1]
    GW = total.shape[0]
    QW = GW // count

    @pl.when(pl.program_id(0) == 0)
    def _():
        for at in range(pairs):
            turned[at] = lefts[at][...].T

    for at in range(pairs):
        right = rights[at][...]
        total[...] = mm(turned[at], right, ((1,), (0,)))
        for k in range(count):
            start = pl.multiple_of((spot_ref[0] ^ k) * QW, 8)
            outs[k][0, at * QW : (at + 1) * QW] = total[pl.ds(start, QW)].astype(bf16)
    if step_ref is not None:
        value = mm(step_ref[...].astype(bf16), rights[0][...], ((0,), (0,)))
        for k in range(count):
            keep = ((spot_ref[0] ^ k) == 0).astype(f32)
            outs[k][0, QW : QW + 8] = (value * keep).astype(bf16)


def partial_kernel(count, pairs, spot_ref, *refs):
    lefts, rights = refs[:pairs], refs[pairs : 2 * pairs]
    step_ref = refs[2 * pairs] if pairs == 1 else None
    outs = refs[len(refs) - count - pairs - (pairs == 1) : len(refs) - pairs - (pairs == 1)]
    sums = refs[len(refs) - pairs - (pairs == 1) :]
    b = pl.program_id(0)
    lefts = [r[...] for r in lefts]
    rights = [r[...] for r in rights]
    if step_ref is not None:
        lefts.append(step_ref[...].astype(bf16))
        rights.append(rights[0])
    for left, right, total in zip(lefts, rights, sums, strict=True):
        value = mm(left, right, ((0,), (0,)))

        @pl.when(b == 0)
        def _(value=value, total=total):
            total[...] = value

        @pl.when(b > 0)
        def _(value=value, total=total):
            total[...] += value

    @pl.when(b == pl.num_programs(0) - 1)
    def _():
        GW, D = sums[0].shape
        QW, Dl = GW // count, D // count
        for k in range(count):
            part = spot_ref[0] ^ k
            start = pl.multiple_of(part * QW, 8)
            for j in range(count):
                cols = slice(j * Dl, (j + 1) * Dl)
                for at in range(pairs):
                    outs[k][j, at * QW : (at + 1) * QW] = sums[at][pl.ds(start, QW), cols].astype(
                        bf16
                    )
                if step_ref is not None:
                    keep = (part == 0).astype(f32)
                    outs[k][j, QW : QW + 8] = (sums[1][:, cols] * keep).astype(bf16)


def sum_kernel(outs_count, spot_ref, *refs):
    i = pl.program_id(0)
    outs = refs[len(refs) - outs_count :]
    total = sum(r[0].astype(f32) for r in refs[: len(refs) - outs_count]).astype(bf16)
    for k, out in enumerate(outs):

        @pl.when(i == k)
        def _(out=out):
            out[...] = total


def place_rows(count, spot_ref, step, own, other, rows, out_ref):
    q, c, f = spot_ref[0], spot_ref[1], spot_ref[2]
    far = lax.rem(f - lax.rem(step, count) + count, count)
    width = rows.stop - rows.start
    for side in range(2):
        owner = c if side == 0 else 1 - c

        @pl.when((step >= owner * count) & (step < (owner + 1) * count))
        def _(side=side):
            for k in range(count):
                value = own[k][far, rows] if side == 0 else other[k, far, rows]
                out_ref[pl.ds(pl.multiple_of((q ^ k) * width, 8), width)] = value.astype(f32)


def early_grads_kernel(count, spot_ref, *refs):
    own, other, in_ref, out_ref = refs[:count], refs[count], refs[-2], refs[-1]
    QW = own[0].shape[1] // 2
    step = pl.program_id(0)
    place_rows(count, spot_ref, step, own, other, slice(0, QW), out_ref)
    place_rows(count, spot_ref, step, own, other, slice(QW, 2 * QW), in_ref)


def pair_grads_kernel(spot_ref, pair_ref, array_ref, out_ref):
    out_ref[...] = pair_ref[...]


def late_grads_kernel(count, QW, heads, spot_ref, *refs):
    own, other, in_ref = refs[:count], refs[count], refs[-1]
    step = pl.program_id(0)
    place_rows(count, spot_ref, step, own, other, slice(0, QW), in_ref)
    q, c, f = spot_ref[0], spot_ref[1], spot_ref[2]
    GW = in_ref.shape[0]
    groups = 2 * count
    for block in range(-(-(2 * N + H) // GW)):

        @pl.when(step == groups + block)
        def _(block=block):
            first = block * GW
            for k in range(count):

                @pl.when((q ^ k) == 0)
                def _(k=k):
                    for g in range(groups):
                        at = 2 * N + g * heads - first
                        if at < 0 or at >= GW:
                            continue
                        far = lax.rem(f - g % count + count, count)
                        mine = own[k][far, QW : QW + 8].astype(f32)
                        theirs = other[k, far, QW : QW + 8].astype(f32)
                        value = jnp.where(c == g // count, mine, theirs)
                        in_ref[at : at + heads] = value[0:heads]


def body(
    block_in,
    norm_gain,
    in_weight,
    conv_inner_weight,
    conv_inner_bias,
    conv_pair_weight,
    conv_pair_bias,
    step_bias,
    decay_log,
    skip_gain,
    gate_gain,
    out_weight,
    cotangent,
):
    S = lax.axis_size("seq")
    F = lax.axis_size("fsdp")
    devices = S * F
    R = S // F
    s = lax.axis_index("seq")
    f = lax.axis_index("fsdp")
    q = s // R
    c = s % R
    member = c * F + f
    spot = jnp.stack([q, c, f]).astype(jnp.int32)
    tokens, D = block_in.shape
    TL = tokens * S
    blocks = TL // Q
    half = blocks // 2
    HG = H // S
    GW = HG * P_SIZE
    QW = GW // F
    DI = H * P_SIZE
    Dl = in_weight.shape[0]
    PF = P_SIZE // F
    NP = 2 * N
    PH = N // F
    absolute = QW % 16 != 0 or PH % 16 != 0
    twins = [(i, i ^ 1) for i in range(S)]
    back = [(i + R, i) for i in range(S - R)]
    bits = [1 << i for i in range(F.bit_length() - 1)]
    struct = jax.ShapeDtypeStruct

    def twin(value):
        return lax.ppermute(value, "seq", twins)

    def from_part(value, k):
        return lax.ppermute(value, "seq", [(i, i ^ (k * R)) for i in range(S)])

    def from_line(value, k):
        return lax.ppermute(value, "fsdp", [(i, (i + k) % F) for i in range(F)])

    def take(value, at, axis=0):
        return lax.dynamic_index_in_dim(value, at, axis, keepdims=False)

    def line_chain(value):
        up, down, ups, downs = value, value, [], []
        for k in range(1, F):
            up = lax.ppermute(up, "fsdp", [(i, i + 1) for i in range(k - 1, F - 1)])
            down = lax.ppermute(down, "fsdp", [(i, i - 1) for i in range(1, F - k + 1)])
            ups.append(up)
            downs.append(down)
        line = []
        for j in range(F):
            here = value
            for k in range(1, F):
                if j + k < F:
                    here = jnp.where(f == j + k, ups[k - 1], here)
                if j - k >= 0:
                    here = jnp.where(f == j - k, downs[k - 1], here)
            line.append(here)
        return jnp.concatenate(line, axis=0)

    def line_ordered(rel):
        line = []
        for j in range(F):
            here = rel[0]
            for k in range(1, F):
                here = jnp.where(lax.rem(f - k + F, F) == j, rel[k], here)
            line.append(here)
        return jnp.concatenate(line, axis=0)

    def gather_parts(value, order):
        pieces = {0: value}
        for bit in order:
            pieces.update({k ^ bit: from_part(v, bit) for k, v in list(pieces.items())})
        return [pieces[k] for k in range(F)]

    def in_order(pieces):
        if not absolute:
            return pieces
        out = []
        for j in range(F):
            here = pieces[0]
            for k in range(1, F):
                here = jnp.where(q == (j ^ k), pieces[k], here)
            out.append(here)
        return out

    def rows_of(width, shift=0):
        return pl.BlockSpec((Q, width), lambda i, p: (i + shift, 0))

    def rows_back(width):
        return pl.BlockSpec((Q, width), lambda i, p: (blocks - 1 - i, 0))

    def rows_half(width):
        return pl.BlockSpec((Q, width), lambda i, p: (lax.rem(i, half), 0))

    def fixed(*shape):
        return pl.BlockSpec(shape, lambda i, p: (0,) * len(shape))

    def per_block(rows, width, shift=0):
        return pl.BlockSpec((1, rows, width), lambda i, p: (i + shift, 0, 0))

    def per_block_back(rows, width):
        return pl.BlockSpec((1, rows, width), lambda i, p: (blocks - 1 - i, 0, 0))

    def half_of(width, own):
        def index(i, p):
            return (
                jnp.where(p[1] == own, jnp.maximum(i - half, 0), jnp.minimum(i, half - 1)), 0
            )

        return pl.BlockSpec((Q, width), index)

    def half_of_back(width, own):
        def index(i, p):
            at = blocks - 1 - i
            return (
                jnp.where(p[1] == own, jnp.maximum(at - half, 0), jnp.minimum(at, half - 1)), 0
            )

        return pl.BlockSpec((Q, width), index)

    across = pl.BlockSpec((8, Q), lambda i, p: (0, i))
    across_back = pl.BlockSpec((8, Q), lambda i, p: (0, blocks - 1 - i))
    anywhere = pl.BlockSpec(memory_space=pl.ANY)

    def call(kernel, steps, in_specs, out_specs, out_shape, scratch=(), aliases=None):
        return pl.pallas_call(
            kernel,
            grid_spec=pltpu.PrefetchScalarGridSpec(
                num_scalar_prefetch=1,
                grid=(steps,),
                in_specs=in_specs,
                out_specs=out_specs,
                scratch_shapes=list(scratch),
            ),
            out_shape=out_shape,
            input_output_aliases=aliases or {},
            compiler_params=pltpu.CompilerParams(dimension_semantics=("arbitrary",)),
        )

    small = jnp.concatenate(
        [
            conv_inner_weight.reshape(KW, HG * PF),
            conv_inner_bias.reshape(1, HG * PF),
            gate_gain.reshape(1, HG * PF),
        ],
        axis=0,
    )
    small = jnp.pad(small, ((0, 0), (0, 128 - HG * PF)))
    heads_row = jnp.concatenate([step_bias, decay_log, skip_gain])
    heads_row = jnp.pad(heads_row, (0, 128 - 3 * HG))[None]
    small = jnp.concatenate([small, heads_row, jnp.zeros((1, 128), f32)], axis=0)
    small_all = spread(small, everyone, devices)
    small_here = lax.dynamic_slice(small_all, (member * F, 0, 0), (F, 8, 128))
    chan = small_here[:, : KW + 2, : HG * PF].reshape(F, KW + 2, HG, PF)
    chan = jnp.transpose(chan, (1, 2, 0, 3)).reshape(KW + 2, GW)
    heads_here = small_here[0, KW + 2]
    bias_h = heads_here[:HG]
    rate_h = jnp.exp(heads_here[HG : 2 * HG])
    skip_h = heads_here[2 * HG : 3 * HG]

    hidden = block_in.astype(f32)
    inverse_scale = lax.rsqrt(jnp.mean(hidden * hidden, axis=1, keepdims=True) + norm_epsilon)
    normed = (hidden * inverse_scale * norm_gain[None, :]).astype(bf16)
    x_line = line_chain(normed)
    x_other = twin(x_line)
    last_rows = x_line[F * tokens - 16 :]
    edge_own = lax.ppermute(last_rows, "seq", [(i, i + R) for i in range(S - R) if i % R == R - 1])
    edge_twin = lax.ppermute(last_rows, "seq", [(i, i + 1) for i in range(S - R) if i % R == R - 1])

    columns = jnp.transpose(in_weight)
    HA = QW // 2 if QW % 32 == 0 else QW

    def rows_for(place):
        group = c * F + place
        inner = lax.dynamic_slice(columns, (DI + group * GW + q * QW, 0), (QW, Dl))
        pair = lax.dynamic_slice(columns, (2 * DI + q * 2 * PH, 0), (2 * PH, Dl))
        step = lax.dynamic_slice(columns, (2 * DI + NP + group * HG, 0), (HG, Dl))
        step = jnp.pad(step, ((0, 8 - HG), (0, 0)))
        return jnp.concatenate([inner[:HA], pair[:PH], inner[HA:], pair[PH:], step], axis=0)

    def later_rows_for(place):
        group = c * F + place
        gate_part = lax.dynamic_slice(columns, (group * GW + q * QW, 0), (QW, Dl))
        out_part = lax.dynamic_slice(out_weight, (group * GW + q * QW, 0), (QW, Dl))
        return jnp.concatenate([gate_part, out_part], axis=0)

    def line_rows(pick):
        return [pick(f)] + [from_line(pick(lax.rem(f + k, F)), k) for k in range(1, F)]

    first_rows = line_rows(rows_for)
    rows_a = jnp.stack([value[: HA + PH] for value in first_rows])
    rows_b = jnp.stack([value[HA + PH :] for value in first_rows])
    if F == 4:
        beside_a, beside_b = from_part(rows_a, 1), from_part(rows_b, 2)
        pieces_a = [rows_a, beside_a, from_part(rows_a, 2), from_part(beside_a, 2)]
        pieces_b = [rows_b, from_part(rows_b, 1), beside_b, from_part(beside_b, 1)]
    else:
        pieces_a, pieces_b = gather_parts(rows_a, bits), gather_parts(rows_b, bits)
    pieces_a, pieces_b = in_order(pieces_a), in_order(pieces_b)

    later = line_rows(later_rows_for)
    later = jnp.stack(later)
    cot_rel = [from_line(cotangent, k) for k in range(1, F)]

    conv_x = jnp.concatenate([chan[: KW + 1], jnp.zeros((7 - KW, GW), f32)], axis=0)
    conv_p = jnp.concatenate(
        [conv_pair_weight, conv_pair_bias[None], jnp.zeros((7 - KW, NP), f32)], axis=0
    )
    heads = jnp.pad(jnp.stack([bias_h, rate_h]), ((0, 6), (0, 128 - HG)))
    wide_rows = jnp.concatenate(
        [
            chan[KW + 1][None],
            jnp.repeat(skip_h, P_SIZE)[None],
            jnp.full((1, GW), 1.0 / DI, f32),
            jnp.zeros((5, GW), f32),
        ],
        axis=0,
    )
    weight_pieces = [piece for pair in zip(pieces_a, pieces_b, strict=True) for piece in pair]
    (
        x_group, in_rows, pair_in, rawx, rawp, actx, actp, slopex, slopep, dt, cum, cumt,
        step_in, local, total, final,
    ) = call(
        functools.partial(project_kernel, absolute, QW),
        blocks,
        [rows_half(D), rows_half(D), fixed(16, D), fixed(16, D)]
        + [fixed(F, HA + PH, Dl), fixed(F, QW - HA + PH + 8, Dl)] * F
        + [fixed(8, GW), fixed(8, NP), fixed(8, 128)],
        [
            rows_of(D), fixed(GW + 8, D), fixed(NP, D),
            rows_of(GW), rows_of(NP), rows_of(GW), rows_of(NP), rows_of(GW),
            rows_of(NP), rows_of(8), rows_of(8), across, rows_of(8), per_block(N, GW),
            per_block(8, GW), fixed(N + 8, GW),
        ],
        [
            struct((TL, D), bf16), struct((GW + 8, D), bf16), struct((NP, D), bf16),
            struct((TL, GW), bf16), struct((TL, NP), bf16),
            struct((TL, GW), bf16), struct((TL, NP), bf16), struct((TL, GW), bf16),
            struct((TL, NP), bf16), struct((TL, 8), f32), struct((TL, 8), f32),
            struct((8, TL), f32), struct((TL, 8), f32), struct((blocks, N, GW), f32),
            struct((blocks, 8, GW), f32), struct((N + 8, GW), f32),
        ],
        [
            pltpu.VMEM((N, GW), f32), pltpu.VMEM((8, GW), f32),
            pltpu.VMEM((Q + 8, GW), f32), pltpu.VMEM((Q + 8, NP), f32),
        ],
    )(spot, x_line, x_other, edge_own, edge_twin, *weight_pieces, conv_x, conv_p, heads)

    finals = [from_part(final, k) for k in range(1, F)]
    later_pieces = in_order([later] + [from_part(later, k) for k in range(1, F)])
    *cot_rel, final_low = lax.optimization_barrier((*cot_rel, final[:8]))
    cot_line = line_ordered([cotangent] + cot_rel)
    cot_other = twin(cot_line)
    y_intra = call(
        intra_kernel,
        blocks,
        [rows_of(GW), rows_of(NP), rows_of(8), rows_of(8), across],
        rows_of(GW),
        struct((TL, GW), f32),
    )(spot, actx, actp, dt, cum, cumt)
    cot_group, gate_rows, out_rows, gate, back_normed = call(
        functools.partial(cotangent_kernel, absolute),
        blocks,
        [rows_half(D), rows_half(D), rows_of(D)] + [fixed(F, 2 * QW, Dl)] * F,
        [rows_of(D), fixed(GW, D), fixed(GW, D), rows_of(GW), rows_of(GW)],
        [
            struct((TL, D), bf16), struct((GW, D), bf16), struct((GW, D), bf16),
            struct((TL, GW), bf16), struct((TL, GW), bf16),
        ],
    )(spot, cot_line, cot_other, x_group, *later_pieces)
    y_inter, states, sums = call(
        inter_kernel,
        blocks,
        [
            rows_of(GW), rows_of(NP), rows_of(8), per_block(8, GW), per_block(N, GW),
            rows_of(GW), rows_of(GW), rows_of(GW), fixed(8, GW),
        ]
        + [fixed(N + 8, GW)] * (F - 1),
        [rows_of(GW), per_block(N, GW), across],
        [struct((TL, GW), f32), struct((blocks, N, GW), bf16), struct((8, TL), f32)],
        [pltpu.VMEM((8, GW), f32), pltpu.VMEM((N, GW), f32)],
    )(spot, actx, actp, cum, total, local, y_intra, gate, back_normed, wide_rows, *finals)

    sums = sums + twin(sums)
    sums = [sums] + [from_line(sums, k) for k in range(1, F)]
    gated_normed, back_gate, dy, local_back, first_back, small_sums, away, mine = call(
        gate_kernel,
        blocks,
        [
            rows_back(GW), rows_back(NP), rows_back(8), per_block_back(8, GW), rows_back(GW),
            rows_back(GW), rows_back(GW), rows_back(GW), fixed(8, GW),
        ]
        + [across_back] * F
        + [fixed(GW, D)],
        [
            rows_back(GW), rows_back(GW), rows_back(GW), per_block_back(N, GW), fixed(N, GW),
            fixed(8, GW), half_of_back(D, 0), half_of_back(D, 1),
        ],
        [
            struct((TL, GW), bf16), struct((TL, GW), bf16), struct((TL, GW), bf16),
            struct((blocks, N, GW), f32), struct((N, GW), f32), struct((8, GW), f32),
            struct((TL // 2, D), bf16), struct((TL // 2, D), bf16),
        ],
        [pltpu.VMEM((N, GW), f32)],
    )(
        spot, actx, actp, cum, total, y_intra, y_inter, gate, back_normed, wide_rows, *sums,
        out_rows,
    )
    skip_part = jnp.sum(small_sums[1].reshape(HG, P_SIZE), axis=1)
    firsts = [from_part(first_back, k) for k in range(1, F)]

    def by_line(arrays):
        rows, width = arrays[0].shape[1:]
        block = pl.BlockSpec((1, rows, width), lambda i, p: (lax.rem(p[2] + i, F), 0, 0))
        sums = call(
            functools.partial(sum_kernel, F),
            F,
            [block] * len(arrays),
            [fixed(rows, width)] * F,
            [struct((rows, width), bf16)] * F,
        )(spot, *arrays)
        return [sums[0]] + [from_line(sums[k], k) for k in range(1, F)]

    def add_group(away, mine):
        shape = (F, tokens, mine.shape[1])
        pieces = by_line([mine.reshape(shape), twin(away).reshape(shape)])
        return sum(piece.astype(f32) for piece in pieces)

    def partial_sums(lefts, rights, step):
        pairs = len(lefts)
        rows = pairs * QW + (0 if step is None else 8)
        extra = [] if step is None else [step]
        if Dl % 128 == 0:
            columns_of = pl.BlockSpec((TL, Dl), lambda i, p: (0, i))
            return call(
                functools.partial(partial_blocks_kernel, F, pairs),
                F,
                [fixed(TL, GW)] * pairs + [columns_of] * pairs + [fixed(TL, 8)] * len(extra),
                [pl.BlockSpec((1, rows, Dl), lambda i, p: (i, 0, 0))] * F,
                [struct((F, rows, Dl), bf16)] * F,
                [pltpu.VMEM((pairs, GW, TL), bf16), pltpu.VMEM((GW, Dl), f32)],
            )(spot, *lefts, *rights, *extra)
        return call(
            functools.partial(partial_kernel, F, pairs),
            blocks,
            [rows_of(GW)] * pairs + [rows_of(D)] * pairs + [rows_of(8)] * len(extra),
            [fixed(F, rows, Dl)] * F,
            [struct((F, rows, Dl), bf16)] * F,
            [pltpu.VMEM((GW, D), f32)] * pairs + [pltpu.VMEM((8, D), f32)] * len(extra),
        )(spot, *lefts, *rights, *extra)

    def share(pieces):
        piece = jnp.stack(pieces)
        mine = [piece] + [from_part(piece, k) for k in range(1, F)]
        return mine + [twin(jnp.stack(mine))]

    block_out = (hidden + add_group(away, mine)).astype(bf16)

    early = partial_sums([gated_normed, back_gate], [cot_group, x_group], None)
    early = [early[0]] + [from_part(early[k], k) for k in range(1, F)]
    early = share(by_line(early))

    du_intra, dbc = call(
        back_intra_kernel,
        blocks,
        [
            rows_of(GW), rows_of(NP), rows_of(8), rows_of(8), across, rows_of(GW),
            per_block(N, GW),
        ],
        [rows_of(GW), rows_of(NP)],
        [struct((TL, GW), f32), struct((TL, NP), f32)],
    )(spot, actx, actp, dt, cum, cumt, dy, states)

    dprex, dprep, back_step, head_sums, edge_back = call(
        back_inter_kernel,
        blocks,
        [
            rows_of(GW), rows_of(NP), rows_of(GW), rows_of(NP), rows_of(8), rows_of(8),
            rows_of(8), per_block(8, GW), fixed(8, GW), per_block(N, GW), per_block(N, GW),
            rows_of(GW), rows_of(GW), rows_of(GW), rows_of(GW), rows_of(NP), fixed(8, 128),
            fixed(8, GW),
        ]
        + [fixed(N + 8, GW)] * (F - 1)
        + [fixed(N, GW)] * (F - 1),
        [rows_of(GW), rows_of(NP), rows_of(8), fixed(8, 8), fixed(8, GW + NP)],
        [
            struct((TL, GW), f32), struct((TL, NP), f32), struct((TL, 8), f32),
            struct((8, 8), f32), struct((8, GW + NP), f32),
        ],
        [pltpu.VMEM((8, GW), f32), pltpu.VMEM((N, GW), f32)],
    )(
        spot, actx, actp, slopex, slopep, dt, cum, step_in, total, final[N:], local_back,
        states, dy, y_intra, y_inter, du_intra, dbc, heads, wide_rows, *finals, *firsts,
    )
    halo_back = lax.ppermute(edge_back, "seq", back)

    def following(width):
        return pl.BlockSpec(
            (8, width), lambda i, p: (jnp.minimum((i + 1) * (Q // 8), TL // 8 - 1), 0)
        )

    (
        back_inner, pair_away, pair_mine, conv_x_part, conv_p_part, away, mine, gain_rows,
    ) = call(
        back_conv_kernel,
        blocks,
        [
            rows_of(GW), rows_of(NP), following(GW), following(NP), fixed(8, GW + NP),
            rows_of(GW), rows_of(NP), fixed(8, GW), fixed(8, NP), rows_of(GW), rows_of(8),
            rows_of(D), fixed(GW, D), fixed(GW + 8, D),
        ],
        [
            rows_of(GW), half_of(NP, 0), half_of(NP, 1), fixed(8, GW), fixed(8, NP),
            half_of(D, 0), half_of(D, 1), fixed(8, D),
        ],
        [
            struct((TL, GW), bf16), struct((TL // 2, NP), bf16), struct((TL // 2, NP), bf16),
            struct((8, GW), f32), struct((8, NP), f32), struct((TL // 2, D), bf16),
            struct((TL // 2, D), bf16), struct((8, D), f32),
        ],
        [pltpu.VMEM((Q + 8, GW), f32), pltpu.VMEM((Q + 8, NP), f32)],
    )(
        spot, dprex, dprep, dprex, dprep, halo_back, rawx, rawp, conv_x, conv_p, back_gate,
        back_step, x_group, gate_rows, in_rows,
    )

    late = partial_sums([back_inner], [x_group], back_step)
    late = [late[0]] + [from_part(late[k], k) for k in range(1, F)]
    pair_own = add_group(pair_away, pair_mine).astype(bf16)
    back_in = add_group(away, mine)
    late = share(by_line(late))

    rest_rel = [pair_own] + [from_line(pair_own, k) for k in range(1, F)]
    rest_line = []
    for j in range(F):
        here = pair_own
        for k in range(1, F):
            here = jnp.where(lax.rem(f - k + F, F) == j, rest_rel[k], here)
        rest_line.append(here)
    rest_line = jnp.stack(rest_line)
    rest_other = twin(rest_line)
    rest = jnp.concatenate(
        [jnp.where(c == 0, rest_line, rest_other), jnp.where(c == 0, rest_other, rest_line)],
        axis=0,
    )
    pair_all = rest.reshape(TL, NP)
    x_rows = lax.dynamic_slice(x_group, (0, f * Dl), (TL, Dl))
    grad_rest = dot_f32(pair_all, x_rows, ((0,), (0,)))
    for bit in bits:
        grad_rest = grad_rest.astype(bf16)
        grad_rest = grad_rest.astype(f32) + from_part(grad_rest, bit).astype(f32)

    pair_again = lax.optimization_barrier(pair_own)
    back_pair_in = dot_f32(pair_own, pair_in, ((1,), (0,)))
    gain_part = gain_rows[0] + jnp.sum(
        dot_f32(pair_again, pair_in, ((1,), (0,))) * normed.astype(f32), axis=0
    )
    gain_part = lax.optimization_barrier(gain_part / norm_gain)
    per_channel = jnp.concatenate([conv_x_part[: KW + 1], small_sums[:1]], axis=0)
    per_channel = jnp.transpose(per_channel.reshape(KW + 2, HG, F, PF), (2, 0, 1, 3))
    per_channel = jnp.pad(
        per_channel.reshape(F, KW + 2, HG * PF), ((0, 0), (0, 0), (0, 128 - HG * PF))
    )
    per_head = jnp.concatenate([head_sums[0, :HG], head_sums[1, :HG], skip_part])
    per_head = jnp.broadcast_to(jnp.pad(per_head, (0, 128 - 3 * HG))[None, None], (F, 1, 128))
    slots = jnp.concatenate([per_channel, per_head, jnp.zeros((F, 1, 128), f32)], axis=1)
    shared = jnp.concatenate([conv_p_part[: KW + 1].reshape(-1), gain_part])
    count = shared.shape[0]
    lines = -(-count // 1024) * 8
    shared = jnp.pad(shared, (0, lines * 128 - count)).reshape(lines, 128)
    shared = shared + twin(shared)
    small = jnp.concatenate([slots.reshape(F * 8, 128), shared], axis=0)
    for bit in bits:
        small = small + from_part(small, bit)
    slots, shared = small[: F * 8].reshape(F, 8, 128), small[F * 8 :]
    for bit in bits:
        shared = shared + lax.ppermute(shared, "fsdp", [(i, i ^ bit) for i in range(F)])
    owners = [
        ((qq * R + cc) * F + ff, (cc * F + ff) * F + qq)
        for qq in range(F)
        for cc in range(R)
        for ff in range(F)
    ]
    mine_small = lax.ppermute(take(slots, q), everyone, owners)
    shared = shared.reshape(-1)
    pair_grads = shared[: (KW + 1) * NP].reshape(KW + 1, NP)
    gain_sum = shared[(KW + 1) * NP : count]
    channel_grads = mine_small[: KW + 2, : HG * PF].reshape(KW + 2, HG, PF)
    head_grads = mine_small[KW + 2]

    back_in = back_in + back_pair_in
    scaled_back = back_in * norm_gain[None, :]
    inverse_cubed = inverse_scale * inverse_scale * inverse_scale
    grad_input = (
        cotangent.astype(f32)
        + inverse_scale * scaled_back
        - hidden * inverse_cubed * jnp.mean(scaled_back * hidden, axis=1, keepdims=True)
    ).astype(bf16)

    E = in_weight.shape[1]
    grad_in_weight = call(
        functools.partial(late_grads_kernel, F, QW, HG),
        S + -(-(E - 2 * DI) // GW),
        [fixed(F, QW + 8, Dl)] * F + [fixed(F, F, QW + 8, Dl)],
        pl.BlockSpec((GW, Dl), lambda i, p: (S + i, 0)),
        struct((E, Dl), f32),
    )(spot, *late)
    grad_in_weight, grad_out_weight = call(
        functools.partial(early_grads_kernel, F),
        S,
        [fixed(F, 2 * QW, Dl)] * F + [fixed(F, F, 2 * QW, Dl), anywhere],
        [pl.BlockSpec((GW, Dl), lambda i, p: (i, 0))] * 2,
        [struct((E, Dl), f32), struct((DI, Dl), f32)],
        aliases={F + 2: 0},
    )(spot, *early, grad_in_weight)
    grad_in_weight = call(
        pair_grads_kernel,
        1,
        [fixed(NP, Dl), anywhere],
        pl.BlockSpec((NP, Dl), lambda i, p: (2 * DI // NP, 0)),
        struct((E, Dl), f32),
        aliases={2: 0},
    )(spot, grad_rest, grad_in_weight)
    grad_in_weight = jnp.transpose(grad_in_weight)
    return (
        block_out,
        grad_input,
        gain_sum,
        grad_in_weight,
        channel_grads[:KW],
        channel_grads[KW],
        pair_grads[:KW],
        pair_grads[KW],
        head_grads[:HG],
        head_grads[HG : 2 * HG],
        head_grads[2 * HG : 3 * HG],
        channel_grads[KW + 1],
        grad_out_weight,
    )


def solution(mesh):
    in_specs = (
        P(("seq", "fsdp"), None),
        P(),
        P("fsdp", None),
        P(None, "seq", "fsdp"),
        P("seq", "fsdp"),
        P(),
        P(),
        P("seq"),
        P("seq"),
        P("seq"),
        P("seq", "fsdp"),
        P(None, "fsdp"),
        P(("seq", "fsdp"), None),
    )
    out_specs = (
        P(("seq", "fsdp"), None),
        P(("seq", "fsdp"), None),
        P(),
        P("fsdp", None),
        P(None, "seq", "fsdp"),
        P("seq", "fsdp"),
        P(),
        P(),
        P("seq"),
        P("seq"),
        P("seq"),
        P("seq", "fsdp"),
        P(None, "fsdp"),
    )

    return jax.shard_map(body, mesh=mesh, in_specs=in_specs, out_specs=out_specs, check_vma=False)
```

profile of v0, /device:TPU:0, one launch (start us, length us, event | category | flops | bytes accessed | tf_op | source)
XLA Modules:
  0.0 513.2 jit_solution(1511443246119182816)
XLA Ops:
  4.9 5.6 %collective-permute-start = (bf16[128,1536]{1,0:T(8,128)(2,1)S(1)}, bf16[128,1536]{1,0:T(8,128)(2,1)S(1)}, u32[]{:S(2)}, u32[]{:S(2)}) collective-permute-start(bf16[128,1536]{1,0:T(8,128)(2,1)S(1)} %fusion.4), channel_id=1, source_target_pairs={{0,1},{1,2},{2,3},{4,5},{5,6},{6,7},{8,9},{9,10},{10,11},{12,13},{... | collective-permute-start | bytes 1179656 | tf_op jit(solution)/shard_map/ppermute | solution.py:695
  23.8 14.7 %collective-permute-done.11 = bf16[168,384]{1,0:T(8,128)(2,1)S(1)} collective-permute-done((bf16[168,384]{1,0:T(8,128)(2,1)S(1)}, bf16[168,384]{1,0:T(8,128)(2,1)S(1)}, u32[]{:S(2)}, u32[]{:S(2)}) %collective-permute-start.11) | collective-permute-done | bytes 129056 | tf_op jit(solution)/shard_map/ppermute | solution.py:687
  38.5 8.5 %collective-permute-start.10 = (bf16[168,384]{1,0:T(8,128)(2,1)S(1)}, bf16[168,384]{1,0:T(8,128)(2,1)S(1)}, u32[]{:S(2)}, u32[]{:S(2)}) collective-permute-start(bf16[168,384]{1,0:T(8,128)(2,1)S(1)} %constant_dynamic-update-slice_fusion.3), channel_id=1, source_target_pairs={{0,2},{1,3},{2,0},{3,1},{4,6},{5,7},{6,4},{7,5},{8,10},{9,11},{10,... | collective-permute-start | bytes 387080 | tf_op jit(solution)/shard_map/ppermute | solution.py:687
  54.8 5.9 %collective-permute-done.9 = bf16[168,384]{1,0:T(8,128)(2,1)S(1)} collective-permute-done((bf16[168,384]{1,0:T(8,128)(2,1)}, bf16[168,384]{1,0:T(8,128)(2,1)S(1)}, u32[]{:S(2)}, u32[]{:S(2)}) %collective-permute-start.9) | collective-permute-done | bytes 129056 | tf_op jit(solution)/shard_map/ppermute | solution.py:687
  63.7 5.0 collective-permute-start.23
  76.8 5.7 %collective-permute-done.4 = bf16[128,1536]{1,0:T(8,128)(2,1)S(1)} collective-permute-done((bf16[128,1536]{1,0:T(8,128)(2,1)S(1)}, bf16[128,1536]{1,0:T(8,128)(2,1)S(1)}, u32[]{:S(2)}, u32[]{:S(2)}) %collective-permute-start.4) | collective-permute-done | bytes 393248 | tf_op jit(solution)/shard_map/ppermute | solution.py:696
  84.6 12.5 %collective-permute-done.5 = bf16[128,1536]{1,0:T(8,128)(2,1)S(1)} collective-permute-done((bf16[128,1536]{1,0:T(8,128)(2,1)S(1)}, bf16[128,1536]{1,0:T(8,128)(2,1)S(1)}, u32[]{:S(2)}, u32[]{:S(2)}) %collective-permute-start.5) | collective-permute-done | bytes 393248 | tf_op jit(solution)/shard_map/ppermute | solution.py:696
  145.5 15.3 %shard_map.228 = (bf16[1024,1536]{1,0:T(8,128)(2,1)}, bf16[392,1536]{1,0:T(8,128)(2,1)}, bf16[256,1536]{1,0:T(8,128)(2,1)}, bf16[1024,384]{1,0:T(8,128)(2,1)}, b...) custom-call(s32[3]{0:T(128)} %pad_add_fusion.spot_ref, ...), custom_call_target="tpu_custom_call" | custom-call | tf_op jit(solution)/shard_map/pallas_call | solution.py:873
  165.1 6.1 %shard_map.229.y_ref = f32[1024,384]{1,0:T(8,128)} custom-call(s32[3]{0:T(128)} %pad_add_fusion.spot_ref, bf16[1024,384]{1,0:T(8,128)(2,1)} %get-tuple-element.93.actx_ref, bf16[1024,256]{1,0:T(8,128)(2,1)} %get-tuple-element.94.actp_ref, f32[1024,8]{1,0:T(8,128)} %get-tuple-element.97.dt_ref, f32[1024,8]{1,0:T(8,128)} %get-tuple-element.95.cum_ref, ...), custom_call_target="tpu_custom_call" | custom-call | tf_op jit(solution)/shard_map/pallas_call | solution.py:904
  171.2 9.9 %shard_map.230 = (bf16[1024,1536]{1,0:T(8,128)(2,1)}, bf16[384,1536]{1,0:T(8,128)(2,1)}, bf16[384,1536]{1,0:T(8,128)(2,1)}, bf16[1024,384]{1,0:T(8,128)(2,1)}, bf16[1024,384]{1,0:T(8,128)(2,1)}) custom-call(s32[3]{0:T(128)} %pad_add_fusion.spot_ref, bf16[512,1536]{1,0:T(8,128)(2,1)} %copy-done.2, bf16[512,1536]{1,0:T(8,128)(2,1)} %collective-permute-done.21.other_ref, ...), custom_call_target="tpu_custom_call" | custom-call | tf_op jit(solution)/shard_map/pallas_call | solution.py:911
  181.9 6.9 %shard_map.231 = (f32[1024,384]{1,0:T(8,128)}, bf16[4,128,384]{2,1,0:T(8,128)(2,1)}, f32[8,1024]{1,0:T(8,128)}) custom-call(s32[3]{0:T(128)} %pad_add_fusion.spot_ref, bf16[1024,384]{1,0:T(8,128)(2,1)} %get-tuple-element.93.actx_ref, bf16[1024,256]{1,0:T(8,128)(2,1)} %get-tuple-element.94.actp_ref, f32[1024,8]{1,0:T(8,128)} %get-tuple-element.95.cum_ref, ...), custom_call_target="tpu_custom_call" | custom-call | tf_op jit(solution)/shard_map/pallas_call | solution.py:921
  188.8 13.5 %collective-permute-start.31 = (f32[8,1024]{1,0:T(8,128)}, f32[8,1024]{1,0:T(8,128)S(1)}, u32[]{:S(2)}, u32[]{:S(2)}) collective-permute-start(f32[8,1024]{1,0:T(8,128)} %get-tuple-element.108), channel_id=1, source_target_pairs={{0,4},{4,0},{8,12},{12,8},{16,20},{20,16},{24,28},{28,24},{1,5},{5... | collective-permute-start | bytes 98312 | tf_op jit(solution)/shard_map/ppermute | solution.py:681
  213.8 12.4 %shard_map.232 = (bf16[1024,384]{1,0:T(8,128)(2,1)}, bf16[1024,384]{1,0:T(8,128)(2,1)}, bf16[1024,384]{1,0:T(8,128)(2,1)}, f32[4,128,384]{2,1,0:T(8,128)}, f32[1...) custom-call(s32[3]{0:T(128)} %pad_add_fusion.spot_ref, ...), custom_call_target="tpu_custom_call" | custom-call | tf_op jit(solution)/shard_map/pallas_call | solution.py:936
  231.1 8.7 %shard_map.234 = (f32[1024,384]{1,0:T(8,128)}, f32[1024,256]{1,0:T(8,128)}) custom-call(s32[3]{0:T(128)} %pad_add_fusion.spot_ref, bf16[1024,384]{1,0:T(8,128)(2,1)} %get-tuple-element.93.actx_ref, bf16[1024,256]{1,0:T(8,128)(2,1)} %get-tuple-element.94.actp_ref, f32[1024,8]{1,0:T(8,128)} %get-tuple-element.97.dt_ref, f32[1024,8]{1,0:T(8,128)} %get-tuple-element.95.cum_ref, ...), custom_call_target="tpu_custom_call" | custom-call | tf_op jit(solution)/shard_map/pallas_call | solution.py:1013
  240.6 11.2 %shard_map.235 = (f32[1024,384]{1,0:T(8,128)}, f32[1024,256]{1,0:T(8,128)}, f32[1024,8]{1,0:T(8,128)}, f32[8,8]{1,0:T(8,128)}, f32[8,640]{1,0:T(8,128)}) custom-call(s32[3]{0:T(128)} %pad_add_fusion.spot_ref, bf16[1024,384]{1,0:T(8,128)(2,1)} %get-tuple-element.93.actx_ref, bf16[1024,256]{1,0:T(8,128)(2,1)} %get-tuple-element.94.actp_ref, ...), custom_call_target="tpu_custom_call" | custom-call | tf_op jit(solution)/shard_map/pallas_call | solution.py:1024
  254.1 8.6 %shard_map.239 = (bf16[4,192,384]{2,1,0:T(8,128)(2,1)}, bf16[4,192,384]{2,1,0:T(8,128)(2,1)}, bf16[4,192,384]{2,1,0:T(8,128)(2,1)}, bf16[4,192,384]{2,1,0:T(8,128)(2,1)}) custom-call(s32[3]{0:T(128)} %pad_add_fusion.spot_ref, bf16[1024,384]{1,0:T(8,128)(2,1)} %get-tuple-element.152.refs_0_, bf16[1024,384]{1,0:T(8,128)(2,1)} %get-tuple-element.130.bgate_ref.refs_1_, ...), custom_call_target="tpu_custom_call" | custom-call | tf_op jit(solution)/shard_map/pallas_call | solution.py:985
  267.6 14.5 %shard_map.236 = (bf16[1024,384]{1,0:T(8,128)(2,1)}, bf16[512,256]{1,0:T(8,128)(2,1)}, bf16[512,256]{1,0:T(8,128)(2,1)}, f32[8,384]{1,0:T(8,128)}, f32[8,256]{1,...) custom-call(s32[3]{0:T(128)} %pad_add_fusion.spot_ref, ...), custom_call_target="tpu_custom_call" | custom-call | tf_op jit(solution)/shard_map/pallas_call | solution.py:1054
  284.7 6.6 %shard_map.241 = (bf16[4,104,384]{2,1,0:T(8,128)(2,1)}, bf16[4,104,384]{2,1,0:T(8,128)(2,1)}, bf16[4,104,384]{2,1,0:T(8,128)(2,1)}, bf16[4,104,384]{2,1,0:T(8,128)(2,1)}) custom-call(s32[3]{0:T(128)} %pad_add_fusion.spot_ref, bf16[1024,384]{1,0:T(8,128)(2,1)} %get-tuple-element.162.refs_0_, bf16[1024,1536]{1,0:T(8,128)(2,1)} %get-tuple-element.103.x_ref.refs_3_.refs_1_, ...), custom_call_target="tpu_custom_call" | custom-call | tf_op jit(solution)/shard_map/pallas_call | solution.py:985
  306.7 17.0 %collective-permute-done.72.refs_1_ = bf16[4,104,384]{2,1,0:T(8,128)(2,1)} collective-permute-done((bf16[4,104,384]{2,1,0:T(8,128)(2,1)}, bf16[4,104,384]{2,1,0:T(8,128)(2,1)}, u32[]{:S(2)}, u32[]{:S(2)}) %collective-permute-start.72) | collective-permute-done | bytes 319520 | tf_op jit(solution)/shard_map/ppermute | solution.py:684
  325.8 12.6 %collective-permute-done.73.refs_2_ = bf16[4,104,384]{2,1,0:T(8,128)(2,1)S(1)} collective-permute-done((bf16[4,104,384]{2,1,0:T(8,128)(2,1)}, bf16[4,104,384]{2,1,0:T(8,128)(2,1)S(1)}, u32[]{:S(2)}, u32[]{:S(2)}) %collective-permute-start.73) | collective-permute-done | bytes 319520 | tf_op jit(solution)/shard_map/ppermute | solution.py:684
  366.8 6.1 %collective-permute-start.54 = (f32[24,128]{1,0:T(8,128)S(1)}, f32[24,128]{1,0:T(8,128)S(1)}, u32[]{:S(2)}, u32[]{:S(2)}) collective-permute-start(f32[24,128]{1,0:T(8,128)S(1)} %slice.255), channel_id=1, source_target_pairs={{0,1},{1,0},{2,3},{3,2},{4,5},{5,4},{6,7},{7,6},{8,9},{9,8},{10,11... | collective-permute-start | bytes 36872 | tf_op jit(solution)/shard_map/ppermute | solution.py:1127
  375.7 6.6 %collective-permute-start.70 = (bf16[4,192,384]{2,1,0:T(8,128)(2,1)S(1)}, bf16[4,192,384]{2,1,0:T(8,128)(2,1)S(1)}, u32[]{:S(2)}, u32[]{:S(2)}) collective-permute-start(bf16[4,192,384]{2,1,0:T(8,128)(2,1)S(1)} %get-tuple-element.226.refs_0_), channel_id=1, source_target_pairs={{0,24},{4,28},{8,16},{12,20},{16,8},{20,12},{24,0},{28,4},{1,25},{... | collective-permute-start | bytes 1769480 | tf_op jit(solution)/shard_map/ppermute | solution.py:684
  385.5 11.1 %collective-permute-done.70.refs_3_ = bf16[4,192,384]{2,1,0:T(8,128)(2,1)S(1)} collective-permute-done((bf16[4,192,384]{2,1,0:T(8,128)(2,1)S(1)}, bf16[4,192,384]{2,1,0:T(8,128)(2,1)S(1)}, u32[]{:S(2)}, u32[]{:S(2)}) %collective-permute-start.70) | collective-permute-done | bytes 589856 | tf_op jit(solution)/shard_map/ppermute | solution.py:684
  399.5 9.6 %collective-permute-done.69.refs_2_ = bf16[4,192,384]{2,1,0:T(8,128)(2,1)S(1)} collective-permute-done((bf16[4,192,384]{2,1,0:T(8,128)(2,1)S(1)}, bf16[4,192,384]{2,1,0:T(8,128)(2,1)S(1)}, u32[]{:S(2)}, u32[]{:S(2)}) %collective-permute-start.69) | collective-permute-done | bytes 589856 | tf_op jit(solution)/shard_map/ppermute | solution.py:684
  424.2 4.9 shard_map.237
  439.1 4.8 shard_map.233
  443.9 11.4 %collective-permute-start.36 = (bf16[128,1536]{1,0:T(8,128)(2,1)}, bf16[128,1536]{1,0:T(8,128)(2,1)S(1)}, u32[]{:S(2)}, u32[]{:S(2)}) collective-permute-start(bf16[128,1536]{1,0:T(8,128)(2,1)} %get-tuple-element.113), channel_id=1, source_target_pairs={{0,1},{1,2},{2,3},{3,0},{4,5},{5,6},{6,7},{7,4},{8,9},{9,10},{10,1... | collective-permute-start | bytes 1179656 | tf_op jit(solution)/shard_map/ppermute | solution.py:687
  455.3 4.8 collective-permute-done.45
  460.1 20.5 %collective-permute-start.38 = (bf16[128,1536]{1,0:T(8,128)(2,1)}, bf16[128,1536]{1,0:T(8,128)(2,1)S(1)}, u32[]{:S(2)}, u32[]{:S(2)}) collective-permute-start(bf16[128,1536]{1,0:T(8,128)(2,1)} %get-tuple-element.115), channel_id=1, source_target_pairs={{0,3},{1,0},{2,1},{3,2},{4,7},{5,4},{6,5},{7,6},{8,11},{9,8},{10,9... | collective-permute-start | bytes 1179656 | tf_op jit(solution)/shard_map/ppermute | solution.py:687
  482.5 9.0 %collective-permute-done.37 = bf16[128,1536]{1,0:T(8,128)(2,1)S(1)} collective-permute-done((bf16[128,1536]{1,0:T(8,128)(2,1)}, bf16[128,1536]{1,0:T(8,128)(2,1)S(1)}, u32[]{:S(2)}, u32[]{:S(2)}) %collective-permute-start.37) | collective-permute-done | bytes 393248 | tf_op jit(solution)/shard_map/ppermute | solution.py:687
  496.1 6.7 %shard_map.243.refs_5_ = f32[6448,384]{1,0:T(8,128)} custom-call(s32[3]{0:T(128)} %pad_add_fusion.spot_ref, bf16[4,104,384]{2,1,0:T(8,128)(2,1)} %get-tuple-element.232.refs_0_, bf16[4,104,384]{2,1,0:T(8,128)(2,1)} %collective-permute-done.78.refs_1_, bf16[4,104,384]{2,1,0:T(8,128)(2,1)} %collective-permute-done.79.refs_2_, ...), custom_call_target="tpu_custom_call" | custom-call | tf_op jit(solution)/shard_map/pallas_call | solution.py:1151
  502.8 7.9 %shard_map.244 = (f32[6448,384]{1,0:T(8,128)}, f32[3072,384]{1,0:T(8,128)}) custom-call(s32[3]{0:T(128)} %pad_add_fusion.spot_ref, bf16[4,192,384]{2,1,0:T(8,128)(2,1)} %copy-done.7, bf16[4,192,384]{2,1,0:T(8,128)(2,1)} %copy-done.6, bf16[4,192,384]{2,1,0:T(8,128)(2,1)} %copy-done.5, ...), custom_call_target="tpu_custom_call", output_to_operand_aliasing={{0}: (6, {})} | custom-call | tf_op jit(solution)/shard_map/pallas_call | solution.py:1158
  (391 shorter events, 207.0 us)
Async XLA Ops:
  3.6 57.2 %collective-permute-start.3 = (bf16[128,1536]{1,0:T(8,128)(2,1)S(1)}, bf16[128,1536]{1,0:T(8,128)(2,1)S(1)}, u32[]{:S(2)}, u32[]{:S(2)}) collective-permute-start(bf16[128,1536]{1,0:T(8,128)(2,1)S(1)} %fusion.4), channel_id=1, source_target_pairs={{1,0},{2,1},{3,2},{5,4},{6,5},{7,6},{9,8},{10,9},{11,10},{13,12},{... | collective-permute-start | bytes 1179656 | tf_op jit(solution)/shard_map/ppermute | solution.py:696
  4.9 57.2 %collective-permute-start = (bf16[128,1536]{1,0:T(8,128)(2,1)S(1)}, bf16[128,1536]{1,0:T(8,128)(2,1)S(1)}, u32[]{:S(2)}, u32[]{:S(2)}) collective-permute-start(bf16[128,1536]{1,0:T(8,128)(2,1)S(1)} %fusion.4), channel_id=1, source_target_pairs={{0,1},{1,2},{2,3},{4,5},{5,6},{6,7},{8,9},{9,10},{10,11},{12,13},{... | collective-permute-start | bytes 1179656 | tf_op jit(solution)/shard_map/ppermute | solution.py:695
  10.5 53.2 %collective-permute-start.20 = (bf16[128,1536]{1,0:T(8,128)(2,1)}, bf16[128,1536]{1,0:T(8,128)(2,1)S(1)}, u32[]{:S(2)}, u32[]{:S(2)}) collective-permute-start(bf16[128,1536]{1,0:T(8,128)(2,1)} %param.25), channel_id=1, source_target_pairs={{0,3},{1,0},{2,1},{3,2},{4,7},{5,4},{6,5},{7,6},{8,11},{9,8},{10,9... | collective-permute-start | bytes 1179656 | tf_op jit(solution)/shard_map/ppermute | solution.py:687
  12.4 56.3 %collective-permute-start.19 = (bf16[128,1536]{1,0:T(8,128)(2,1)}, bf16[128,1536]{1,0:T(8,128)(2,1)S(1)}, u32[]{:S(2)}, u32[]{:S(2)}) collective-permute-start(bf16[128,1536]{1,0:T(8,128)(2,1)} %param.25), channel_id=1, source_target_pairs={{0,2},{1,3},{2,0},{3,1},{4,6},{5,7},{6,4},{7,5},{8,10},{9,11},{10,... | collective-permute-start | bytes 1179656 | tf_op jit(solution)/shard_map/ppermute | solution.py:687
  17.7 20.8 %collective-permute-start.11 = (bf16[168,384]{1,0:T(8,128)(2,1)S(1)}, bf16[168,384]{1,0:T(8,128)(2,1)S(1)}, u32[]{:S(2)}, u32[]{:S(2)}) collective-permute-start(bf16[168,384]{1,0:T(8,128)(2,1)S(1)} %constant_dynamic-update-slice_fusion.6), channel_id=1, source_target_pairs={{0,3},{1,0},{2,1},{3,2},{4,7},{5,4},{6,5},{7,6},{8,11},{9,8},{10,9... | collective-permute-start | bytes 387080 | tf_op jit(solution)/shard_map/ppermute | solution.py:687
  60.8 21.6 %collective-permute-start.4 = (bf16[128,1536]{1,0:T(8,128)(2,1)S(1)}, bf16[128,1536]{1,0:T(8,128)(2,1)S(1)}, u32[]{:S(2)}, u32[]{:S(2)}) collective-permute-start(bf16[128,1536]{1,0:T(8,128)(2,1)S(1)} %collective-permute-done.3), channel_id=1, source_target_pairs={{1,0},{2,1},{5,4},{6,5},{9,8},{10,9},{13,12},{14,13},{17,16},{18,1... | collective-permute-start | bytes 1179656 | tf_op jit(solution)/shard_map/ppermute | solution.py:696
  62.1 21.6 %collective-permute-start.1 = (bf16[128,1536]{1,0:T(8,128)(2,1)S(1)}, bf16[128,1536]{1,0:T(8,128)(2,1)S(1)}, u32[]{:S(2)}, u32[]{:S(2)}) collective-permute-start(bf16[128,1536]{1,0:T(8,128)(2,1)S(1)} %collective-permute-done), channel_id=1, source_target_pairs={{1,2},{2,3},{5,6},{6,7},{9,10},{10,11},{13,14},{14,15},{17,18},{18... | collective-permute-start | bytes 1179656 | tf_op jit(solution)/shard_map/ppermute | solution.py:695
  63.7 36.9 %collective-permute-start.23 = (bf16[192,384]{1,0:T(8,128)(2,1)S(1)}, bf16[192,384]{1,0:T(8,128)(2,1)S(1)}, u32[]{:S(2)}, u32[]{:S(2)}) collective-permute-start(bf16[192,384]{1,0:T(8,128)(2,1)S(1)} %pad_maximum_fusion.12), channel_id=1, source_target_pairs={{0,2},{1,3},{2,0},{3,1},{4,6},{5,7},{6,4},{7,5},{8,10},{9,11},{10,... | collective-permute-start | bytes 442376 | tf_op jit(solution)/shard_map/ppermute | solution.py:687
  68.7 32.5 %collective-permute-start.24 = (bf16[192,384]{1,0:T(8,128)(2,1)}, bf16[192,384]{1,0:T(8,128)(2,1)S(1)}, u32[]{:S(2)}, u32[]{:S(2)}) collective-permute-start(bf16[192,384]{1,0:T(8,128)(2,1)} %pad_maximum_fusion.13), channel_id=1, source_target_pairs={{0,3},{1,0},{2,1},{3,2},{4,7},{5,4},{6,5},{7,6},{8,11},{9,8},{10,9... | collective-permute-start | bytes 442376 | tf_op jit(solution)/shard_map/ppermute | solution.py:687
  73.9 27.5 %collective-permute-start.22 = (bf16[192,384]{1,0:T(8,128)(2,1)}, bf16[192,384]{1,0:T(8,128)(2,1)S(1)}, u32[]{:S(2)}, u32[]{:S(2)}) collective-permute-start(bf16[192,384]{1,0:T(8,128)(2,1)} %pad_maximum_fusion.11), channel_id=1, source_target_pairs={{0,1},{1,2},{2,3},{3,0},{4,5},{5,6},{6,7},{7,4},{8,9},{9,10},{10,1... | collective-permute-start | bytes 442376 | tf_op jit(solution)/shard_map/ppermute | solution.py:687
  101.2 44.3 %collective-permute-start.6 = (bf16[512,1536]{1,0:T(8,128)(2,1)S(1)}, bf16[512,1536]{1,0:T(8,128)(2,1)}, u32[]{:S(2)}, u32[]{:S(2)}) collective-permute-start(bf16[512,1536]{1,0:T(8,128)(2,1)S(1)} %pad_maximum_fusion.1.mine_ref), channel_id=1, source_target_pairs={{0,4},{4,0},{8,12},{12,8},{16,20},{20,16},{24,28},{28,24},{1,5},{5... | collective-permute-start | bytes 4718600 | tf_op jit(solution)/shard_map/ppermute | solution.py:681
  101.4 69.8 %collective-permute-start.21 = (bf16[512,1536]{1,0:T(8,128)(2,1)S(1)}, bf16[512,1536]{1,0:T(8,128)(2,1)}, u32[]{:S(2)}, u32[]{:S(2)}) collective-permute-start(bf16[512,1536]{1,0:T(8,128)(2,1)S(1)} %pad_maximum_fusion.2.mine_ref), channel_id=1, source_target_pairs={{0,4},{4,0},{8,12},{12,8},{16,20},{20,16},{24,28},{28,24},{1,5},{5... | collective-permute-start | bytes 4718600 | tf_op jit(solution)/shard_map/ppermute | solution.py:681
  122.4 40.9 %collective-permute-start.27 = (bf16[4,192,384]{2,1,0:T(8,128)(2,1)}, bf16[4,192,384]{2,1,0:T(8,128)(2,1)}, u32[]{:S(2)}, u32[]{:S(2)}) collective-permute-start(bf16[4,192,384]{2,1,0:T(8,128)(2,1)} %pad_maximum_fusion.4.refs_0_), channel_id=1, source_target_pairs={{0,24},{4,28},{8,16},{12,20},{16,8},{20,12},{24,0},{28,4},{1,25},{... | collective-permute-start | bytes 1769480 | tf_op jit(solution)/shard_map/ppermute | solution.py:684
  124.9 38.7 %collective-permute-start.26 = (bf16[4,192,384]{2,1,0:T(8,128)(2,1)}, bf16[4,192,384]{2,1,0:T(8,128)(2,1)}, u32[]{:S(2)}, u32[]{:S(2)}) collective-permute-start(bf16[4,192,384]{2,1,0:T(8,128)(2,1)} %pad_maximum_fusion.4.refs_0_), channel_id=1, source_target_pairs={{0,16},{4,20},{8,24},{12,28},{16,0},{20,4},{24,8},{28,12},{1,17},{... | collective-permute-start | bytes 1769480 | tf_op jit(solution)/shard_map/ppermute | solution.py:684
  128.1 43.1 %collective-permute-start.25 = (bf16[4,192,384]{2,1,0:T(8,128)(2,1)}, bf16[4,192,384]{2,1,0:T(8,128)(2,1)}, u32[]{:S(2)}, u32[]{:S(2)}) collective-permute-start(bf16[4,192,384]{2,1,0:T(8,128)(2,1)} %pad_maximum_fusion.4.refs_0_), channel_id=1, source_target_pairs={{0,8},{4,12},{8,0},{12,4},{16,24},{20,28},{24,16},{28,20},{1,9},{5... | collective-permute-start | bytes 1769480 | tf_op jit(solution)/shard_map/ppermute | solution.py:684
  160.8 20.2 %collective-permute-start.30 = (f32[136,384]{1,0:T(8,128)}, f32[136,384]{1,0:T(8,128)S(1)}, u32[]{:S(2)}, u32[]{:S(2)}) collective-permute-start(f32[136,384]{1,0:T(8,128)} %get-tuple-element.106), channel_id=1, source_target_pairs={{0,24},{4,28},{8,16},{12,20},{16,8},{20,12},{24,0},{28,4},{1,25},{... | collective-permute-start | bytes 626696 | tf_op jit(solution)/shard_map/ppermute | solution.py:684
  262.7 81.4 %collective-permute-start.62 = (bf16[4,192,384]{2,1,0:T(8,128)(2,1)}, bf16[4,192,384]{2,1,0:T(8,128)(2,1)S(1)}, u32[]{:S(2)}, u32[]{:S(2)}) collective-permute-start(bf16[4,192,384]{2,1,0:T(8,128)(2,1)} %get-tuple-element.155), channel_id=1, source_target_pairs={{0,8},{4,12},{8,0},{12,4},{16,24},{20,28},{24,16},{28,20},{1,9},{5... | collective-permute-start | bytes 1769480 | tf_op jit(solution)/shard_map/ppermute | solution.py:684
  265.3 82.4 %collective-permute-start.63 = (bf16[4,192,384]{2,1,0:T(8,128)(2,1)}, bf16[4,192,384]{2,1,0:T(8,128)(2,1)S(1)}, u32[]{:S(2)}, u32[]{:S(2)}) collective-permute-start(bf16[4,192,384]{2,1,0:T(8,128)(2,1)} %get-tuple-element.156), channel_id=1, source_target_pairs={{0,16},{4,20},{8,24},{12,28},{16,0},{20,4},{24,8},{28,12},{1,17},{... | collective-permute-start | bytes 1769480 | tf_op jit(solution)/shard_map/ppermute | solution.py:684
  302.5 45.4 %collective-permute-start.64 = (bf16[4,192,384]{2,1,0:T(8,128)(2,1)}, bf16[4,192,384]{2,1,0:T(8,128)(2,1)S(1)}, u32[]{:S(2)}, u32[]{:S(2)}) collective-permute-start(bf16[4,192,384]{2,1,0:T(8,128)(2,1)} %get-tuple-element.157), channel_id=1, source_target_pairs={{0,24},{4,28},{8,16},{12,20},{16,8},{20,12},{24,0},{28,4},{1,25},{... | collective-permute-start | bytes 1769480 | tf_op jit(solution)/shard_map/ppermute | solution.py:684
  347.8 74.4 %collective-permute-start.43 = (bf16[512,1536]{1,0:T(8,128)(2,1)}, bf16[512,1536]{1,0:T(8,128)(2,1)}, u32[]{:S(2)}, u32[]{:S(2)}) collective-permute-start(bf16[512,1536]{1,0:T(8,128)(2,1)} %get-tuple-element.135), channel_id=1, source_target_pairs={{0,4},{4,0},{8,12},{12,8},{16,20},{20,16},{24,28},{28,24},{1,5},{5... | collective-permute-start | bytes 4718600 | tf_op jit(solution)/shard_map/ppermute | solution.py:681
  375.0 62.3 %collective-permute-start.35 = (bf16[512,1536]{1,0:T(8,128)(2,1)}, bf16[512,1536]{1,0:T(8,128)(2,1)}, u32[]{:S(2)}, u32[]{:S(2)}) collective-permute-start(bf16[512,1536]{1,0:T(8,128)(2,1)} %get-tuple-element.111), channel_id=1, source_target_pairs={{0,4},{4,0},{8,12},{12,8},{16,20},{20,16},{24,28},{28,24},{1,5},{5... | collective-permute-start | bytes 4718600 | tf_op jit(solution)/shard_map/ppermute | solution.py:681
  375.7 20.9 %collective-permute-start.70 = (bf16[4,192,384]{2,1,0:T(8,128)(2,1)S(1)}, bf16[4,192,384]{2,1,0:T(8,128)(2,1)S(1)}, u32[]{:S(2)}, u32[]{:S(2)}) collective-permute-start(bf16[4,192,384]{2,1,0:T(8,128)(2,1)S(1)} %get-tuple-element.226.refs_0_), channel_id=1, source_target_pairs={{0,24},{4,28},{8,16},{12,20},{16,8},{20,12},{24,0},{28,4},{1,25},{... | collective-permute-start | bytes 1769480 | tf_op jit(solution)/shard_map/ppermute | solution.py:684
  382.3 26.8 %collective-permute-start.69 = (bf16[4,192,384]{2,1,0:T(8,128)(2,1)S(1)}, bf16[4,192,384]{2,1,0:T(8,128)(2,1)S(1)}, u32[]{:S(2)}, u32[]{:S(2)}) collective-permute-start(bf16[4,192,384]{2,1,0:T(8,128)(2,1)S(1)} %get-tuple-element.226.refs_0_), channel_id=1, source_target_pairs={{0,16},{4,20},{8,24},{12,28},{16,0},{20,4},{24,8},{28,12},{1,17},{... | collective-permute-start | bytes 1769480 | tf_op jit(solution)/shard_map/ppermute | solution.py:684
  383.8 26.6 %collective-permute-start.68 = (bf16[4,192,384]{2,1,0:T(8,128)(2,1)S(1)}, bf16[4,192,384]{2,1,0:T(8,128)(2,1)S(1)}, u32[]{:S(2)}, u32[]{:S(2)}) collective-permute-start(bf16[4,192,384]{2,1,0:T(8,128)(2,1)S(1)} %get-tuple-element.226.refs_0_), channel_id=1, source_target_pairs={{0,8},{4,12},{8,0},{12,4},{16,24},{20,28},{24,16},{28,20},{1,9},{5... | collective-permute-start | bytes 1769480 | tf_op jit(solution)/shard_map/ppermute | solution.py:684
  396.5 19.6 %collective-permute-start.80 = (bf16[4,104,384]{2,1,0:T(8,128)(2,1)}, bf16[4,104,384]{2,1,0:T(8,128)(2,1)}, u32[]{:S(2)}, u32[]{:S(2)}) collective-permute-start(bf16[4,104,384]{2,1,0:T(8,128)(2,1)} %get-tuple-element.232.refs_0_), channel_id=1, source_target_pairs={{0,24},{4,28},{8,16},{12,20},{16,8},{20,12},{24,0},{28,4},{1,25},{... | collective-permute-start | bytes 958472 | tf_op jit(solution)/shard_map/ppermute | solution.py:684
  413.7 89.1 %collective-permute-start.71 = (bf16[4,4,192,384]{3,2,1,0:T(8,128)(2,1)S(1)}, bf16[4,4,192,384]{3,2,1,0:T(8,128)(2,1)}, u32[]{:S(2)}, u32[]{:S(2)}) collective-permute-start(bf16[4,4,192,384]{3,2,1,0:T(8,128)(2,1)S(1)} %pad_maximum_fusion), channel_id=1, source_target_pairs={{0,4},{4,0},{8,12},{12,8},{16,20},{20,16},{24,28},{28,24},{1,5},{5... | collective-permute-start | bytes 7077896 | tf_op jit(solution)/shard_map/ppermute | solution.py:681
  429.5 30.7 %collective-permute-start.45 = (bf16[128,1536]{1,0:T(8,128)(2,1)}, bf16[128,1536]{1,0:T(8,128)(2,1)}, u32[]{:S(2)}, u32[]{:S(2)}) collective-permute-start(bf16[128,1536]{1,0:T(8,128)(2,1)} %get-tuple-element.138), channel_id=1, source_target_pairs={{0,2},{1,3},{2,0},{3,1},{4,6},{5,7},{6,4},{7,5},{8,10},{9,11},{10,... | collective-permute-start | bytes 1179656 | tf_op jit(solution)/shard_map/ppermute | solution.py:687
  430.2 29.9 %collective-permute-start.46 = (bf16[128,1536]{1,0:T(8,128)(2,1)}, bf16[128,1536]{1,0:T(8,128)(2,1)}, u32[]{:S(2)}, u32[]{:S(2)}) collective-permute-start(bf16[128,1536]{1,0:T(8,128)(2,1)} %get-tuple-element.139), channel_id=1, source_target_pairs={{0,3},{1,0},{2,1},{3,2},{4,7},{5,4},{6,5},{7,6},{8,11},{9,8},{10,9... | collective-permute-start | bytes 1179656 | tf_op jit(solution)/shard_map/ppermute | solution.py:687
  437.3 58.8 %collective-permute-start.81 = (bf16[4,4,104,384]{3,2,1,0:T(8,128)(2,1)}, bf16[4,4,104,384]{3,2,1,0:T(8,128)(2,1)}, u32[]{:S(2)}, u32[]{:S(2)}) collective-permute-start(bf16[4,4,104,384]{3,2,1,0:T(8,128)(2,1)} %pad_maximum_fusion.3), channel_id=1, source_target_pairs={{0,4},{4,0},{8,12},{12,8},{16,20},{20,16},{24,28},{28,24},{1,5},{5... | collective-permute-start | bytes 3833864 | tf_op jit(solution)/shard_map/ppermute | solution.py:681
  443.9 38.6 %collective-permute-start.36 = (bf16[128,1536]{1,0:T(8,128)(2,1)}, bf16[128,1536]{1,0:T(8,128)(2,1)S(1)}, u32[]{:S(2)}, u32[]{:S(2)}) collective-permute-start(bf16[128,1536]{1,0:T(8,128)(2,1)} %get-tuple-element.113), channel_id=1, source_target_pairs={{0,1},{1,2},{2,3},{3,0},{4,5},{5,6},{6,7},{7,4},{8,9},{9,10},{10,1... | collective-permute-start | bytes 1179656 | tf_op jit(solution)/shard_map/ppermute | solution.py:687
  460.1 31.4 %collective-permute-start.37 = (bf16[128,1536]{1,0:T(8,128)(2,1)}, bf16[128,1536]{1,0:T(8,128)(2,1)S(1)}, u32[]{:S(2)}, u32[]{:S(2)}) collective-permute-start(bf16[128,1536]{1,0:T(8,128)(2,1)} %get-tuple-element.114), channel_id=1, source_target_pairs={{0,2},{1,3},{2,0},{3,1},{4,6},{5,7},{6,4},{7,5},{8,10},{9,11},{10,... | collective-permute-start | bytes 1179656 | tf_op jit(solution)/shard_map/ppermute | solution.py:687
  460.1 34.7 %collective-permute-start.38 = (bf16[128,1536]{1,0:T(8,128)(2,1)}, bf16[128,1536]{1,0:T(8,128)(2,1)S(1)}, u32[]{:S(2)}, u32[]{:S(2)}) collective-permute-start(bf16[128,1536]{1,0:T(8,128)(2,1)} %get-tuple-element.115), channel_id=1, source_target_pairs={{0,3},{1,0},{2,1},{3,2},{4,7},{5,4},{6,5},{7,6},{8,11},{9,8},{10,9... | collective-permute-start | bytes 1179656 | tf_op jit(solution)/shard_map/ppermute | solution.py:687
  (110 other events, 1718.4 us)
where the time goes:
time: 518 us; the launch traced here: 513 us
  starting transfers between devices  171 us (33%)
  Pallas kernels  138 us (27%)
  waiting for transfers between devices  136 us (26%)
  local copies, waits for them, and re-layouts  37.2 us (7%)
  other arithmetic  25.1 us (5%)
    ppermute x30, starting transfers between devices, from_line(): return lax.ppermute(value, 'fsdp', [(i, (i + k) % F) for i in range(F)])  84.3 us
    ppermute x31, waiting for transfers between devices, from_part(): return lax.ppermute(value, 'seq', [(i, i ^ k * R) for i in range(S)])  62.1 us
    ppermute x30, waiting for transfers between devices, from_line(): return lax.ppermute(value, 'fsdp', [(i, (i + k) % F) for i in range(F)])  52.9 us
    ppermute x31, starting transfers between devices, from_part(): return lax.ppermute(value, 'seq', [(i, i ^ k * R) for i in range(S)])  45.9 us
    pallas_call x5, Pallas kernels, by_line(): call(functools.partial(sum_kernel, F), F, [block] * len(arrays), [fixed(r...  21 us
    ppermute x3, waiting for transfers between devices, line_chain(): down = lax.ppermute(down, 'fsdp', [(i, i - 1) for i in range(1, F - k + 1)])  18.1 us
    pallas_call x1, Pallas kernels, body(): call(functools.partial(project_kernel, absolute, QW), blocks, [rows_half(...  15.3 us
    pallas_call x2, Pallas kernels, partial_sums(): call(functools.partial(partial_blocks_kernel, F, pairs), F, [fixed(TL, GW...  15.2 us
  transfers between devices with their start and end apart: 84, of which 25 were waited for; matrix products, arithmetic and copies ran while one was open for 11% of the time, Pallas kernels for 19%

commit v1 on v0

--- a/solution.py
+++ b/solution.py
@@ -25,10 +25,6 @@
 def spread(value, axis, count):
     copies = jnp.broadcast_to(value[None], (count,) + value.shape)
     return lax.all_to_all(copies, axis, 0, 0, tiled=True)
-
-
-def dot_f32(left, right, dims, batch=((), ())):
-    return lax.dot_general(left, right, (dims, batch), preferred_element_type=f32)
 
 
 def mm(left, right, dims, precision=None):
@@ -125,6 +121,82 @@
     @pl.when(jnp.logical_not(mine))
     def _():
         away_ref[...] = value
+
+
+def params_kernel(
+    places, width, spot_ref, small_ref, pair_ref, convx_ref, convp_ref, heads_ref, rows_ref
+):
+    GW = convx_ref.shape[1]
+    heads = GW // P_SIZE
+    lane = lax.broadcasted_iota(jnp.int32, (128, GW), 0)
+    chan = lax.broadcasted_iota(jnp.int32, (128, GW), 1)
+    inside = chan % P_SIZE
+    total = jnp.zeros((8, GW), f32)
+    for place in range(places):
+        hot = (inside // width == place) & (
+            lane == (chan // P_SIZE) * width + inside % width
+        )
+        total = total + mm_ones(hot.astype(f32), small_ref[place], ((1,), (0,)), True)
+    row = lax.broadcasted_iota(jnp.int32, (8, GW), 0)
+    convx_ref[...] = jnp.where(row <= KW, total, 0.0)
+    convp_ref[...] = pair_ref[...]
+    line = small_ref[0, KW + 2 : KW + 3]
+    at = lax.broadcasted_iota(jnp.int32, (128, 128), 0)
+    to = lax.broadcasted_iota(jnp.int32, (128, 128), 1)
+
+    def shifted(start):
+        hot = (at == to + start) & (to < heads)
+        return mm_ones(hot.astype(f32), jnp.broadcast_to(line, (8, 128)), ((1,), (0,)), True)
+
+    used = lax.broadcasted_iota(jnp.int32, (8, 128), 1) < heads
+    rate = jnp.where(used, jnp.exp(shifted(heads)), 0.0)
+    down = lax.broadcasted_iota(jnp.int32, (8, 128), 0)
+    heads_ref[...] = jnp.where(down == 0, shifted(0), jnp.where(down == 1, rate, 0.0))
+    skip = widen(shifted(2 * heads)[:, 0:8], GW)
+    gain = jnp.broadcast_to(total[KW + 1 : KW + 2], (8, GW))
+    share = jnp.full((8, GW), 1.0 / (H * P_SIZE), f32)
+    rows_ref[...] = jnp.where(
+        row == 0, gain, jnp.where(row == 1, skip, jnp.where(row == 2, share, 0.0))
+    )
+
+
+def pack_kernel(
+    places, width, spot_ref, convx_ref, sums_ref, heads_ref, convp_ref, gain_ref, norm_ref, out_ref
+):
+    GW = convx_ref.shape[1]
+    heads = GW // P_SIZE
+    row = lax.broadcasted_iota(jnp.int32, (8, GW), 0)
+    gate = jnp.broadcast_to(sums_ref[0:1], (8, GW))
+    value = jnp.where(row <= KW, convx_ref[...], jnp.where(row == KW + 1, gate, 0.0))
+    lane = lax.broadcasted_iota(jnp.int32, (GW, 128), 1)
+    chan = lax.broadcasted_iota(jnp.int32, (GW, 128), 0)
+    inside = chan % P_SIZE
+    at = lax.broadcasted_iota(jnp.int32, (8, 128), 0)
+    to = lax.broadcasted_iota(jnp.int32, (8, 128), 1)
+    line = mm_ones(((to == at) & (at < heads)).astype(f32), heads_ref[...], ((1,), (0,)), True)
+    both = line[0:1]
+    line = mm_ones(
+        ((to == at + heads) & (at < heads)).astype(f32), heads_ref[...], ((1,), (0,)), True
+    )
+    both = both + line[1:2]
+    skip = (lane == 2 * heads + chan // P_SIZE).astype(f32)
+    both = both + mm_ones(skip, sums_ref[...], ((1,), (0,)), True)[1:2]
+    down = lax.broadcasted_iota(jnp.int32, (8, 128), 0)
+    both = jnp.where(down == KW + 2, jnp.broadcast_to(both, (8, 128)), 0.0)
+    for place in range(places):
+        hot = (inside // width == place) & (
+            lane == (chan // P_SIZE) * width + inside % width
+        )
+        out_ref[place * 8 : place * 8 + 8] = (
+            mm_ones(hot.astype(f32), value, ((1,), (0,)), True) + both
+        )
+    at = places * 8
+    out_ref[at : at + 8] = convp_ref[:, 0:128]
+    out_ref[at + 8 : at + 16] = convp_ref[:, 128:256]
+    out_ref[at + 16 :] = jnp.zeros((out_ref.shape[0] - at - 16, 128), f32)
+    gain = gain_ref[0:1] / norm_ref[...]
+    for j in range(gain_ref.shape[1] // 128):
+        out_ref[at + 16 + j : at + 17 + j] = gain[:, j * 128 : (j + 1) * 128]
 
 
 def project_kernel(
@@ -442,8 +514,8 @@
 
 def back_conv_kernel(
     spot_ref, dprex_ref, dprep_ref, nextx_ref, nextp_ref, halo_ref, rawx_ref, rawp_ref,
-    cwx_ref, cwp_ref, bgate_ref, step_ref, x_ref, wgate_ref, win_ref,
-    backx_ref, pair_away_ref, pair_mine_ref, gradx_ref, gradp_ref, away_ref, mine_ref, gain_ref,
+    cwx_ref, cwp_ref, bgate_ref, step_ref, x_ref, wgate_ref, win_ref, wpair_ref,
+    backx_ref, backp_ref, gradx_ref, gradp_ref, away_ref, mine_ref, gain_ref,
     extx, extp,
 ):
     b = pl.program_id(0)
@@ -471,10 +543,11 @@
     inner = conv(dprex_ref, nextx_ref, halo_ref[:, 0:GW], rawx_ref, cwx_ref, extx, gradx_ref)
     backx_ref[...] = inner
     pair = conv(dprep_ref, nextp_ref, halo_ref[:, GW:], rawp_ref, cwp_ref, extp, gradp_ref)
-    to_halves(spot_ref, b, pair, pair_away_ref, pair_mine_ref)
+    backp_ref[...] = pair
     value = mm(bgate_ref[...], wgate_ref[...], ((1,), (0,)))
     value = value + mm(step_ref[...].astype(bf16), win_ref[GW : GW + 8], ((1,), (0,)))
     value = value + mm(inner, win_ref[0:GW], ((1,), (0,)))
+    value = value + mm(pair, wpair_ref[...], ((1,), (0,)))
     gain_ref[0:1] += jnp.sum(value * x_ref[...].astype(f32), axis=0, keepdims=True)
     to_halves(spot_ref, b, value.astype(bf16), away_ref, mine_ref)
 
@@ -507,8 +580,9 @@
 
 def partial_blocks_kernel(count, pairs, spot_ref, *refs):
     lefts, rights = refs[:pairs], refs[pairs : 2 * pairs]
-    step_ref = refs[2 * pairs] if pairs == 1 else None
-    outs, turned, total = refs[-count - 2 : -2], refs[-2], refs[-1]
+    step_ref, pair_ref = refs[2:4] if pairs == 1 else (None, None)
+    held = 4 if pairs == 1 else 2
+    outs, turned, total = refs[-count - held : -held], refs[-held], refs[1 - held]
     GW = total.shape[0]
     QW = GW // count
 
@@ -516,6 +590,8 @@
     def _():
         for at in range(pairs):
             turned[at] = lefts[at][...].T
+        if pair_ref is not None:
+            refs[-2][...] = pair_ref[...].T
 
     for at in range(pairs):
         right = rights[at][...]
@@ -528,19 +604,24 @@
         for k in range(count):
             keep = ((spot_ref[0] ^ k) == 0).astype(f32)
             outs[k][0, QW : QW + 8] = (value * keep).astype(bf16)
+        refs[-1][...] = mm(refs[-2][...], rights[0][...], ((1,), (0,)))
+        PW = refs[-1].shape[0] // count
+        for k in range(count):
+            start = pl.multiple_of((spot_ref[0] ^ k) * PW, 8)
+            outs[k][0, QW + 8 : QW + 8 + PW] = refs[-1][pl.ds(start, PW)].astype(bf16)
 
 
 def partial_kernel(count, pairs, spot_ref, *refs):
     lefts, rights = refs[:pairs], refs[pairs : 2 * pairs]
-    step_ref = refs[2 * pairs] if pairs == 1 else None
-    outs = refs[len(refs) - count - pairs - (pairs == 1) : len(refs) - pairs - (pairs == 1)]
-    sums = refs[len(refs) - pairs - (pairs == 1) :]
+    step_ref, pair_ref = refs[2:4] if pairs == 1 else (None, None)
+    held = 3 if pairs == 1 else pairs
+    outs, sums = refs[len(refs) - count - held : len(refs) - held], refs[len(refs) - held :]
     b = pl.program_id(0)
     lefts = [r[...] for r in lefts]
     rights = [r[...] for r in rights]
     if step_ref is not None:
-        lefts.append(step_ref[...].astype(bf16))
-        rights.append(rights[0])
+        lefts.extend([step_ref[...].astype(bf16), pair_ref[...]])
+        rights.extend([rights[0], rights[0]])
     for left, right, total in zip(lefts, rights, sums, strict=True):
         value = mm(left, right, ((0,), (0,)))
 
@@ -568,6 +649,9 @@
                 if step_ref is not None:
                     keep = (part == 0).astype(f32)
                     outs[k][j, QW : QW + 8] = (sums[1][:, cols] * keep).astype(bf16)
+                    PW = sums[2].shape[0] // count
+                    at = pl.multiple_of(part * PW, 8)
+                    outs[k][j, QW + 8 : QW + 8 + PW] = sums[2][pl.ds(at, PW), cols].astype(bf16)
 
 
 def sum_kernel(outs_count, spot_ref, *refs):
@@ -601,10 +685,6 @@
     step = pl.program_id(0)
     place_rows(count, spot_ref, step, own, other, slice(0, QW), out_ref)
     place_rows(count, spot_ref, step, own, other, slice(QW, 2 * QW), in_ref)
-
-
-def pair_grads_kernel(spot_ref, pair_ref, array_ref, out_ref):
-    out_ref[...] = pair_ref[...]
 
 
 def late_grads_kernel(count, QW, heads, spot_ref, *refs):
@@ -619,7 +699,20 @@
         @pl.when(step == groups + block)
         def _(block=block):
             first = block * GW
+            PW = 2 * N // count
+            base = QW + 8
             for k in range(count):
+                total = sum(
+                    own[k][g, base : base + PW].astype(f32)
+                    + other[k, g, base : base + PW].astype(f32)
+                    for g in range(count)
+                )
+                start = (q ^ k) * PW - first
+
+                @pl.when((start >= 0) & (start < GW))
+                def _(total=total, start=start):
+                    in_ref[pl.ds(pl.multiple_of(start, 8), PW)] = total
+
 
                 @pl.when((q ^ k) == 0)
                 def _(k=k):
@@ -801,13 +894,6 @@
     small = jnp.concatenate([small, heads_row, jnp.zeros((1, 128), f32)], axis=0)
     small_all = spread(small, everyone, devices)
     small_here = lax.dynamic_slice(small_all, (member * F, 0, 0), (F, 8, 128))
-    chan = small_here[:, : KW + 2, : HG * PF].reshape(F, KW + 2, HG, PF)
-    chan = jnp.transpose(chan, (1, 2, 0, 3)).reshape(KW + 2, GW)
-    heads_here = small_here[0, KW + 2]
-    bias_h = heads_here[:HG]
-    rate_h = jnp.exp(heads_here[HG : 2 * HG])
-    skip_h = heads_here[2 * HG : 3 * HG]
-
     hidden = block_in.astype(f32)
     inverse_scale = lax.rsqrt(jnp.mean(hidden * hidden, axis=1, keepdims=True) + norm_epsilon)
     normed = (hidden * inverse_scale * norm_gain[None, :]).astype(bf16)
@@ -852,20 +938,19 @@
     later = jnp.stack(later)
     cot_rel = [from_line(cotangent, k) for k in range(1, F)]
 
-    conv_x = jnp.concatenate([chan[: KW + 1], jnp.zeros((7 - KW, GW), f32)], axis=0)
-    conv_p = jnp.concatenate(
+    pair_params = jnp.concatenate(
         [conv_pair_weight, conv_pair_bias[None], jnp.zeros((7 - KW, NP), f32)], axis=0
     )
-    heads = jnp.pad(jnp.stack([bias_h, rate_h]), ((0, 6), (0, 128 - HG)))
-    wide_rows = jnp.concatenate(
-        [
-            chan[KW + 1][None],
-            jnp.repeat(skip_h, P_SIZE)[None],
-            jnp.full((1, GW), 1.0 / DI, f32),
-            jnp.zeros((5, GW), f32),
+    conv_x, conv_p, heads, wide_rows = call(
+        functools.partial(params_kernel, F, PF),
+        1,
+        [fixed(F, 8, 128), fixed(8, NP)],
+        [fixed(8, GW), fixed(8, NP), fixed(8, 128), fixed(8, GW)],
+        [
+            struct((8, GW), f32), struct((8, NP), f32), struct((8, 128), f32),
+            struct((8, GW), f32),
         ],
-        axis=0,
-    )
+    )(spot, small_here, pair_params)
     weight_pieces = [piece for pair in zip(pieces_a, pieces_b, strict=True) for piece in pair]
     (
         x_group, in_rows, pair_in, rawx, rawp, actx, actp, slopex, slopep, dt, cum, cumt,
@@ -956,7 +1041,6 @@
         spot, actx, actp, cum, total, y_intra, y_inter, gate, back_normed, wide_rows, *sums,
         out_rows,
     )
-    skip_part = jnp.sum(small_sums[1].reshape(HG, P_SIZE), axis=1)
     firsts = [from_part(first_back, k) for k in range(1, F)]
 
     def by_line(arrays):
@@ -976,27 +1060,32 @@
         pieces = by_line([mine.reshape(shape), twin(away).reshape(shape)])
         return sum(piece.astype(f32) for piece in pieces)
 
-    def partial_sums(lefts, rights, step):
+    def partial_sums(lefts, rights, extra):
         pairs = len(lefts)
-        rows = pairs * QW + (0 if step is None else 8)
-        extra = [] if step is None else [step]
+        rows = pairs * QW + (8 + 2 * PH if extra else 0)
         if Dl % 128 == 0:
             columns_of = pl.BlockSpec((TL, Dl), lambda i, p: (0, i))
             return call(
                 functools.partial(partial_blocks_kernel, F, pairs),
                 F,
-                [fixed(TL, GW)] * pairs + [columns_of] * pairs + [fixed(TL, 8)] * len(extra),
+                [fixed(TL, GW)] * pairs
+                + [columns_of] * pairs
+                + [fixed(*value.shape) for value in extra],
                 [pl.BlockSpec((1, rows, Dl), lambda i, p: (i, 0, 0))] * F,
                 [struct((F, rows, Dl), bf16)] * F,
-                [pltpu.VMEM((pairs, GW, TL), bf16), pltpu.VMEM((GW, Dl), f32)],
+                [pltpu.VMEM((pairs, GW, TL), bf16), pltpu.VMEM((GW, Dl), f32)]
+                + [pltpu.VMEM((NP, TL), bf16), pltpu.VMEM((NP, Dl), f32)] * bool(extra),
             )(spot, *lefts, *rights, *extra)
         return call(
             functools.partial(partial_kernel, F, pairs),
             blocks,
-            [rows_of(GW)] * pairs + [rows_of(D)] * pairs + [rows_of(8)] * len(extra),
+            [rows_of(GW)] * pairs
+            + [rows_of(D)] * pairs
+            + [rows_of(value.shape[1]) for value in extra],
             [fixed(F, rows, Dl)] * F,
             [struct((F, rows, Dl), bf16)] * F,
-            [pltpu.VMEM((GW, D), f32)] * pairs + [pltpu.VMEM((8, D), f32)] * len(extra),
+            [pltpu.VMEM((GW, D), f32)] * pairs
+            + [pltpu.VMEM((value.shape[1], D), f32) for value in extra],
         )(spot, *lefts, *rights, *extra)
 
     def share(pieces):
@@ -1006,7 +1095,7 @@
 
     block_out = (hidden + add_group(away, mine)).astype(bf16)
 
-    early = partial_sums([gated_normed, back_gate], [cot_group, x_group], None)
+    early = partial_sums([gated_normed, back_gate], [cot_group, x_group], ())
     early = [early[0]] + [from_part(early[k], k) for k in range(1, F)]
     early = share(by_line(early))
 
@@ -1050,79 +1139,46 @@
         )
 
     (
-        back_inner, pair_away, pair_mine, conv_x_part, conv_p_part, away, mine, gain_rows,
+        back_inner, back_pair, conv_x_part, conv_p_part, away, mine, gain_rows,
     ) = call(
         back_conv_kernel,
         blocks,
         [
             rows_of(GW), rows_of(NP), following(GW), following(NP), fixed(8, GW + NP),
             rows_of(GW), rows_of(NP), fixed(8, GW), fixed(8, NP), rows_of(GW), rows_of(8),
-            rows_of(D), fixed(GW, D), fixed(GW + 8, D),
+            rows_of(D), fixed(GW, D), fixed(GW + 8, D), fixed(NP, D),
         ],
         [
-            rows_of(GW), half_of(NP, 0), half_of(NP, 1), fixed(8, GW), fixed(8, NP),
+            rows_of(GW), rows_of(NP), fixed(8, GW), fixed(8, NP),
             half_of(D, 0), half_of(D, 1), fixed(8, D),
         ],
         [
-            struct((TL, GW), bf16), struct((TL // 2, NP), bf16), struct((TL // 2, NP), bf16),
-            struct((8, GW), f32), struct((8, NP), f32), struct((TL // 2, D), bf16),
+            struct((TL, GW), bf16), struct((TL, NP), bf16), struct((8, GW), f32), struct((8, NP), f32), struct((TL // 2, D), bf16),
             struct((TL // 2, D), bf16), struct((8, D), f32),
         ],
         [pltpu.VMEM((Q + 8, GW), f32), pltpu.VMEM((Q + 8, NP), f32)],
     )(
         spot, dprex, dprep, dprex, dprep, halo_back, rawx, rawp, conv_x, conv_p, back_gate,
-        back_step, x_group, gate_rows, in_rows,
-    )
-
-    late = partial_sums([back_inner], [x_group], back_step)
+        back_step, x_group, gate_rows, in_rows, pair_in,
+    )
+
+    late = partial_sums([back_inner], [x_group], (back_step, back_pair))
     late = [late[0]] + [from_part(late[k], k) for k in range(1, F)]
-    pair_own = add_group(pair_away, pair_mine).astype(bf16)
     back_in = add_group(away, mine)
     late = share(by_line(late))
 
-    rest_rel = [pair_own] + [from_line(pair_own, k) for k in range(1, F)]
-    rest_line = []
-    for j in range(F):
-        here = pair_own
-        for k in range(1, F):
-            here = jnp.where(lax.rem(f - k + F, F) == j, rest_rel[k], here)
-        rest_line.append(here)
-    rest_line = jnp.stack(rest_line)
-    rest_other = twin(rest_line)
-    rest = jnp.concatenate(
-        [jnp.where(c == 0, rest_line, rest_other), jnp.where(c == 0, rest_other, rest_line)],
-        axis=0,
-    )
-    pair_all = rest.reshape(TL, NP)
-    x_rows = lax.dynamic_slice(x_group, (0, f * Dl), (TL, Dl))
-    grad_rest = dot_f32(pair_all, x_rows, ((0,), (0,)))
-    for bit in bits:
-        grad_rest = grad_rest.astype(bf16)
-        grad_rest = grad_rest.astype(f32) + from_part(grad_rest, bit).astype(f32)
-
-    pair_again = lax.optimization_barrier(pair_own)
-    back_pair_in = dot_f32(pair_own, pair_in, ((1,), (0,)))
-    gain_part = gain_rows[0] + jnp.sum(
-        dot_f32(pair_again, pair_in, ((1,), (0,))) * normed.astype(f32), axis=0
-    )
-    gain_part = lax.optimization_barrier(gain_part / norm_gain)
-    per_channel = jnp.concatenate([conv_x_part[: KW + 1], small_sums[:1]], axis=0)
-    per_channel = jnp.transpose(per_channel.reshape(KW + 2, HG, F, PF), (2, 0, 1, 3))
-    per_channel = jnp.pad(
-        per_channel.reshape(F, KW + 2, HG * PF), ((0, 0), (0, 0), (0, 128 - HG * PF))
-    )
-    per_head = jnp.concatenate([head_sums[0, :HG], head_sums[1, :HG], skip_part])
-    per_head = jnp.broadcast_to(jnp.pad(per_head, (0, 128 - 3 * HG))[None, None], (F, 1, 128))
-    slots = jnp.concatenate([per_channel, per_head, jnp.zeros((F, 1, 128), f32)], axis=1)
-    shared = jnp.concatenate([conv_p_part[: KW + 1].reshape(-1), gain_part])
-    count = shared.shape[0]
-    lines = -(-count // 1024) * 8
-    shared = jnp.pad(shared, (0, lines * 128 - count)).reshape(lines, 128)
-    shared = shared + twin(shared)
-    small = jnp.concatenate([slots.reshape(F * 8, 128), shared], axis=0)
+    rows = F * 8 + 16 + -(-D // 1024) * 8
+    small = call(
+        functools.partial(pack_kernel, F, PF),
+        1,
+        [fixed(8, GW), fixed(8, GW), fixed(8, 8), fixed(8, NP), fixed(8, D), fixed(1, D)],
+        fixed(rows, 128),
+        struct((rows, 128), f32),
+    )(spot, conv_x_part, small_sums, head_sums, conv_p_part, gain_rows, norm_gain[None])
     for bit in bits:
         small = small + from_part(small, bit)
     slots, shared = small[: F * 8].reshape(F, 8, 128), small[F * 8 :]
+    shared = shared + twin(shared)
     for bit in bits:
         shared = shared + lax.ppermute(shared, "fsdp", [(i, i ^ bit) for i in range(F)])
     owners = [
@@ -1132,13 +1188,11 @@
         for ff in range(F)
     ]
     mine_small = lax.ppermute(take(slots, q), everyone, owners)
-    shared = shared.reshape(-1)
-    pair_grads = shared[: (KW + 1) * NP].reshape(KW + 1, NP)
-    gain_sum = shared[(KW + 1) * NP : count]
+    pair_grads = jnp.concatenate([shared[:8], shared[8:16]], axis=1)[: KW + 1]
+    gain_sum = shared[16:].reshape(-1)[:D]
     channel_grads = mine_small[: KW + 2, : HG * PF].reshape(KW + 2, HG, PF)
     head_grads = mine_small[KW + 2]
 
-    back_in = back_in + back_pair_in
     scaled_back = back_in * norm_gain[None, :]
     inverse_cubed = inverse_scale * inverse_scale * inverse_scale
     grad_input = (
@@ -1148,29 +1202,21 @@
     ).astype(bf16)
 
     E = in_weight.shape[1]
+    grad_in_weight, grad_out_weight = call(
+        functools.partial(early_grads_kernel, F),
+        S,
+        [fixed(F, 2 * QW, Dl)] * F + [fixed(F, F, 2 * QW, Dl)],
+        [pl.BlockSpec((GW, Dl), lambda i, p: (i, 0))] * 2,
+        [struct((E, Dl), f32), struct((DI, Dl), f32)],
+    )(spot, *early)
     grad_in_weight = call(
         functools.partial(late_grads_kernel, F, QW, HG),
         S + -(-(E - 2 * DI) // GW),
-        [fixed(F, QW + 8, Dl)] * F + [fixed(F, F, QW + 8, Dl)],
+        [fixed(F, QW + 8 + 2 * PH, Dl)] * F + [fixed(F, F, QW + 8 + 2 * PH, Dl), anywhere],
         pl.BlockSpec((GW, Dl), lambda i, p: (S + i, 0)),
         struct((E, Dl), f32),
-    )(spot, *late)
-    grad_in_weight, grad_out_weight = call(
-        functools.partial(early_grads_kernel, F),
-        S,
-        [fixed(F, 2 * QW, Dl)] * F + [fixed(F, F, 2 * QW, Dl), anywhere],
-        [pl.BlockSpec((GW, Dl), lambda i, p: (i, 0))] * 2,
-        [struct((E, Dl), f32), struct((DI, Dl), f32)],
         aliases={F + 2: 0},
-    )(spot, *early, grad_in_weight)
-    grad_in_weight = call(
-        pair_grads_kernel,
-        1,
-        [fixed(NP, Dl), anywhere],
-        pl.BlockSpec((NP, Dl), lambda i, p: (2 * DI // NP, 0)),
-        struct((E, Dl), f32),
-        aliases={2: 0},
-    )(spot, grad_rest, grad_in_weight)
+    )(spot, *late, grad_in_weight)
     grad_in_weight = jnp.transpose(grad_in_weight)
     return (
         block_out,

time: 518 us -> 529 us (1.021)
  waiting for transfers between devices: 136 us -> 179 us
  starting transfers between devices: 171 us -> 150 us
  local copies, waits for them, and re-layouts: 37.2 us -> 26.6 us
    all_to_all x1, waiting for transfers between devices: 0.01 us -> 18.2 us  [spread(): return lax.all_to_all(copies, axis, 0, 0, tiled=True)]
    ppermute x10 -> x8, starting transfers between devices: 14.7 us -> 0.93 us  [twin(): return lax.ppermute(value, 'seq', twins)]
    slice x15 -> x2, local copies, waits for them, and re-layouts: 13.5 us -> 1.3 us  [the longest x1 1.29 us: body(): gain_sum = shared[16:].reshape(-1)[:D]]
    ppermute x31 -> x29, starting transfers between devices: 45.9 us -> 34.4 us  [from_part(): return lax.ppermute(value, 'seq', [(i, i ^ k * R) for i in range(S)])]
    ppermute x31 -> x29, waiting for transfers between devices: 62.1 us -> 73.1 us  [from_part(): return lax.ppermute(value, 'seq', [(i, i ^ k * R) for i in range(S)])]
    ppermute x30 -> x24, waiting for transfers between devices: 52.9 us -> 61.3 us  [from_line(): return lax.ppermute(value, 'fsdp', [(i, (i + k) % F) for i in range(F)])]
    ppermute x2, starting transfers between devices: 7.4 us -> 13.3 us  [body(): lax.ppermute(shared, 'fsdp', [(i, i ^ bit) for i in range(F)])]
    ppermute x30 -> x24, starting transfers between devices: 84.3 us -> 81.1 us  [from_line(): return lax.ppermute(value, 'fsdp', [(i, (i + k) % F) for i in range(F)])]
  transfers between devices with their start and end apart: 84 -> 74, of which waited for: 25 -> 29; matrix products, arithmetic and copies ran while one was open for 11% -> 9% of each run, Pallas kernels for 19% -> 20%
where the time goes in v1:
time: 529 us; the launch traced here: 525 us
  waiting for transfers between devices  179 us (34%)
  starting transfers between devices  150 us (28%)
  Pallas kernels  139 us (26%)
  other arithmetic  29 us (5%)
  local copies, waits for them, and re-layouts  26.6 us (5%)
    ppermute x24, starting transfers between devices, from_line(): return lax.ppermute(value, 'fsdp', [(i, (i + k) % F) for i in range(F)])  81.1 us
    ppermute x29, waiting for transfers between devices, from_part(): return lax.ppermute(value, 'seq', [(i, i ^ k * R) for i in range(S)])  73.1 us
    ppermute x24, waiting for transfers between devices, from_line(): return lax.ppermute(value, 'fsdp', [(i, (i + k) % F) for i in range(F)])  61.3 us
    ppermute x29, starting transfers between devices, from_part(): return lax.ppermute(value, 'seq', [(i, i ^ k * R) for i in range(S)])  34.4 us
    all_to_all x1, waiting for transfers between devices, spread(): return lax.all_to_all(copies, axis, 0, 0, tiled=True)  18.2 us
    ppermute x3, waiting for transfers between devices, line_chain(): down = lax.ppermute(down, 'fsdp', [(i, i - 1) for i in range(1, F - k + 1)])  18.1 us
    pallas_call x4, Pallas kernels, by_line(): call(functools.partial(sum_kernel, F), F, [block] * len(arrays), [fixed(r...  18 us
    pallas_call x2, Pallas kernels, partial_sums(): call(functools.partial(partial_blocks_kernel, F, pairs), F, [fixed(TL, GW...  16.7 us
  transfers between devices with their start and end apart: 74, of which 29 were waited for; matrix products, arithmetic and copies ran while one was open for 9% of the time, Pallas kernels for 20%

profile of v1, /device:TPU:0, one launch (start us, length us, event | category | flops | bytes accessed | tf_op | source)
XLA Modules:
  0.0 524.5 jit_solution(2645427665431697548)
XLA Ops:
  4.8 5.6 %collective-permute-start = (bf16[128,1536]{1,0:T(8,128)(2,1)S(1)}, bf16[128,1536]{1,0:T(8,128)(2,1)S(1)}, u32[]{:S(2)}, u32[]{:S(2)}) collective-permute-start(bf16[128,1536]{1,0:T(8,128)(2,1)S(1)} %fusion.2), channel_id=1, source_target_pairs={{0,1},{1,2},{2,3},{4,5},{5,6},{6,7},{8,9},{9,10},{10,11},{12,13},{... | collective-permute-start | bytes 1179656 | tf_op jit(solution)/shard_map/ppermute | solution.py:788
  23.0 15.4 %collective-permute-done.11 = bf16[168,384]{1,0:T(8,128)(2,1)S(1)} collective-permute-done((bf16[168,384]{1,0:T(8,128)(2,1)S(1)}, bf16[168,384]{1,0:T(8,128)(2,1)S(1)}, u32[]{:S(2)}, u32[]{:S(2)}) %collective-permute-start.11) | collective-permute-done | bytes 129056 | tf_op jit(solution)/shard_map/ppermute | solution.py:780
  38.5 8.5 %collective-permute-start.10 = (bf16[168,384]{1,0:T(8,128)(2,1)S(1)}, bf16[168,384]{1,0:T(8,128)(2,1)S(1)}, u32[]{:S(2)}, u32[]{:S(2)}) collective-permute-start(bf16[168,384]{1,0:T(8,128)(2,1)S(1)} %constant_dynamic-update-slice_fusion.3), channel_id=1, source_target_pairs={{0,2},{1,3},{2,0},{3,1},{4,6},{5,7},{6,4},{7,5},{8,10},{9,11},{10,... | collective-permute-start | bytes 387080 | tf_op jit(solution)/shard_map/ppermute | solution.py:780
  54.9 5.9 %collective-permute-done.9 = bf16[168,384]{1,0:T(8,128)(2,1)S(1)} collective-permute-done((bf16[168,384]{1,0:T(8,128)(2,1)}, bf16[168,384]{1,0:T(8,128)(2,1)S(1)}, u32[]{:S(2)}, u32[]{:S(2)}) %collective-permute-start.9) | collective-permute-done | bytes 129056 | tf_op jit(solution)/shard_map/ppermute | solution.py:780
  63.5 5.1 collective-permute-start.23
  76.8 5.6 %collective-permute-done.4 = bf16[128,1536]{1,0:T(8,128)(2,1)S(1)} collective-permute-done((bf16[128,1536]{1,0:T(8,128)(2,1)S(1)}, bf16[128,1536]{1,0:T(8,128)(2,1)S(1)}, u32[]{:S(2)}, u32[]{:S(2)}) %collective-permute-start.4) | collective-permute-done | bytes 393248 | tf_op jit(solution)/shard_map/ppermute | solution.py:789
  84.6 12.4 %collective-permute-done.5 = bf16[128,1536]{1,0:T(8,128)(2,1)S(1)} collective-permute-done((bf16[128,1536]{1,0:T(8,128)(2,1)S(1)}, bf16[128,1536]{1,0:T(8,128)(2,1)S(1)}, u32[]{:S(2)}, u32[]{:S(2)}) %collective-permute-start.5) | collective-permute-done | bytes 393248 | tf_op jit(solution)/shard_map/ppermute | solution.py:789
  125.7 4.9 all-to-all-start
  134.5 18.2 %all-to-all-done = f32[32,8,128]{2,1,0:T(8,128)} async-done(((f32[32,8,128]{2,1,0:T(8,128)}), f32[32,8,128]{2,1,0:T(8,128)}, u32[]{:S(2)}, u32[]{:S(2)}) %all-to-all-start) | async-done | bytes 131104 | tf_op jit(solution)/shard_map/all_to_all | solution.py:27
  156.5 15.2 %shard_map.229 = (bf16[1024,1536]{1,0:T(8,128)(2,1)}, bf16[392,1536]{1,0:T(8,128)(2,1)}, bf16[256,1536]{1,0:T(8,128)(2,1)}, bf16[1024,384]{1,0:T(8,128)(2,1)}, b...) custom-call(s32[3]{0:T(128)} %pad_add_fusion.spot_ref, ...), custom_call_target="tpu_custom_call" | custom-call | tf_op jit(solution)/shard_map/pallas_call | solution.py:958
  175.3 6.0 %shard_map.230.y_ref = f32[1024,384]{1,0:T(8,128)} custom-call(s32[3]{0:T(128)} %pad_add_fusion.spot_ref, bf16[1024,384]{1,0:T(8,128)(2,1)} %get-tuple-element.95.actx_ref, bf16[1024,256]{1,0:T(8,128)(2,1)} %get-tuple-element.96.actp_ref, f32[1024,8]{1,0:T(8,128)} %get-tuple-element.99.dt_ref, f32[1024,8]{1,0:T(8,128)} %get-tuple-element.97.cum_ref, ...), custom_call_target="tpu_custom_call" | custom-call | tf_op jit(solution)/shard_map/pallas_call | solution.py:989
  181.4 9.9 %shard_map.231 = (bf16[1024,1536]{1,0:T(8,128)(2,1)}, bf16[384,1536]{1,0:T(8,128)(2,1)}, bf16[384,1536]{1,0:T(8,128)(2,1)}, bf16[1024,384]{1,0:T(8,128)(2,1)}, bf16[1024,384]{1,0:T(8,128)(2,1)}) custom-call(s32[3]{0:T(128)} %pad_add_fusion.spot_ref, bf16[512,1536]{1,0:T(8,128)(2,1)} %copy-done.2, bf16[512,1536]{1,0:T(8,128)(2,1)} %collective-permute-done.21.other_ref, ...), custom_call_target="tpu_custom_call" | custom-call | tf_op jit(solution)/shard_map/pallas_call | solution.py:996
  192.1 6.9 %shard_map.232 = (f32[1024,384]{1,0:T(8,128)}, bf16[4,128,384]{2,1,0:T(8,128)(2,1)}, f32[8,1024]{1,0:T(8,128)}) custom-call(s32[3]{0:T(128)} %pad_add_fusion.spot_ref, bf16[1024,384]{1,0:T(8,128)(2,1)} %get-tuple-element.95.actx_ref, bf16[1024,256]{1,0:T(8,128)(2,1)} %get-tuple-element.96.actp_ref, f32[1024,8]{1,0:T(8,128)} %get-tuple-element.97.cum_ref, ...), custom_call_target="tpu_custom_call" | custom-call | tf_op jit(solution)/shard_map/pallas_call | solution.py:1006
  208.5 12.3 %shard_map.233 = (bf16[1024,384]{1,0:T(8,128)(2,1)}, bf16[1024,384]{1,0:T(8,128)(2,1)}, bf16[1024,384]{1,0:T(8,128)(2,1)}, f32[4,128,384]{2,1,0:T(8,128)}, f32[1...) custom-call(s32[3]{0:T(128)} %pad_add_fusion.spot_ref, ...), custom_call_target="tpu_custom_call" | custom-call | tf_op jit(solution)/shard_map/pallas_call | solution.py:1021
  220.9 8.8 %shard_map.242 = (bf16[4,192,384]{2,1,0:T(8,128)(2,1)}, bf16[4,192,384]{2,1,0:T(8,128)(2,1)}, bf16[4,192,384]{2,1,0:T(8,128)(2,1)}, bf16[4,192,384]{2,1,0:T(8,128)(2,1)}) custom-call(s32[3]{0:T(128)} %pad_add_fusion.spot_ref, bf16[1024,384]{1,0:T(8,128)(2,1)} %get-tuple-element.159.refs_0_, bf16[1024,384]{1,0:T(8,128)(2,1)} %get-tuple-element.133.bgate_ref.refs_1_, ...), custom_call_target="tpu_custom_call" | custom-call | tf_op jit(solution)/shard_map/pallas_call | solution.py:1068
  235.6 26.5 %collective-permute-done.41.refs_5_ = f32[128,384]{1,0:T(8,128)S(1)} collective-permute-done((f32[128,384]{1,0:T(8,128)S(1)}, f32[128,384]{1,0:T(8,128)S(1)}, u32[]{:S(2)}, u32[]{:S(2)}) %collective-permute-start.41) | collective-permute-done | bytes 196640 | tf_op jit(solution)/shard_map/ppermute | solution.py:777
  263.7 8.6 %shard_map.235 = (f32[1024,384]{1,0:T(8,128)}, f32[1024,256]{1,0:T(8,128)}) custom-call(s32[3]{0:T(128)} %pad_add_fusion.spot_ref, bf16[1024,384]{1,0:T(8,128)(2,1)} %get-tuple-element.95.actx_ref, bf16[1024,256]{1,0:T(8,128)(2,1)} %get-tuple-element.96.actp_ref, f32[1024,8]{1,0:T(8,128)} %get-tuple-element.99.dt_ref, f32[1024,8]{1,0:T(8,128)} %get-tuple-element.97.cum_ref, ...), custom_call_target="tpu_custom_call" | custom-call | tf_op jit(solution)/shard_map/pallas_call | solution.py:1102
  273.1 11.1 %shard_map.236 = (f32[1024,384]{1,0:T(8,128)}, f32[1024,256]{1,0:T(8,128)}, f32[1024,8]{1,0:T(8,128)}, f32[8,8]{1,0:T(8,128)}, f32[8,640]{1,0:T(8,128)}) custom-call(s32[3]{0:T(128)} %pad_add_fusion.spot_ref, bf16[1024,384]{1,0:T(8,128)(2,1)} %get-tuple-element.95.actx_ref, bf16[1024,256]{1,0:T(8,128)(2,1)} %get-tuple-element.96.actp_ref, ...), custom_call_target="tpu_custom_call" | custom-call | tf_op jit(solution)/shard_map/pallas_call | solution.py:1113
  290.7 13.4 %shard_map.237 = (bf16[1024,384]{1,0:T(8,128)(2,1)}, bf16[1024,256]{1,0:T(8,128)(2,1)}, f32[8,384]{1,0:T(8,128)}, f32[8,256]{1,0:T(8,128)}, bf16[512,1536]{1,0:T...) custom-call(s32[3]{0:T(128)} %pad_add_fusion.spot_ref, f32[1024,384]{1,0:T(8,128)} %get-tuple-element.128.dprex_ref.nextx_ref, ...), custom_call_target="tpu_custom_call" | custom-call | tf_op jit(solution)/shard_map/pallas_call | solution.py:1143
  304.1 8.0 %shard_map.240 = (bf16[4,168,384]{2,1,0:T(8,128)(2,1)}, bf16[4,168,384]{2,1,0:T(8,128)(2,1)}, bf16[4,168,384]{2,1,0:T(8,128)(2,1)}, bf16[4,168,384]{2,1,0:T(8,128)(2,1)}) custom-call(s32[3]{0:T(128)} %pad_add_fusion.spot_ref, bf16[1024,384]{1,0:T(8,128)(2,1)} %get-tuple-element.149.refs_0_, bf16[1024,1536]{1,0:T(8,128)(2,1)} %get-tuple-element.105.x_ref.refs_1_.refs_3_, ...), custom_call_target="tpu_custom_call" | custom-call | tf_op jit(solution)/shard_map/pallas_call | solution.py:1068
  338.0 18.9 %collective-permute-done.53.refs_2_ = bf16[4,168,384]{2,1,0:T(8,128)(2,1)} collective-permute-done((bf16[4,168,384]{2,1,0:T(8,128)(2,1)}, bf16[4,168,384]{2,1,0:T(8,128)(2,1)}, u32[]{:S(2)}, u32[]{:S(2)}) %collective-permute-start.53) | collective-permute-done | bytes 516128 | tf_op jit(solution)/shard_map/ppermute | solution.py:777
  379.3 6.5 %collective-permute-done.56 = bf16[168,384]{1,0:T(8,128)(2,1)S(1)} collective-permute-done((bf16[168,384]{1,0:T(8,128)(2,1)}, bf16[168,384]{1,0:T(8,128)(2,1)S(1)}, u32[]{:S(2)}, u32[]{:S(2)}) %collective-permute-start.56) | collective-permute-done | bytes 129056 | tf_op jit(solution)/shard_map/ppermute | solution.py:780
  394.2 9.9 %collective-permute-done.60.refs_3_ = bf16[4,168,384]{2,1,0:T(8,128)(2,1)} collective-permute-done((bf16[4,168,384]{2,1,0:T(8,128)(2,1)}, bf16[4,168,384]{2,1,0:T(8,128)(2,1)}, u32[]{:S(2)}, u32[]{:S(2)}) %collective-permute-start.60) | collective-permute-done | bytes 516128 | tf_op jit(solution)/shard_map/ppermute | solution.py:777
  404.1 9.6 %collective-permute-done.59.refs_2_ = bf16[4,168,384]{2,1,0:T(8,128)(2,1)} collective-permute-done((bf16[4,168,384]{2,1,0:T(8,128)(2,1)}, bf16[4,168,384]{2,1,0:T(8,128)(2,1)}, u32[]{:S(2)}, u32[]{:S(2)}) %collective-permute-start.59) | collective-permute-done | bytes 516128 | tf_op jit(solution)/shard_map/ppermute | solution.py:777
  417.4 8.3 %collective-permute-start.50 = (f32[32,128]{1,0:T(8,128)S(1)}, f32[32,128]{1,0:T(8,128)S(1)}, u32[]{:S(2)}, u32[]{:S(2)}) collective-permute-start(f32[32,128]{1,0:T(8,128)S(1)} %get-tuple-element.227), channel_id=1, source_target_pairs={{0,1},{1,0},{2,3},{3,2},{4,5},{5,4},{6,7},{7,6},{8,9},{9,8},{10,11... | collective-permute-start | bytes 49160 | tf_op jit(solution)/shard_map/ppermute | solution.py:1183
  427.4 5.1 collective-permute-start.51
  447.3 4.9 shard_map.234
  453.7 14.6 %collective-permute-start.36 = (bf16[128,1536]{1,0:T(8,128)(2,1)}, bf16[128,1536]{1,0:T(8,128)(2,1)S(1)}, u32[]{:S(2)}, u32[]{:S(2)}) collective-permute-start(bf16[128,1536]{1,0:T(8,128)(2,1)} %get-tuple-element.116), channel_id=1, source_target_pairs={{0,1},{1,2},{2,3},{3,0},{4,5},{5,6},{6,7},{7,4},{8,9},{9,10},{10,1... | collective-permute-start | bytes 1179656 | tf_op jit(solution)/shard_map/ppermute | solution.py:780
  470.7 22.4 %collective-permute-start.38 = (bf16[128,1536]{1,0:T(8,128)(2,1)}, bf16[128,1536]{1,0:T(8,128)(2,1)S(1)}, u32[]{:S(2)}, u32[]{:S(2)}) collective-permute-start(bf16[128,1536]{1,0:T(8,128)(2,1)} %get-tuple-element.118), channel_id=1, source_target_pairs={{0,3},{1,0},{2,1},{3,2},{4,7},{5,4},{6,5},{7,6},{8,11},{9,8},{10,9... | collective-permute-start | bytes 1179656 | tf_op jit(solution)/shard_map/ppermute | solution.py:780
  494.6 6.5 %collective-permute-done.37 = bf16[128,1536]{1,0:T(8,128)(2,1)S(1)} collective-permute-done((bf16[128,1536]{1,0:T(8,128)(2,1)}, bf16[128,1536]{1,0:T(8,128)(2,1)S(1)}, u32[]{:S(2)}, u32[]{:S(2)}) %collective-permute-start.37) | collective-permute-done | bytes 393248 | tf_op jit(solution)/shard_map/ppermute | solution.py:780
  509.2 7.9 %shard_map.244 = (f32[6448,384]{1,0:T(8,128)}, f32[3072,384]{1,0:T(8,128)}) custom-call(s32[3]{0:T(128)} %pad_add_fusion.spot_ref, bf16[4,192,384]{2,1,0:T(8,128)(2,1)} %copy-done.6, bf16[4,192,384]{2,1,0:T(8,128)(2,1)} %copy-done.5, bf16[4,192,384]{2,1,0:T(8,128)(2,1)} %copy-done.4, bf16[4,192,384]{2,1,0:T(8,128)(2,1)} %copy-done.3, ...), custom_call_target="tpu_custom_call" | custom-call | tf_op jit(solution)/shard_map/pallas_call | solution.py:1205
  517.1 7.4 %shard_map.245 = f32[6448,384]{1,0:T(8,128)} custom-call(s32[3]{0:T(128)} %pad_add_fusion.spot_ref, bf16[4,168,384]{2,1,0:T(8,128)(2,1)} %get-tuple-element.213.refs_0_, bf16[4,168,384]{2,1,0:T(8,128)(2,1)} %collective-permute-done.58.refs_1_, bf16[4,168,384]{2,1,0:T(8,128)(2,1)} %collective-permute-done.59.refs_2_, ...), custom_call_target="tpu_custom_call", output_to_operand_aliasing={{}: (6, {})} | custom-call | tf_op jit(solution)/shard_map/pallas_call | solution.py:1212
  (297 shorter events, 192.7 us)
Async XLA Ops:
  3.5 57.2 %collective-permute-start.3 = (bf16[128,1536]{1,0:T(8,128)(2,1)S(1)}, bf16[128,1536]{1,0:T(8,128)(2,1)S(1)}, u32[]{:S(2)}, u32[]{:S(2)}) collective-permute-start(bf16[128,1536]{1,0:T(8,128)(2,1)S(1)} %fusion.2), channel_id=1, source_target_pairs={{1,0},{2,1},{3,2},{5,4},{6,5},{7,6},{9,8},{10,9},{11,10},{13,12},{... | collective-permute-start | bytes 1179656 | tf_op jit(solution)/shard_map/ppermute | solution.py:789
  4.8 57.2 %collective-permute-start = (bf16[128,1536]{1,0:T(8,128)(2,1)S(1)}, bf16[128,1536]{1,0:T(8,128)(2,1)S(1)}, u32[]{:S(2)}, u32[]{:S(2)}) collective-permute-start(bf16[128,1536]{1,0:T(8,128)(2,1)S(1)} %fusion.2), channel_id=1, source_target_pairs={{0,1},{1,2},{2,3},{4,5},{5,6},{6,7},{8,9},{9,10},{10,11},{12,13},{... | collective-permute-start | bytes 1179656 | tf_op jit(solution)/shard_map/ppermute | solution.py:788
  10.5 53.1 %collective-permute-start.20 = (bf16[128,1536]{1,0:T(8,128)(2,1)}, bf16[128,1536]{1,0:T(8,128)(2,1)S(1)}, u32[]{:S(2)}, u32[]{:S(2)}) collective-permute-start(bf16[128,1536]{1,0:T(8,128)(2,1)} %param.25), channel_id=1, source_target_pairs={{0,3},{1,0},{2,1},{3,2},{4,7},{5,4},{6,5},{7,6},{8,11},{9,8},{10,9... | collective-permute-start | bytes 1179656 | tf_op jit(solution)/shard_map/ppermute | solution.py:780
  12.4 56.2 %collective-permute-start.19 = (bf16[128,1536]{1,0:T(8,128)(2,1)}, bf16[128,1536]{1,0:T(8,128)(2,1)S(1)}, u32[]{:S(2)}, u32[]{:S(2)}) collective-permute-start(bf16[128,1536]{1,0:T(8,128)(2,1)} %param.25), channel_id=1, source_target_pairs={{0,2},{1,3},{2,0},{3,1},{4,6},{5,7},{6,4},{7,5},{8,10},{9,11},{10,... | collective-permute-start | bytes 1179656 | tf_op jit(solution)/shard_map/ppermute | solution.py:780
  63.5 36.1 %collective-permute-start.23 = (bf16[192,384]{1,0:T(8,128)(2,1)S(1)}, bf16[192,384]{1,0:T(8,128)(2,1)S(1)}, u32[]{:S(2)}, u32[]{:S(2)}) collective-permute-start(bf16[192,384]{1,0:T(8,128)(2,1)S(1)} %pad_maximum_fusion.10), channel_id=1, source_target_pairs={{0,2},{1,3},{2,0},{3,1},{4,6},{5,7},{6,4},{7,5},{8,10},{9,11},{10,... | collective-permute-start | bytes 442376 | tf_op jit(solution)/shard_map/ppermute | solution.py:780
  68.6 32.3 %collective-permute-start.24 = (bf16[192,384]{1,0:T(8,128)(2,1)}, bf16[192,384]{1,0:T(8,128)(2,1)S(1)}, u32[]{:S(2)}, u32[]{:S(2)}) collective-permute-start(bf16[192,384]{1,0:T(8,128)(2,1)} %pad_maximum_fusion.11), channel_id=1, source_target_pairs={{0,3},{1,0},{2,1},{3,2},{4,7},{5,4},{6,5},{7,6},{8,11},{9,8},{10,9... | collective-permute-start | bytes 442376 | tf_op jit(solution)/shard_map/ppermute | solution.py:780
  73.9 28.2 %collective-permute-start.22 = (bf16[192,384]{1,0:T(8,128)(2,1)}, bf16[192,384]{1,0:T(8,128)(2,1)}, u32[]{:S(2)}, u32[]{:S(2)}) collective-permute-start(bf16[192,384]{1,0:T(8,128)(2,1)} %pad_maximum_fusion.9), channel_id=1, source_target_pairs={{0,1},{1,2},{2,3},{3,0},{4,5},{5,6},{6,7},{7,4},{8,9},{9,10},{10,1... | collective-permute-start | bytes 442376 | tf_op jit(solution)/shard_map/ppermute | solution.py:780
  99.1 57.4 %collective-permute-start.6 = (bf16[512,1536]{1,0:T(8,128)(2,1)S(1)}, bf16[512,1536]{1,0:T(8,128)(2,1)}, u32[]{:S(2)}, u32[]{:S(2)}) collective-permute-start(bf16[512,1536]{1,0:T(8,128)(2,1)S(1)} %pad_maximum_fusion.2.mine_ref), channel_id=1, source_target_pairs={{0,4},{4,0},{8,12},{12,8},{16,20},{20,16},{24,28},{28,24},{1,5},{5... | collective-permute-start | bytes 4718600 | tf_op jit(solution)/shard_map/ppermute | solution.py:774
  99.7 81.7 %collective-permute-start.21 = (bf16[512,1536]{1,0:T(8,128)(2,1)S(1)}, bf16[512,1536]{1,0:T(8,128)(2,1)}, u32[]{:S(2)}, u32[]{:S(2)}) collective-permute-start(bf16[512,1536]{1,0:T(8,128)(2,1)S(1)} %pad_maximum_fusion.3.mine_ref), channel_id=1, source_target_pairs={{0,4},{4,0},{8,12},{12,8},{16,20},{20,16},{24,28},{28,24},{1,5},{5... | collective-permute-start | bytes 4718600 | tf_op jit(solution)/shard_map/ppermute | solution.py:774
  121.3 52.2 %collective-permute-start.27 = (bf16[4,192,384]{2,1,0:T(8,128)(2,1)}, bf16[4,192,384]{2,1,0:T(8,128)(2,1)}, u32[]{:S(2)}, u32[]{:S(2)}) collective-permute-start(bf16[4,192,384]{2,1,0:T(8,128)(2,1)} %pad_maximum_fusion.4.refs_0_), channel_id=1, source_target_pairs={{0,24},{4,28},{8,16},{12,20},{16,8},{20,12},{24,0},{28,4},{1,25},{... | collective-permute-start | bytes 1769480 | tf_op jit(solution)/shard_map/ppermute | solution.py:777
  123.2 51.1 %collective-permute-start.26 = (bf16[4,192,384]{2,1,0:T(8,128)(2,1)}, bf16[4,192,384]{2,1,0:T(8,128)(2,1)}, u32[]{:S(2)}, u32[]{:S(2)}) collective-permute-start(bf16[4,192,384]{2,1,0:T(8,128)(2,1)} %pad_maximum_fusion.4.refs_0_), channel_id=1, source_target_pairs={{0,16},{4,20},{8,24},{12,28},{16,0},{20,4},{24,8},{28,12},{1,17},{... | collective-permute-start | bytes 1769480 | tf_op jit(solution)/shard_map/ppermute | solution.py:777
  125.7 27.0 %all-to-all-start = ((f32[32,8,128]{2,1,0:T(8,128)}), f32[32,8,128]{2,1,0:T(8,128)}, u32[]{:S(2)}, u32[]{:S(2)}) async-start(f32[32,8,128]{2,1,0:T(8,128)} %broadcast_in_dim.27), calls=%async_computation | async-start | bytes 262144 | tf_op jit(solution)/shard_map/all_to_all | solution.py:27
  130.6 50.7 %collective-permute-start.25 = (bf16[4,192,384]{2,1,0:T(8,128)(2,1)}, bf16[4,192,384]{2,1,0:T(8,128)(2,1)}, u32[]{:S(2)}, u32[]{:S(2)}) collective-permute-start(bf16[4,192,384]{2,1,0:T(8,128)(2,1)} %pad_maximum_fusion.4.refs_0_), channel_id=1, source_target_pairs={{0,8},{4,12},{8,0},{12,4},{16,24},{20,28},{24,16},{28,20},{1,9},{5... | collective-permute-start | bytes 1769480 | tf_op jit(solution)/shard_map/ppermute | solution.py:777
  229.7 85.1 %collective-permute-start.62 = (bf16[4,192,384]{2,1,0:T(8,128)(2,1)}, bf16[4,192,384]{2,1,0:T(8,128)(2,1)S(1)}, u32[]{:S(2)}, u32[]{:S(2)}) collective-permute-start(bf16[4,192,384]{2,1,0:T(8,128)(2,1)} %get-tuple-element.162), channel_id=1, source_target_pairs={{0,8},{4,12},{8,0},{12,4},{16,24},{20,28},{24,16},{28,20},{1,9},{5... | collective-permute-start | bytes 1769480 | tf_op jit(solution)/shard_map/ppermute | solution.py:777
  230.6 84.1 %collective-permute-start.63 = (bf16[4,192,384]{2,1,0:T(8,128)(2,1)}, bf16[4,192,384]{2,1,0:T(8,128)(2,1)S(1)}, u32[]{:S(2)}, u32[]{:S(2)}) collective-permute-start(bf16[4,192,384]{2,1,0:T(8,128)(2,1)} %get-tuple-element.163), channel_id=1, source_target_pairs={{0,16},{4,20},{8,24},{12,28},{16,0},{20,4},{24,8},{28,12},{1,17},{... | collective-permute-start | bytes 1769480 | tf_op jit(solution)/shard_map/ppermute | solution.py:777
  231.8 82.9 %collective-permute-start.64 = (bf16[4,192,384]{2,1,0:T(8,128)(2,1)}, bf16[4,192,384]{2,1,0:T(8,128)(2,1)S(1)}, u32[]{:S(2)}, u32[]{:S(2)}) collective-permute-start(bf16[4,192,384]{2,1,0:T(8,128)(2,1)} %get-tuple-element.164), channel_id=1, source_target_pairs={{0,24},{4,28},{8,16},{12,20},{16,8},{20,12},{24,0},{28,4},{1,25},{... | collective-permute-start | bytes 1769480 | tf_op jit(solution)/shard_map/ppermute | solution.py:777
  233.1 29.0 %collective-permute-start.41 = (f32[128,384]{1,0:T(8,128)S(1)}, f32[128,384]{1,0:T(8,128)S(1)}, u32[]{:S(2)}, u32[]{:S(2)}) collective-permute-start(f32[128,384]{1,0:T(8,128)S(1)} %copy-done.41), channel_id=1, source_target_pairs={{0,24},{4,28},{8,16},{12,20},{16,8},{20,12},{24,0},{28,4},{1,25},{... | collective-permute-start | bytes 589832 | tf_op jit(solution)/shard_map/ppermute | solution.py:777
  234.8 37.6 %collective-permute-start.40 = (f32[128,384]{1,0:T(8,128)S(1)}, f32[128,384]{1,0:T(8,128)S(1)}, u32[]{:S(2)}, u32[]{:S(2)}) collective-permute-start(f32[128,384]{1,0:T(8,128)S(1)} %copy-done.41), channel_id=1, source_target_pairs={{0,16},{4,20},{8,24},{12,28},{16,0},{20,4},{24,8},{28,12},{1,17},{... | collective-permute-start | bytes 589832 | tf_op jit(solution)/shard_map/ppermute | solution.py:777
  320.3 36.6 %collective-permute-start.53 = (bf16[4,168,384]{2,1,0:T(8,128)(2,1)}, bf16[4,168,384]{2,1,0:T(8,128)(2,1)}, u32[]{:S(2)}, u32[]{:S(2)}) collective-permute-start(bf16[4,168,384]{2,1,0:T(8,128)(2,1)} %get-tuple-element.153), channel_id=1, source_target_pairs={{0,16},{4,20},{8,24},{12,28},{16,0},{20,4},{24,8},{28,12},{1,17},{... | collective-permute-start | bytes 1548296 | tf_op jit(solution)/shard_map/ppermute | solution.py:777
  320.3 36.6 %collective-permute-start.54 = (bf16[4,168,384]{2,1,0:T(8,128)(2,1)}, bf16[4,168,384]{2,1,0:T(8,128)(2,1)}, u32[]{:S(2)}, u32[]{:S(2)}) collective-permute-start(bf16[4,168,384]{2,1,0:T(8,128)(2,1)} %get-tuple-element.154), channel_id=1, source_target_pairs={{0,24},{4,28},{8,16},{12,20},{16,8},{20,12},{24,0},{28,4},{1,25},{... | collective-permute-start | bytes 1548296 | tf_op jit(solution)/shard_map/ppermute | solution.py:777
  334.5 53.8 %collective-permute-start.70 = (bf16[4,192,384]{2,1,0:T(8,128)(2,1)S(1)}, bf16[4,192,384]{2,1,0:T(8,128)(2,1)S(1)}, u32[]{:S(2)}, u32[]{:S(2)}) collective-permute-start(bf16[4,192,384]{2,1,0:T(8,128)(2,1)S(1)} %get-tuple-element.211.refs_0_), channel_id=1, source_target_pairs={{0,24},{4,28},{8,16},{12,20},{16,8},{20,12},{24,0},{28,4},{1,25},{... | collective-permute-start | bytes 1769480 | tf_op jit(solution)/shard_map/ppermute | solution.py:777
  334.9 54.1 %collective-permute-start.69 = (bf16[4,192,384]{2,1,0:T(8,128)(2,1)S(1)}, bf16[4,192,384]{2,1,0:T(8,128)(2,1)S(1)}, u32[]{:S(2)}, u32[]{:S(2)}) collective-permute-start(bf16[4,192,384]{2,1,0:T(8,128)(2,1)S(1)} %get-tuple-element.211.refs_0_), channel_id=1, source_target_pairs={{0,16},{4,20},{8,24},{12,28},{16,0},{20,4},{24,8},{28,12},{1,17},{... | collective-permute-start | bytes 1769480 | tf_op jit(solution)/shard_map/ppermute | solution.py:777
  336.7 53.3 %collective-permute-start.68 = (bf16[4,192,384]{2,1,0:T(8,128)(2,1)S(1)}, bf16[4,192,384]{2,1,0:T(8,128)(2,1)S(1)}, u32[]{:S(2)}, u32[]{:S(2)}) collective-permute-start(bf16[4,192,384]{2,1,0:T(8,128)(2,1)S(1)} %get-tuple-element.211.refs_0_), channel_id=1, source_target_pairs={{0,8},{4,12},{8,0},{12,4},{16,24},{20,28},{24,16},{28,20},{1,9},{5... | collective-permute-start | bytes 1769480 | tf_op jit(solution)/shard_map/ppermute | solution.py:777
  385.7 48.8 %collective-permute-start.43 = (bf16[512,1536]{1,0:T(8,128)(2,1)}, bf16[512,1536]{1,0:T(8,128)(2,1)}, u32[]{:S(2)}, u32[]{:S(2)}) collective-permute-start(bf16[512,1536]{1,0:T(8,128)(2,1)} %get-tuple-element.139), channel_id=1, source_target_pairs={{0,4},{4,0},{8,12},{12,8},{16,20},{20,16},{24,28},{28,24},{1,5},{5... | collective-permute-start | bytes 4718600 | tf_op jit(solution)/shard_map/ppermute | solution.py:774
  385.7 58.2 %collective-permute-start.35 = (bf16[512,1536]{1,0:T(8,128)(2,1)}, bf16[512,1536]{1,0:T(8,128)(2,1)}, u32[]{:S(2)}, u32[]{:S(2)}) collective-permute-start(bf16[512,1536]{1,0:T(8,128)(2,1)} %get-tuple-element.114), channel_id=1, source_target_pairs={{0,4},{4,0},{8,12},{12,8},{16,20},{20,16},{24,28},{28,24},{1,5},{5... | collective-permute-start | bytes 4718600 | tf_op jit(solution)/shard_map/ppermute | solution.py:774
  404.1 103.7 %collective-permute-start.71 = (bf16[4,4,192,384]{3,2,1,0:T(8,128)(2,1)}, bf16[4,4,192,384]{3,2,1,0:T(8,128)(2,1)S(1)}, u32[]{:S(2)}, u32[]{:S(2)}) collective-permute-start(bf16[4,4,192,384]{3,2,1,0:T(8,128)(2,1)} %pad_maximum_fusion), channel_id=1, source_target_pairs={{0,4},{4,0},{8,12},{12,8},{16,20},{20,16},{24,28},{28,24},{1,5},{5... | collective-permute-start | bytes 7077896 | tf_op jit(solution)/shard_map/ppermute | solution.py:774
  416.7 100.4 %collective-permute-start.61 = (bf16[4,4,168,384]{3,2,1,0:T(8,128)(2,1)}, bf16[4,4,168,384]{3,2,1,0:T(8,128)(2,1)}, u32[]{:S(2)}, u32[]{:S(2)}) collective-permute-start(bf16[4,4,168,384]{3,2,1,0:T(8,128)(2,1)} %pad_maximum_fusion.1), channel_id=1, source_target_pairs={{0,4},{4,0},{8,12},{12,8},{16,20},{20,16},{24,28},{28,24},{1,5},{5... | collective-permute-start | bytes 6193160 | tf_op jit(solution)/shard_map/ppermute | solution.py:774
  441.4 29.2 %collective-permute-start.45 = (bf16[128,1536]{1,0:T(8,128)(2,1)}, bf16[128,1536]{1,0:T(8,128)(2,1)}, u32[]{:S(2)}, u32[]{:S(2)}) collective-permute-start(bf16[128,1536]{1,0:T(8,128)(2,1)} %get-tuple-element.142), channel_id=1, source_target_pairs={{0,2},{1,3},{2,0},{3,1},{4,6},{5,7},{6,4},{7,5},{8,10},{9,11},{10,... | collective-permute-start | bytes 1179656 | tf_op jit(solution)/shard_map/ppermute | solution.py:780
  444.0 26.7 %collective-permute-start.46 = (bf16[128,1536]{1,0:T(8,128)(2,1)}, bf16[128,1536]{1,0:T(8,128)(2,1)}, u32[]{:S(2)}, u32[]{:S(2)}) collective-permute-start(bf16[128,1536]{1,0:T(8,128)(2,1)} %get-tuple-element.143), channel_id=1, source_target_pairs={{0,3},{1,0},{2,1},{3,2},{4,7},{5,4},{6,5},{7,6},{8,11},{9,8},{10,9... | collective-permute-start | bytes 1179656 | tf_op jit(solution)/shard_map/ppermute | solution.py:780
  453.7 40.9 %collective-permute-start.36 = (bf16[128,1536]{1,0:T(8,128)(2,1)}, bf16[128,1536]{1,0:T(8,128)(2,1)S(1)}, u32[]{:S(2)}, u32[]{:S(2)}) collective-permute-start(bf16[128,1536]{1,0:T(8,128)(2,1)} %get-tuple-element.116), channel_id=1, source_target_pairs={{0,1},{1,2},{2,3},{3,0},{4,5},{5,6},{6,7},{7,4},{8,9},{9,10},{10,1... | collective-permute-start | bytes 1179656 | tf_op jit(solution)/shard_map/ppermute | solution.py:780
  470.6 30.4 %collective-permute-start.37 = (bf16[128,1536]{1,0:T(8,128)(2,1)}, bf16[128,1536]{1,0:T(8,128)(2,1)S(1)}, u32[]{:S(2)}, u32[]{:S(2)}) collective-permute-start(bf16[128,1536]{1,0:T(8,128)(2,1)} %get-tuple-element.117), channel_id=1, source_target_pairs={{0,2},{1,3},{2,0},{3,1},{4,6},{5,7},{6,4},{7,5},{8,10},{9,11},{10,... | collective-permute-start | bytes 1179656 | tf_op jit(solution)/shard_map/ppermute | solution.py:780
  470.7 34.5 %collective-permute-start.38 = (bf16[128,1536]{1,0:T(8,128)(2,1)}, bf16[128,1536]{1,0:T(8,128)(2,1)S(1)}, u32[]{:S(2)}, u32[]{:S(2)}) collective-permute-start(bf16[128,1536]{1,0:T(8,128)(2,1)} %get-tuple-element.118), channel_id=1, source_target_pairs={{0,3},{1,0},{2,1},{3,2},{4,7},{5,4},{6,5},{7,6},{8,11},{9,8},{10,9... | collective-permute-start | bytes 1179656 | tf_op jit(solution)/shard_map/ppermute | solution.py:780
  (84 other events, 1276.6 us)

commit v2 on v1

--- a/solution.py
+++ b/solution.py
@@ -197,6 +197,36 @@
     gain = gain_ref[0:1] / norm_ref[...]
     for j in range(gain_ref.shape[1] // 128):
         out_ref[at + 16 + j : at + 17 + j] = gain[:, j * 128 : (j + 1) * 128]
+
+
+def pick_kernel(
+    spot_ref, inner_ref, gate_ref, pair_ref, step_ref, out_ref, *refs
+):
+    count = len(refs) // 2
+    i = pl.program_id(0)
+    QW, PW = inner_ref.shape[0], pair_ref.shape[0]
+    HA, PH = QW // 2, PW // 2
+    heads = QW * count // P_SIZE
+    group = spot_ref[1] * count + lax.rem(spot_ref[2] + i, count)
+    step = step_ref[...]
+    down = lax.broadcasted_iota(jnp.int32, step.shape, 0)
+    step = jnp.where(down < H, step, jnp.zeros_like(step))
+    row = lax.broadcasted_iota(jnp.int32, (8, step.shape[0]), 0)
+    col = lax.broadcasted_iota(jnp.int32, (8, step.shape[0]), 1)
+    hot = ((col == row + group * heads) & (row < heads)).astype(f32).astype(bf16)
+    step = mm(hot, step, ((1,), (0,))).astype(bf16)
+    for k in range(count):
+        first, later = refs[k], refs[count + k]
+
+        @pl.when(i == k)
+        def _(first=first, later=later):
+            first[0:HA] = inner_ref[0:HA]
+            first[HA : HA + PH] = pair_ref[0:PH]
+            first[HA + PH : QW + PH] = inner_ref[HA:QW]
+            first[QW + PH : QW + PW] = pair_ref[PH:PW]
+            first[QW + PW : QW + PW + 8] = step
+            later[0:QW] = gate_ref[...]
+            later[QW : 2 * QW] = out_ref[...]
 
 
 def project_kernel(
@@ -832,9 +862,6 @@
     def rows_back(width):
         return pl.BlockSpec((Q, width), lambda i, p: (blocks - 1 - i, 0))
 
-    def rows_half(width):
-        return pl.BlockSpec((Q, width), lambda i, p: (lax.rem(i, half), 0))
-
     def fixed(*shape):
         return pl.BlockSpec(shape, lambda i, p: (0,) * len(shape))
 
@@ -920,10 +947,35 @@
         out_part = lax.dynamic_slice(out_weight, (group * GW + q * QW, 0), (QW, Dl))
         return jnp.concatenate([gate_part, out_part], axis=0)
 
-    def line_rows(pick):
-        return [pick(f)] + [from_line(pick(lax.rem(f + k, F)), k) for k in range(1, F)]
-
-    first_rows = line_rows(rows_for)
+    def line_rows(rows):
+        return [rows[0]] + [from_line(rows[k], k) for k in range(1, F)]
+
+    if QW % 32 == 0 and DI % QW == 0 and 2 * PH >= H:
+
+        def group_rows(width, start):
+            def index(i, p):
+                return (start + (p[1] * F + lax.rem(p[2] + i, F)) * F + p[0], 0)
+
+            return pl.BlockSpec((width, Dl), index)
+
+        picked = call(
+            pick_kernel,
+            F,
+            [
+                group_rows(QW, DI // QW),
+                group_rows(QW, 0),
+                pl.BlockSpec((2 * PH, Dl), lambda i, p: (DI // PH + p[0], 0)),
+                pl.BlockSpec((2 * PH, Dl), lambda i, p: ((2 * DI + NP) // (2 * PH), 0)),
+                group_rows(QW, 0),
+            ],
+            [fixed(QW + 2 * PH + 8, Dl)] * F + [fixed(2 * QW, Dl)] * F,
+            [struct((QW + 2 * PH + 8, Dl), bf16)] * F + [struct((2 * QW, Dl), bf16)] * F,
+        )(spot, columns, columns, columns, columns, out_weight)
+        rows_now, rows_later = picked[:F], picked[F:]
+    else:
+        rows_now = [rows_for(lax.rem(f + k, F)) for k in range(F)]
+        rows_later = [later_rows_for(lax.rem(f + k, F)) for k in range(F)]
+    first_rows = line_rows(rows_now)
     rows_a = jnp.stack([value[: HA + PH] for value in first_rows])
     rows_b = jnp.stack([value[HA + PH :] for value in first_rows])
     if F == 4:
@@ -934,7 +986,7 @@
         pieces_a, pieces_b = gather_parts(rows_a, bits), gather_parts(rows_b, bits)
     pieces_a, pieces_b = in_order(pieces_a), in_order(pieces_b)
 
-    later = line_rows(later_rows_for)
+    later = line_rows(rows_later)
     later = jnp.stack(later)
     cot_rel = [from_line(cotangent, k) for k in range(1, F)]
 
@@ -958,7 +1010,7 @@
     ) = call(
         functools.partial(project_kernel, absolute, QW),
         blocks,
-        [rows_half(D), rows_half(D), fixed(16, D), fixed(16, D)]
+        [half_of(D, 1), half_of(D, 0), fixed(16, D), fixed(16, D)]
         + [fixed(F, HA + PH, Dl), fixed(F, QW - HA + PH + 8, Dl)] * F
         + [fixed(8, GW), fixed(8, NP), fixed(8, 128)],
         [
@@ -996,7 +1048,7 @@
     cot_group, gate_rows, out_rows, gate, back_normed = call(
         functools.partial(cotangent_kernel, absolute),
         blocks,
-        [rows_half(D), rows_half(D), rows_of(D)] + [fixed(F, 2 * QW, Dl)] * F,
+        [half_of(D, 1), half_of(D, 0), rows_of(D)] + [fixed(F, 2 * QW, Dl)] * F,
         [rows_of(D), fixed(GW, D), fixed(GW, D), rows_of(GW), rows_of(GW)],
         [
             struct((TL, D), bf16), struct((GW, D), bf16), struct((GW, D), bf16),
@@ -1192,6 +1244,11 @@
     gain_sum = shared[16:].reshape(-1)[:D]
     channel_grads = mine_small[: KW + 2, : HG * PF].reshape(KW + 2, HG, PF)
     head_grads = mine_small[KW + 2]
+
+    *late_rest, channel_grads, head_grads, pair_grads, gain_sum = lax.optimization_barrier(
+        (*early, channel_grads, head_grads, pair_grads, gain_sum)
+    )
+    early = late_rest
 
     scaled_back = back_in * norm_gain[None, :]
     inverse_cubed = inverse_scale * inverse_scale * inverse_scale

time: 529 us -> 527 us (level)
  waiting for transfers between devices: 179 us -> 223 us
  starting transfers between devices: 150 us -> 114 us
  local copies, waits for them, and re-layouts: 26.6 us -> 19.6 us
    ppermute x24, waiting for transfers between devices: 61.3 us -> 94 us  [from_line(): return lax.ppermute(value, 'fsdp', [(i, (i + k) % F) for i in range(F)])]
    ppermute x24, starting transfers between devices: 81.1 us -> 48.9 us  [from_line(): return lax.ppermute(value, 'fsdp', [(i, (i + k) % F) for i in range(F)])]
    ppermute x2, starting transfers between devices: 13.3 us -> 5.35 us  [body(): lax.ppermute(shared, 'fsdp', [(i, i ^ bit) for i in range(F)])]
    ppermute x2, waiting for transfers between devices: 1.13 us -> 8.08 us  [body(): lax.ppermute(shared, 'fsdp', [(i, i ^ bit) for i in range(F)])]
    ppermute x29, waiting for transfers between devices: 73.1 us -> 79.8 us  [from_part(): return lax.ppermute(value, 'seq', [(i, i ^ k * R) for i in range(S)])]
    pallas_call x2 -> x3, Pallas kernels: 25.2 us -> 28.9 us  [the longest x1 15.3 us: body(): call(functools.partial(project_kernel, absolute, QW), blocks, [half_of(D,...]
  transfers between devices with their start and end apart: 74 -> 74, of which waited for: 29 -> 29; matrix products, arithmetic and copies ran while one was open for 9% -> 7% of each run, Pallas kernels for 20% -> 20%
where the time goes in v2:
time: 527 us; the launch traced here: 524 us
  waiting for transfers between devices  223 us (42%)
  Pallas kernels  142 us (27%)
  starting transfers between devices  114 us (22%)
  other arithmetic  24.3 us (5%)
  local copies, waits for them, and re-layouts  19.6 us (4%)
    ppermute x24, waiting for transfers between devices, from_line(): return lax.ppermute(value, 'fsdp', [(i, (i + k) % F) for i in range(F)])  94 us
    ppermute x29, waiting for transfers between devices, from_part(): return lax.ppermute(value, 'seq', [(i, i ^ k * R) for i in range(S)])  79.8 us
    ppermute x24, starting transfers between devices, from_line(): return lax.ppermute(value, 'fsdp', [(i, (i + k) % F) for i in range(F)])  48.9 us
    ppermute x29, starting transfers between devices, from_part(): return lax.ppermute(value, 'seq', [(i, i ^ k * R) for i in range(S)])  36.5 us
    all_to_all x1, waiting for transfers between devices, spread(): return lax.all_to_all(copies, axis, 0, 0, tiled=True)  19 us
    pallas_call x4, Pallas kernels, by_line(): call(functools.partial(sum_kernel, F), F, [block] * len(arrays), [fixed(r...  18 us
    pallas_call x2, Pallas kernels, partial_sums(): call(functools.partial(partial_blocks_kernel, F, pairs), F, [fixed(TL, GW...  16.7 us
    ppermute x3, waiting for transfers between devices, line_chain(): down = lax.ppermute(down, 'fsdp', [(i, i - 1) for i in range(1, F - k + 1)])  16.2 us
  transfers between devices with their start and end apart: 74, of which 29 were waited for; matrix products, arithmetic and copies ran while one was open for 7% of the time, Pallas kernels for 20%

profile of v2, /device:TPU:0, one launch (start us, length us, event | category | flops | bytes accessed | tf_op | source)
XLA Modules:
  0.0 524.4 jit_solution(6678582737953669312)
XLA Ops:
  4.8 5.6 %collective-permute-start = (bf16[128,1536]{1,0:T(8,128)(2,1)S(1)}, bf16[128,1536]{1,0:T(8,128)(2,1)S(1)}, u32[]{:S(2)}, u32[]{:S(2)}) collective-permute-start(bf16[128,1536]{1,0:T(8,128)(2,1)S(1)} %fusion.2), channel_id=1, source_target_pairs={{0,1},{1,2},{2,3},{4,5},{5,6},{6,7},{8,9},{9,10},{10,11},{12,13},{... | collective-permute-start | bytes 1179656 | tf_op jit(solution)/shard_map/ppermute | solution.py:818
  22.3 17.2 %collective-permute-done.9 = bf16[168,384]{1,0:T(8,128)(2,1)S(1)} collective-permute-done((bf16[168,384]{1,0:T(8,128)(2,1)}, bf16[168,384]{1,0:T(8,128)(2,1)S(1)}, u32[]{:S(2)}, u32[]{:S(2)}) %collective-permute-start.9) | collective-permute-done | bytes 129056 | tf_op jit(solution)/shard_map/ppermute | solution.py:810
  39.5 11.6 %collective-permute-start.10 = (bf16[168,384]{1,0:T(8,128)(2,1)}, bf16[168,384]{1,0:T(8,128)(2,1)S(1)}, u32[]{:S(2)}, u32[]{:S(2)}) collective-permute-start(bf16[168,384]{1,0:T(8,128)(2,1)} %get-tuple-element.111), channel_id=1, source_target_pairs={{0,2},{1,3},{2,0},{3,1},{4,6},{5,7},{6,4},{7,5},{8,10},{9,11},{10,... | collective-permute-start | bytes 387080 | tf_op jit(solution)/shard_map/ppermute | solution.py:810
  51.0 5.1 collective-permute-done.10
  63.4 6.9 %collective-permute-start.22 = (bf16[192,384]{1,0:T(8,128)(2,1)}, bf16[192,384]{1,0:T(8,128)(2,1)S(1)}, u32[]{:S(2)}, u32[]{:S(2)}) collective-permute-start(bf16[192,384]{1,0:T(8,128)(2,1)} %get-tuple-element.128), channel_id=1, source_target_pairs={{0,1},{1,2},{2,3},{3,0},{4,5},{5,6},{6,7},{7,4},{8,9},{9,10},{10,1... | collective-permute-start | bytes 442376 | tf_op jit(solution)/shard_map/ppermute | solution.py:810
  84.6 11.9 %collective-permute-done.5 = bf16[128,1536]{1,0:T(8,128)(2,1)S(1)} collective-permute-done((bf16[128,1536]{1,0:T(8,128)(2,1)S(1)}, bf16[128,1536]{1,0:T(8,128)(2,1)S(1)}, u32[]{:S(2)}, u32[]{:S(2)}) %collective-permute-start.5) | collective-permute-done | bytes 393248 | tf_op jit(solution)/shard_map/ppermute | solution.py:819
  129.7 6.2 %all-to-all-start = ((f32[32,8,128]{2,1,0:T(8,128)}), f32[32,8,128]{2,1,0:T(8,128)}, u32[]{:S(2)}, u32[]{:S(2)}) async-start(f32[32,8,128]{2,1,0:T(8,128)} %broadcast_in_dim.27), calls=%async_computation | async-start | bytes 262144 | tf_op jit(solution)/shard_map/all_to_all | solution.py:27
  137.4 19.0 %all-to-all-done = f32[32,8,128]{2,1,0:T(8,128)} async-done(((f32[32,8,128]{2,1,0:T(8,128)}), f32[32,8,128]{2,1,0:T(8,128)}, u32[]{:S(2)}, u32[]{:S(2)}) %all-to-all-start) | async-done | bytes 131104 | tf_op jit(solution)/shard_map/all_to_all | solution.py:27
  160.1 15.3 %shard_map.230 = (bf16[1024,1536]{1,0:T(8,128)(2,1)}, bf16[392,1536]{1,0:T(8,128)(2,1)}, bf16[256,1536]{1,0:T(8,128)(2,1)}, bf16[1024,384]{1,0:T(8,128)(2,1)}, b...) custom-call(s32[3]{0:T(128)} %pad_add_fusion.spot_ref, ...), custom_call_target="tpu_custom_call" | custom-call | tf_op jit(solution)/shard_map/pallas_call | solution.py:1010
  179.0 6.0 %shard_map.231.y_ref = f32[1024,384]{1,0:T(8,128)} custom-call(s32[3]{0:T(128)} %pad_add_fusion.spot_ref, bf16[1024,384]{1,0:T(8,128)(2,1)} %get-tuple-element.116.actx_ref, bf16[1024,256]{1,0:T(8,128)(2,1)} %get-tuple-element.117.actp_ref, f32[1024,8]{1,0:T(8,128)} %get-tuple-element.120.dt_ref, f32[1024,8]{1,0:T(8,128)} %get-tuple-element.118.cum_ref, ...), custom_call_target="tpu_custom_call" | custom-call | tf_op jit(solution)/shard_map/pallas_call | solution.py:1041
  185.1 9.3 %shard_map.232 = (bf16[1024,1536]{1,0:T(8,128)(2,1)}, bf16[384,1536]{1,0:T(8,128)(2,1)}, bf16[384,1536]{1,0:T(8,128)(2,1)}, bf16[1024,384]{1,0:T(8,128)(2,1)}, bf16[1024,384]{1,0:T(8,128)(2,1)}) custom-call(s32[3]{0:T(128)} %pad_add_fusion.spot_ref, bf16[512,1536]{1,0:T(8,128)(2,1)} %copy-done.2, bf16[512,1536]{1,0:T(8,128)(2,1)} %collective-permute-done.21.other_ref, ...), custom_call_target="tpu_custom_call" | custom-call | tf_op jit(solution)/shard_map/pallas_call | solution.py:1048
  195.2 6.9 %shard_map.233 = (f32[1024,384]{1,0:T(8,128)}, bf16[4,128,384]{2,1,0:T(8,128)(2,1)}, f32[8,1024]{1,0:T(8,128)}) custom-call(s32[3]{0:T(128)} %pad_add_fusion.spot_ref, bf16[1024,384]{1,0:T(8,128)(2,1)} %get-tuple-element.116.actx_ref, bf16[1024,256]{1,0:T(8,128)(2,1)} %get-tuple-element.117.actp_ref, f32[1024,8]{1,0:T(8,128)} %get-tuple-element.118.cum_ref, ...), custom_call_target="tpu_custom_call" | custom-call | tf_op jit(solution)/shard_map/pallas_call | solution.py:1058
  212.4 12.3 %shard_map.234 = (bf16[1024,384]{1,0:T(8,128)(2,1)}, bf16[1024,384]{1,0:T(8,128)(2,1)}, bf16[1024,384]{1,0:T(8,128)(2,1)}, f32[4,128,384]{2,1,0:T(8,128)}, f32[1...) custom-call(s32[3]{0:T(128)} %pad_add_fusion.spot_ref, ...), custom_call_target="tpu_custom_call" | custom-call | tf_op jit(solution)/shard_map/pallas_call | solution.py:1073
  224.7 8.7 %shard_map.240 = (bf16[4,192,384]{2,1,0:T(8,128)(2,1)}, bf16[4,192,384]{2,1,0:T(8,128)(2,1)}, bf16[4,192,384]{2,1,0:T(8,128)(2,1)}, bf16[4,192,384]{2,1,0:T(8,128)(2,1)}) custom-call(s32[3]{0:T(128)} %pad_add_fusion.spot_ref, bf16[1024,384]{1,0:T(8,128)(2,1)} %get-tuple-element.169.refs_0_, bf16[1024,384]{1,0:T(8,128)(2,1)} %get-tuple-element.158.bgate_ref.refs_1_, ...), custom_call_target="tpu_custom_call" | custom-call | tf_op jit(solution)/shard_map/pallas_call | solution.py:1120
  239.4 26.4 %collective-permute-done.41.refs_5_ = f32[128,384]{1,0:T(8,128)S(1)} collective-permute-done((f32[128,384]{1,0:T(8,128)S(1)}, f32[128,384]{1,0:T(8,128)S(1)}, u32[]{:S(2)}, u32[]{:S(2)}) %collective-permute-start.41) | collective-permute-done | bytes 196640 | tf_op jit(solution)/shard_map/ppermute | solution.py:807
  268.2 8.6 %shard_map.236 = (f32[1024,384]{1,0:T(8,128)}, f32[1024,256]{1,0:T(8,128)}) custom-call(s32[3]{0:T(128)} %pad_add_fusion.spot_ref, bf16[1024,384]{1,0:T(8,128)(2,1)} %get-tuple-element.116.actx_ref, bf16[1024,256]{1,0:T(8,128)(2,1)} %get-tuple-element.117.actp_ref, f32[1024,8]{1,0:T(8,128)} %get-tuple-element.120.dt_ref, ...), custom_call_target="tpu_custom_call" | custom-call | tf_op jit(solution)/shard_map/pallas_call | solution.py:1154
  277.6 11.1 %shard_map.237 = (f32[1024,384]{1,0:T(8,128)}, f32[1024,256]{1,0:T(8,128)}, f32[1024,8]{1,0:T(8,128)}, f32[8,8]{1,0:T(8,128)}, f32[8,640]{1,0:T(8,128)}) custom-call(s32[3]{0:T(128)} %pad_add_fusion.spot_ref, bf16[1024,384]{1,0:T(8,128)(2,1)} %get-tuple-element.116.actx_ref, bf16[1024,256]{1,0:T(8,128)(2,1)} %get-tuple-element.117.actp_ref, ...), custom_call_target="tpu_custom_call" | custom-call | tf_op jit(solution)/shard_map/pallas_call | solution.py:1165
  295.2 13.4 %shard_map.238 = (bf16[1024,384]{1,0:T(8,128)(2,1)}, bf16[1024,256]{1,0:T(8,128)(2,1)}, f32[8,384]{1,0:T(8,128)}, f32[8,256]{1,0:T(8,128)}, bf16[512,1536]{1,0:T...) custom-call(s32[3]{0:T(128)} %pad_add_fusion.spot_ref, f32[1024,384]{1,0:T(8,128)} %get-tuple-element.153.dprex_ref.nextx_ref, ...), custom_call_target="tpu_custom_call" | custom-call | tf_op jit(solution)/shard_map/pallas_call | solution.py:1195
  308.6 8.0 %shard_map.243 = (bf16[4,168,384]{2,1,0:T(8,128)(2,1)}, bf16[4,168,384]{2,1,0:T(8,128)(2,1)}, bf16[4,168,384]{2,1,0:T(8,128)(2,1)}, bf16[4,168,384]{2,1,0:T(8,128)(2,1)}) custom-call(s32[3]{0:T(128)} %pad_add_fusion.spot_ref, bf16[1024,384]{1,0:T(8,128)(2,1)} %get-tuple-element.185.refs_0_, bf16[1024,1536]{1,0:T(8,128)(2,1)} %get-tuple-element.126.x_ref.refs_3_.refs_1_, ...), custom_call_target="tpu_custom_call" | custom-call | tf_op jit(solution)/shard_map/pallas_call | solution.py:1120
  330.4 8.7 %collective-permute-done.57 = f32[64,128]{1,0:T(8,128)S(1)} collective-permute-done((f32[64,128]{1,0:T(8,128)}, f32[64,128]{1,0:T(8,128)S(1)}, u32[]{:S(2)}, u32[]{:S(2)}) %collective-permute-start.57) | collective-permute-done | bytes 32800 | tf_op jit(solution)/shard_map/ppermute | solution.py:807
  349.7 8.8 %collective-permute-done.58 = f32[64,128]{1,0:T(8,128)S(1)} collective-permute-done((f32[64,128]{1,0:T(8,128)S(1)}, f32[64,128]{1,0:T(8,128)S(1)}, u32[]{:S(2)}, u32[]{:S(2)}) %collective-permute-start.58) | collective-permute-done | bytes 32800 | tf_op jit(solution)/shard_map/ppermute | solution.py:807
  369.4 8.1 %collective-permute-done.61 = f32[32,128]{1,0:T(8,128)S(1)} collective-permute-done((f32[32,128]{1,0:T(8,128)S(1)}, f32[32,128]{1,0:T(8,128)S(1)}, u32[]{:S(2)}, u32[]{:S(2)}) %collective-permute-start.61) | collective-permute-done | bytes 16416 | tf_op jit(solution)/shard_map/ppermute | solution.py:1235
  383.5 9.8 %collective-permute-done.54.refs_2_ = bf16[4,192,384]{2,1,0:T(8,128)(2,1)S(1)} collective-permute-done((bf16[4,192,384]{2,1,0:T(8,128)(2,1)S(1)}, bf16[4,192,384]{2,1,0:T(8,128)(2,1)S(1)}, u32[]{:S(2)}, u32[]{:S(2)}) %collective-permute-start.54) | collective-permute-done | bytes 589856 | tf_op jit(solution)/shard_map/ppermute | solution.py:807
  398.7 8.0 %collective-permute-done.71.refs_3_ = bf16[4,168,384]{2,1,0:T(8,128)(2,1)S(1)} collective-permute-done((bf16[4,168,384]{2,1,0:T(8,128)(2,1)}, bf16[4,168,384]{2,1,0:T(8,128)(2,1)S(1)}, u32[]{:S(2)}, u32[]{:S(2)}) %collective-permute-start.71) | collective-permute-done | bytes 516128 | tf_op jit(solution)/shard_map/ppermute | solution.py:807
  406.8 9.7 %collective-permute-done.70.refs_2_ = bf16[4,168,384]{2,1,0:T(8,128)(2,1)} collective-permute-done((bf16[4,168,384]{2,1,0:T(8,128)(2,1)}, bf16[4,168,384]{2,1,0:T(8,128)(2,1)}, u32[]{:S(2)}, u32[]{:S(2)}) %collective-permute-start.70) | collective-permute-done | bytes 516128 | tf_op jit(solution)/shard_map/ppermute | solution.py:807
  417.2 5.3 %collective-permute-start.62 = (f32[32,128]{1,0:T(8,128)S(1)}, f32[32,128]{1,0:T(8,128)S(1)}, u32[]{:S(2)}, u32[]{:S(2)}) collective-permute-start(f32[32,128]{1,0:T(8,128)S(1)} %add.123), channel_id=1, source_target_pairs={{0,2},{1,3},{2,0},{3,1},{4,6},{5,7},{6,4},{7,5},{8,10},{9,11},{10,... | collective-permute-start | bytes 49160 | tf_op jit(solution)/shard_map/ppermute | solution.py:1235
  445.1 16.8 %collective-permute-done.45 = bf16[128,1536]{1,0:T(8,128)(2,1)} collective-permute-done((bf16[128,1536]{1,0:T(8,128)(2,1)}, bf16[128,1536]{1,0:T(8,128)(2,1)}, u32[]{:S(2)}, u32[]{:S(2)}) %collective-permute-start.45) | collective-permute-done | bytes 393248 | tf_op jit(solution)/shard_map/ppermute | solution.py:810
  461.9 9.4 %collective-permute-start.38 = (bf16[128,1536]{1,0:T(8,128)(2,1)}, bf16[128,1536]{1,0:T(8,128)(2,1)S(1)}, u32[]{:S(2)}, u32[]{:S(2)}) collective-permute-start(bf16[128,1536]{1,0:T(8,128)(2,1)} %get-tuple-element.143), channel_id=1, source_target_pairs={{0,3},{1,0},{2,1},{3,2},{4,7},{5,4},{6,5},{7,6},{8,11},{9,8},{10,9... | collective-permute-start | bytes 1179656 | tf_op jit(solution)/shard_map/ppermute | solution.py:810
  473.1 21.7 %collective-permute-done.37 = bf16[128,1536]{1,0:T(8,128)(2,1)S(1)} collective-permute-done((bf16[128,1536]{1,0:T(8,128)(2,1)}, bf16[128,1536]{1,0:T(8,128)(2,1)S(1)}, u32[]{:S(2)}, u32[]{:S(2)}) %collective-permute-start.37) | collective-permute-done | bytes 393248 | tf_op jit(solution)/shard_map/ppermute | solution.py:810
  494.7 8.3 %collective-permute-done.38 = bf16[128,1536]{1,0:T(8,128)(2,1)S(1)} collective-permute-done((bf16[128,1536]{1,0:T(8,128)(2,1)}, bf16[128,1536]{1,0:T(8,128)(2,1)S(1)}, u32[]{:S(2)}, u32[]{:S(2)}) %collective-permute-start.38) | collective-permute-done | bytes 393248 | tf_op jit(solution)/shard_map/ppermute | solution.py:810
  507.8 7.9 %shard_map.245 = (f32[6448,384]{1,0:T(8,128)}, f32[3072,384]{1,0:T(8,128)}) custom-call(s32[3]{0:T(128)} %pad_add_fusion.spot_ref, bf16[4,192,384]{2,1,0:T(8,128)(2,1)} %copy-done.6, bf16[4,192,384]{2,1,0:T(8,128)(2,1)} %copy-done.5, bf16[4,192,384]{2,1,0:T(8,128)(2,1)} %copy-done.4, bf16[4,192,384]{2,1,0:T(8,128)(2,1)} %copy-done.3, ...), custom_call_target="tpu_custom_call" | custom-call | tf_op jit(solution)/shard_map/pallas_call | solution.py:1262
  517.0 7.4 %shard_map.246 = f32[6448,384]{1,0:T(8,128)} custom-call(s32[3]{0:T(128)} %pad_add_fusion.spot_ref, bf16[4,168,384]{2,1,0:T(8,128)(2,1)} %get-tuple-element.242.refs_0_, bf16[4,168,384]{2,1,0:T(8,128)(2,1)} %collective-permute-done.69.refs_1_, bf16[4,168,384]{2,1,0:T(8,128)(2,1)} %collective-permute-done.70.refs_2_, ...), custom_call_target="tpu_custom_call", output_to_operand_aliasing={{}: (6, {})} | custom-call | tf_op jit(solution)/shard_map/pallas_call | solution.py:1269
  (280 shorter events, 183.3 us)
Async XLA Ops:
  3.5 57.9 %collective-permute-start.3 = (bf16[128,1536]{1,0:T(8,128)(2,1)S(1)}, bf16[128,1536]{1,0:T(8,128)(2,1)S(1)}, u32[]{:S(2)}, u32[]{:S(2)}) collective-permute-start(bf16[128,1536]{1,0:T(8,128)(2,1)S(1)} %fusion.2), channel_id=1, source_target_pairs={{1,0},{2,1},{3,2},{5,4},{6,5},{7,6},{9,8},{10,9},{11,10},{13,12},{... | collective-permute-start | bytes 1179656 | tf_op jit(solution)/shard_map/ppermute | solution.py:819
  4.8 57.9 %collective-permute-start = (bf16[128,1536]{1,0:T(8,128)(2,1)S(1)}, bf16[128,1536]{1,0:T(8,128)(2,1)S(1)}, u32[]{:S(2)}, u32[]{:S(2)}) collective-permute-start(bf16[128,1536]{1,0:T(8,128)(2,1)S(1)} %fusion.2), channel_id=1, source_target_pairs={{0,1},{1,2},{2,3},{4,5},{5,6},{6,7},{8,9},{9,10},{10,11},{12,13},{... | collective-permute-start | bytes 1179656 | tf_op jit(solution)/shard_map/ppermute | solution.py:818
  10.4 53.0 %collective-permute-start.20 = (bf16[128,1536]{1,0:T(8,128)(2,1)}, bf16[128,1536]{1,0:T(8,128)(2,1)S(1)}, u32[]{:S(2)}, u32[]{:S(2)}) collective-permute-start(bf16[128,1536]{1,0:T(8,128)(2,1)} %param.25), channel_id=1, source_target_pairs={{0,3},{1,0},{2,1},{3,2},{4,7},{5,4},{6,5},{7,6},{8,11},{9,8},{10,9... | collective-permute-start | bytes 1179656 | tf_op jit(solution)/shard_map/ppermute | solution.py:810
  12.3 58.0 %collective-permute-start.19 = (bf16[128,1536]{1,0:T(8,128)(2,1)}, bf16[128,1536]{1,0:T(8,128)(2,1)S(1)}, u32[]{:S(2)}, u32[]{:S(2)}) collective-permute-start(bf16[128,1536]{1,0:T(8,128)(2,1)} %param.25), channel_id=1, source_target_pairs={{0,2},{1,3},{2,0},{3,1},{4,6},{5,7},{6,4},{7,5},{8,10},{9,11},{10,... | collective-permute-start | bytes 1179656 | tf_op jit(solution)/shard_map/ppermute | solution.py:810
  63.4 34.4 %collective-permute-start.22 = (bf16[192,384]{1,0:T(8,128)(2,1)}, bf16[192,384]{1,0:T(8,128)(2,1)S(1)}, u32[]{:S(2)}, u32[]{:S(2)}) collective-permute-start(bf16[192,384]{1,0:T(8,128)(2,1)} %get-tuple-element.128), channel_id=1, source_target_pairs={{0,1},{1,2},{2,3},{3,0},{4,5},{5,6},{6,7},{7,4},{8,9},{9,10},{10,1... | collective-permute-start | bytes 442376 | tf_op jit(solution)/shard_map/ppermute | solution.py:810
  70.3 29.8 %collective-permute-start.23 = (bf16[192,384]{1,0:T(8,128)(2,1)}, bf16[192,384]{1,0:T(8,128)(2,1)S(1)}, u32[]{:S(2)}, u32[]{:S(2)}) collective-permute-start(bf16[192,384]{1,0:T(8,128)(2,1)} %get-tuple-element.129), channel_id=1, source_target_pairs={{0,2},{1,3},{2,0},{3,1},{4,6},{5,7},{6,4},{7,5},{8,10},{9,11},{10,... | collective-permute-start | bytes 442376 | tf_op jit(solution)/shard_map/ppermute | solution.py:810
  75.1 25.6 %collective-permute-start.24 = (bf16[192,384]{1,0:T(8,128)(2,1)}, bf16[192,384]{1,0:T(8,128)(2,1)S(1)}, u32[]{:S(2)}, u32[]{:S(2)}) collective-permute-start(bf16[192,384]{1,0:T(8,128)(2,1)} %get-tuple-element.130), channel_id=1, source_target_pairs={{0,3},{1,0},{2,1},{3,2},{4,7},{5,4},{6,5},{7,6},{8,11},{9,8},{10,9... | collective-permute-start | bytes 442376 | tf_op jit(solution)/shard_map/ppermute | solution.py:810
  96.9 63.2 %collective-permute-start.6 = (bf16[512,1536]{1,0:T(8,128)(2,1)S(1)}, bf16[512,1536]{1,0:T(8,128)(2,1)}, u32[]{:S(2)}, u32[]{:S(2)}) collective-permute-start(bf16[512,1536]{1,0:T(8,128)(2,1)S(1)} %pad_maximum_fusion.2.mine_ref), channel_id=1, source_target_pairs={{0,4},{4,0},{8,12},{12,8},{16,20},{20,16},{24,28},{28,24},{1,5},{5... | collective-permute-start | bytes 4718600 | tf_op jit(solution)/shard_map/ppermute | solution.py:804
  97.6 87.5 %collective-permute-start.21 = (bf16[512,1536]{1,0:T(8,128)(2,1)S(1)}, bf16[512,1536]{1,0:T(8,128)(2,1)}, u32[]{:S(2)}, u32[]{:S(2)}) collective-permute-start(bf16[512,1536]{1,0:T(8,128)(2,1)S(1)} %pad_maximum_fusion.3.mine_ref), channel_id=1, source_target_pairs={{0,4},{4,0},{8,12},{12,8},{16,20},{20,16},{24,28},{28,24},{1,5},{5... | collective-permute-start | bytes 4718600 | tf_op jit(solution)/shard_map/ppermute | solution.py:804
  124.8 52.7 %collective-permute-start.27 = (bf16[4,192,384]{2,1,0:T(8,128)(2,1)}, bf16[4,192,384]{2,1,0:T(8,128)(2,1)}, u32[]{:S(2)}, u32[]{:S(2)}) collective-permute-start(bf16[4,192,384]{2,1,0:T(8,128)(2,1)} %pad_maximum_fusion.4.refs_0_), channel_id=1, source_target_pairs={{0,24},{4,28},{8,16},{12,20},{16,8},{20,12},{24,0},{28,4},{1,25},{... | collective-permute-start | bytes 1769480 | tf_op jit(solution)/shard_map/ppermute | solution.py:807
  126.3 51.7 %collective-permute-start.26 = (bf16[4,192,384]{2,1,0:T(8,128)(2,1)}, bf16[4,192,384]{2,1,0:T(8,128)(2,1)}, u32[]{:S(2)}, u32[]{:S(2)}) collective-permute-start(bf16[4,192,384]{2,1,0:T(8,128)(2,1)} %pad_maximum_fusion.4.refs_0_), channel_id=1, source_target_pairs={{0,16},{4,20},{8,24},{12,28},{16,0},{20,4},{24,8},{28,12},{1,17},{... | collective-permute-start | bytes 1769480 | tf_op jit(solution)/shard_map/ppermute | solution.py:807
  128.1 56.9 %collective-permute-start.25 = (bf16[4,192,384]{2,1,0:T(8,128)(2,1)}, bf16[4,192,384]{2,1,0:T(8,128)(2,1)}, u32[]{:S(2)}, u32[]{:S(2)}) collective-permute-start(bf16[4,192,384]{2,1,0:T(8,128)(2,1)} %pad_maximum_fusion.4.refs_0_), channel_id=1, source_target_pairs={{0,8},{4,12},{8,0},{12,4},{16,24},{20,28},{24,16},{28,20},{1,9},{5... | collective-permute-start | bytes 1769480 | tf_op jit(solution)/shard_map/ppermute | solution.py:807
  129.7 26.7 %all-to-all-start = ((f32[32,8,128]{2,1,0:T(8,128)}), f32[32,8,128]{2,1,0:T(8,128)}, u32[]{:S(2)}, u32[]{:S(2)}) async-start(f32[32,8,128]{2,1,0:T(8,128)} %broadcast_in_dim.27), calls=%async_computation | async-start | bytes 262144 | tf_op jit(solution)/shard_map/all_to_all | solution.py:27
  233.5 85.0 %collective-permute-start.47 = (bf16[4,192,384]{2,1,0:T(8,128)(2,1)}, bf16[4,192,384]{2,1,0:T(8,128)(2,1)S(1)}, u32[]{:S(2)}, u32[]{:S(2)}) collective-permute-start(bf16[4,192,384]{2,1,0:T(8,128)(2,1)} %get-tuple-element.172), channel_id=1, source_target_pairs={{0,8},{4,12},{8,0},{12,4},{16,24},{20,28},{24,16},{28,20},{1,9},{5... | collective-permute-start | bytes 1769480 | tf_op jit(solution)/shard_map/ppermute | solution.py:807
  234.4 85.7 %collective-permute-start.48 = (bf16[4,192,384]{2,1,0:T(8,128)(2,1)}, bf16[4,192,384]{2,1,0:T(8,128)(2,1)S(1)}, u32[]{:S(2)}, u32[]{:S(2)}) collective-permute-start(bf16[4,192,384]{2,1,0:T(8,128)(2,1)} %get-tuple-element.173), channel_id=1, source_target_pairs={{0,16},{4,20},{8,24},{12,28},{16,0},{20,4},{24,8},{28,12},{1,17},{... | collective-permute-start | bytes 1769480 | tf_op jit(solution)/shard_map/ppermute | solution.py:807
  235.9 84.2 %collective-permute-start.49 = (bf16[4,192,384]{2,1,0:T(8,128)(2,1)}, bf16[4,192,384]{2,1,0:T(8,128)(2,1)S(1)}, u32[]{:S(2)}, u32[]{:S(2)}) collective-permute-start(bf16[4,192,384]{2,1,0:T(8,128)(2,1)} %get-tuple-element.174), channel_id=1, source_target_pairs={{0,24},{4,28},{8,16},{12,20},{16,8},{20,12},{24,0},{28,4},{1,25},{... | collective-permute-start | bytes 1769480 | tf_op jit(solution)/shard_map/ppermute | solution.py:807
  237.0 28.8 %collective-permute-start.41 = (f32[128,384]{1,0:T(8,128)S(1)}, f32[128,384]{1,0:T(8,128)S(1)}, u32[]{:S(2)}, u32[]{:S(2)}) collective-permute-start(f32[128,384]{1,0:T(8,128)S(1)} %copy-done.41), channel_id=1, source_target_pairs={{0,24},{4,28},{8,16},{12,20},{16,8},{20,12},{24,0},{28,4},{1,25},{... | collective-permute-start | bytes 589832 | tf_op jit(solution)/shard_map/ppermute | solution.py:807
  238.9 38.0 %collective-permute-start.40 = (f32[128,384]{1,0:T(8,128)S(1)}, f32[128,384]{1,0:T(8,128)S(1)}, u32[]{:S(2)}, u32[]{:S(2)}) collective-permute-start(f32[128,384]{1,0:T(8,128)S(1)} %copy-done.41), channel_id=1, source_target_pairs={{0,16},{4,20},{8,24},{12,28},{16,0},{20,4},{24,8},{28,12},{1,17},{... | collective-permute-start | bytes 589832 | tf_op jit(solution)/shard_map/ppermute | solution.py:807
  316.6 42.0 %collective-permute-start.63 = (bf16[4,168,384]{2,1,0:T(8,128)(2,1)}, bf16[4,168,384]{2,1,0:T(8,128)(2,1)S(1)}, u32[]{:S(2)}, u32[]{:S(2)}) collective-permute-start(bf16[4,168,384]{2,1,0:T(8,128)(2,1)} %get-tuple-element.188), channel_id=1, source_target_pairs={{0,8},{4,12},{8,0},{12,4},{16,24},{20,28},{24,16},{28,20},{1,9},{5... | collective-permute-start | bytes 1548296 | tf_op jit(solution)/shard_map/ppermute | solution.py:807
  318.4 40.2 %collective-permute-start.64 = (bf16[4,168,384]{2,1,0:T(8,128)(2,1)}, bf16[4,168,384]{2,1,0:T(8,128)(2,1)S(1)}, u32[]{:S(2)}, u32[]{:S(2)}) collective-permute-start(bf16[4,168,384]{2,1,0:T(8,128)(2,1)} %get-tuple-element.189), channel_id=1, source_target_pairs={{0,16},{4,20},{8,24},{12,28},{16,0},{20,4},{24,8},{28,12},{1,17},{... | collective-permute-start | bytes 1548296 | tf_op jit(solution)/shard_map/ppermute | solution.py:807
  318.5 40.2 %collective-permute-start.65 = (bf16[4,168,384]{2,1,0:T(8,128)(2,1)}, bf16[4,168,384]{2,1,0:T(8,128)(2,1)}, u32[]{:S(2)}, u32[]{:S(2)}) collective-permute-start(bf16[4,168,384]{2,1,0:T(8,128)(2,1)} %get-tuple-element.190), channel_id=1, source_target_pairs={{0,24},{4,28},{8,16},{12,20},{16,8},{20,12},{24,0},{28,4},{1,25},{... | collective-permute-start | bytes 1548296 | tf_op jit(solution)/shard_map/ppermute | solution.py:807
  347.5 35.2 %collective-permute-start.55 = (bf16[4,192,384]{2,1,0:T(8,128)(2,1)S(1)}, bf16[4,192,384]{2,1,0:T(8,128)(2,1)S(1)}, u32[]{:S(2)}, u32[]{:S(2)}) collective-permute-start(bf16[4,192,384]{2,1,0:T(8,128)(2,1)S(1)} %get-tuple-element.195.refs_0_), channel_id=1, source_target_pairs={{0,24},{4,28},{8,16},{12,20},{16,8},{20,12},{24,0},{28,4},{1,25},{... | collective-permute-start | bytes 1769480 | tf_op jit(solution)/shard_map/ppermute | solution.py:807
  377.5 48.6 %collective-permute-start.43 = (bf16[512,1536]{1,0:T(8,128)(2,1)}, bf16[512,1536]{1,0:T(8,128)(2,1)}, u32[]{:S(2)}, u32[]{:S(2)}) collective-permute-start(bf16[512,1536]{1,0:T(8,128)(2,1)} %get-tuple-element.164), channel_id=1, source_target_pairs={{0,4},{4,0},{8,12},{12,8},{16,20},{20,16},{24,28},{28,24},{1,5},{5... | collective-permute-start | bytes 4718600 | tf_op jit(solution)/shard_map/ppermute | solution.py:804
  377.5 57.1 %collective-permute-start.35 = (bf16[512,1536]{1,0:T(8,128)(2,1)}, bf16[512,1536]{1,0:T(8,128)(2,1)}, u32[]{:S(2)}, u32[]{:S(2)}) collective-permute-start(bf16[512,1536]{1,0:T(8,128)(2,1)} %get-tuple-element.139), channel_id=1, source_target_pairs={{0,4},{4,0},{8,12},{12,8},{16,20},{20,16},{24,28},{28,24},{1,5},{5... | collective-permute-start | bytes 4718600 | tf_op jit(solution)/shard_map/ppermute | solution.py:804
  382.7 24.0 %collective-permute-start.71 = (bf16[4,168,384]{2,1,0:T(8,128)(2,1)}, bf16[4,168,384]{2,1,0:T(8,128)(2,1)S(1)}, u32[]{:S(2)}, u32[]{:S(2)}) collective-permute-start(bf16[4,168,384]{2,1,0:T(8,128)(2,1)} %get-tuple-element.242.refs_0_), channel_id=1, source_target_pairs={{0,24},{4,28},{8,16},{12,20},{16,8},{20,12},{24,0},{28,4},{1,25},{... | collective-permute-start | bytes 1548296 | tf_op jit(solution)/shard_map/ppermute | solution.py:807
  406.7 99.1 %collective-permute-start.56 = (bf16[4,4,192,384]{3,2,1,0:T(8,128)(2,1)}, bf16[4,4,192,384]{3,2,1,0:T(8,128)(2,1)S(1)}, u32[]{:S(2)}, u32[]{:S(2)}) collective-permute-start(bf16[4,4,192,384]{3,2,1,0:T(8,128)(2,1)} %pad_maximum_fusion), channel_id=1, source_target_pairs={{0,4},{4,0},{8,12},{12,8},{16,20},{20,16},{24,28},{28,24},{1,5},{5... | collective-permute-start | bytes 7077896 | tf_op jit(solution)/shard_map/ppermute | solution.py:804
  425.6 91.4 %collective-permute-start.72 = (bf16[4,4,168,384]{3,2,1,0:T(8,128)(2,1)}, bf16[4,4,168,384]{3,2,1,0:T(8,128)(2,1)}, u32[]{:S(2)}, u32[]{:S(2)}) collective-permute-start(bf16[4,4,168,384]{3,2,1,0:T(8,128)(2,1)} %pad_maximum_fusion.1), channel_id=1, source_target_pairs={{0,4},{4,0},{8,12},{12,8},{16,20},{20,16},{24,28},{28,24},{1,5},{5... | collective-permute-start | bytes 6193160 | tf_op jit(solution)/shard_map/ppermute | solution.py:804
  431.8 30.1 %collective-permute-start.45 = (bf16[128,1536]{1,0:T(8,128)(2,1)}, bf16[128,1536]{1,0:T(8,128)(2,1)}, u32[]{:S(2)}, u32[]{:S(2)}) collective-permute-start(bf16[128,1536]{1,0:T(8,128)(2,1)} %get-tuple-element.167), channel_id=1, source_target_pairs={{0,2},{1,3},{2,0},{3,1},{4,6},{5,7},{6,4},{7,5},{8,10},{9,11},{10,... | collective-permute-start | bytes 1179656 | tf_op jit(solution)/shard_map/ppermute | solution.py:810
  434.6 27.3 %collective-permute-start.46 = (bf16[128,1536]{1,0:T(8,128)(2,1)}, bf16[128,1536]{1,0:T(8,128)(2,1)}, u32[]{:S(2)}, u32[]{:S(2)}) collective-permute-start(bf16[128,1536]{1,0:T(8,128)(2,1)} %get-tuple-element.168), channel_id=1, source_target_pairs={{0,3},{1,0},{2,1},{3,2},{4,7},{5,4},{6,5},{7,6},{8,11},{9,8},{10,9... | collective-permute-start | bytes 1179656 | tf_op jit(solution)/shard_map/ppermute | solution.py:810
  445.1 28.0 %collective-permute-start.36 = (bf16[128,1536]{1,0:T(8,128)(2,1)}, bf16[128,1536]{1,0:T(8,128)(2,1)S(1)}, u32[]{:S(2)}, u32[]{:S(2)}) collective-permute-start(bf16[128,1536]{1,0:T(8,128)(2,1)} %get-tuple-element.141), channel_id=1, source_target_pairs={{0,1},{1,2},{2,3},{3,0},{4,5},{5,6},{6,7},{7,4},{8,9},{9,10},{10,1... | collective-permute-start | bytes 1179656 | tf_op jit(solution)/shard_map/ppermute | solution.py:810
  461.9 32.8 %collective-permute-start.37 = (bf16[128,1536]{1,0:T(8,128)(2,1)}, bf16[128,1536]{1,0:T(8,128)(2,1)S(1)}, u32[]{:S(2)}, u32[]{:S(2)}) collective-permute-start(bf16[128,1536]{1,0:T(8,128)(2,1)} %get-tuple-element.142), channel_id=1, source_target_pairs={{0,2},{1,3},{2,0},{3,1},{4,6},{5,7},{6,4},{7,5},{8,10},{9,11},{10,... | collective-permute-start | bytes 1179656 | tf_op jit(solution)/shard_map/ppermute | solution.py:810
  461.9 41.1 %collective-permute-start.38 = (bf16[128,1536]{1,0:T(8,128)(2,1)}, bf16[128,1536]{1,0:T(8,128)(2,1)S(1)}, u32[]{:S(2)}, u32[]{:S(2)}) collective-permute-start(bf16[128,1536]{1,0:T(8,128)(2,1)} %get-tuple-element.143), channel_id=1, source_target_pairs={{0,3},{1,0},{2,1},{3,2},{4,7},{5,4},{6,5},{7,6},{8,11},{9,8},{10,9... | collective-permute-start | bytes 1179656 | tf_op jit(solution)/shard_map/ppermute | solution.py:810
  (84 other events, 1344.0 us)

commit v3 on v2

--- a/solution.py
+++ b/solution.py
@@ -383,7 +383,7 @@
     prefix[...] = prefix[...] + total_ref[0]
     states_ref[0] = low
     yx = mm(actp_ref[:, N : 2 * N], low, ((1,), (0,))) * widen(jnp.exp(cum_ref[...]), GW)
-    yx_ref[...] = yx
+    yx_ref[...] = yx.astype(bf16)
     mixer = y_ref[...] + yx + rows_ref[1:2] * actx_ref[...].astype(f32)
     z = z_ref[...].astype(f32)
     gated = mixer * (z * jax.nn.sigmoid(z))
@@ -416,7 +416,7 @@
     scale = lax.rsqrt(cols[:, 0:1] * rows_ref[2:3, 0:1] + norm_epsilon)
     cross = cols[:, 1:2] * scale * scale * scale * rows_ref[2:3, 0:1]
     x = actx_ref[...].astype(f32)
-    mixer = y_ref[...] + yx_ref[...] + rows_ref[1:2] * x
+    mixer = y_ref[...] + yx_ref[...].astype(f32) + rows_ref[1:2] * x
     z = z_ref[...].astype(f32)
     sig = jax.nn.sigmoid(z)
     silu = z * sig
@@ -514,19 +514,23 @@
     dui = du_ref[...]
     du = dui + du_inter
     dy = dy_ref[...].astype(f32)
-    dprex_ref[...] = (du * dt_wide + rows_ref[1:2] * dy) * slopex_ref[...].astype(f32)
+    dprex_ref[...] = (
+        (du * dt_wide + rows_ref[1:2] * dy) * slopex_ref[...].astype(f32)
+    ).astype(bf16)
     db = dbc_ref[:, 0:N] + mm(uw, low, ((1,), (1,)))
-    dprep_ref[:, 0:N] = db * slopep_ref[:, 0:N].astype(f32)
-    dprep_ref[:, N : 2 * N] = dbc_ref[:, N : 2 * N] * slopep_ref[:, N : 2 * N].astype(f32)
+    dprep_ref[:, 0:N] = (db * slopep_ref[:, 0:N].astype(f32)).astype(bf16)
+    dprep_ref[:, N : 2 * N] = (
+        dbc_ref[:, N : 2 * N] * slopep_ref[:, N : 2 * N].astype(f32)
+    ).astype(bf16)
 
     @pl.when(b == 0)
     def _():
-        edge_ref[:, 0:GW] = dprex_ref[0:8]
-        edge_ref[:, GW:] = dprep_ref[0:8]
+        edge_ref[:, 0:GW] = dprex_ref[0:16].astype(f32)[0:8]
+        edge_ref[:, GW:] = dprep_ref[0:16].astype(f32)[0:8]
 
     sel = pick_heads(GW)
     ddt = mm_ones(sel, x * du, ((1,), (0,)), True)
-    later = mm_ones(sel, dy * (y_ref[...] + yx_ref[...]) - ub * dui, ((1,), (0,)), True)
+    later = mm_ones(sel, dy * (y_ref[...] + yx_ref[...].astype(f32)) - ub * dui, ((1,), (0,)), True)
     earlier = mm_ones(sel, u32 * du_inter, ((1,), (0,)), True)
     over = jnp.sum(grown * states_ref[0].astype(f32), axis=0, keepdims=True)
     over = mm(jnp.broadcast_to(over, (8, GW)), sel, ((1,), (0,)), highest)[0:1] * jnp.exp(total)
@@ -558,15 +562,16 @@
         gain_ref[...] = jnp.zeros_like(gain_ref)
 
     def conv(dpre, following, halo, raw, cw, ext, grad):
-        ext[0:Q] = dpre[...]
-        ext[Q : Q + 8] = jnp.where(last, halo, following[...])
+        here = dpre[...].astype(f32)
+        ext[0:Q] = here
+        ext[Q : Q + 8] = jnp.where(last, halo, following[...].astype(f32)[0:8])
         value = raw[...].astype(f32)
         total = jnp.zeros(dpre.shape, f32)
         for k in range(KW):
             shifted = ext[KW - 1 - k : KW - 1 - k + Q]
             total = total + cw[k : k + 1, :] * shifted
             grad[k : k + 1] += jnp.sum(value * shifted, axis=0, keepdims=True)
-        grad[KW : KW + 1] += jnp.sum(dpre[...], axis=0, keepdims=True)
+        grad[KW : KW + 1] += jnp.sum(here, axis=0, keepdims=True)
         return total.astype(bf16)
 
     GW = dprex_ref.shape[1]
@@ -1064,7 +1069,7 @@
         ]
         + [fixed(N + 8, GW)] * (F - 1),
         [rows_of(GW), per_block(N, GW), across],
-        [struct((TL, GW), f32), struct((blocks, N, GW), bf16), struct((8, TL), f32)],
+        [struct((TL, GW), bf16), struct((blocks, N, GW), bf16), struct((8, TL), f32)],
         [pltpu.VMEM((8, GW), f32), pltpu.VMEM((N, GW), f32)],
     )(spot, actx, actp, cum, total, local, y_intra, gate, back_normed, wide_rows, *finals)
 
@@ -1175,7 +1180,7 @@
         + [fixed(N, GW)] * (F - 1),
         [rows_of(GW), rows_of(NP), rows_of(8), fixed(8, 8), fixed(8, GW + NP)],
         [
-            struct((TL, GW), f32), struct((TL, NP), f32), struct((TL, 8), f32),
+            struct((TL, GW), bf16), struct((TL, NP), bf16), struct((TL, 8), f32),
             struct((8, 8), f32), struct((8, GW + NP), f32),
         ],
         [pltpu.VMEM((8, GW), f32), pltpu.VMEM((N, GW), f32)],
@@ -1187,7 +1192,7 @@
 
     def following(width):
         return pl.BlockSpec(
-            (8, width), lambda i, p: (jnp.minimum((i + 1) * (Q // 8), TL // 8 - 1), 0)
+            (16, width), lambda i, p: (jnp.minimum((i + 1) * (Q // 16), TL // 16 - 1), 0)
         )
 
     (

time: 527 us -> 526 us (level)
  no operation moved by 1% of the time
where the time goes in v3:
time: 526 us; the launch traced here: 524 us
  waiting for transfers between devices  223 us (42%)
  Pallas kernels  142 us (27%)
  starting transfers between devices  114 us (22%)
  other arithmetic  24.3 us (5%)
  local copies, waits for them, and re-layouts  19.6 us (4%)
    ppermute x24, waiting for transfers between devices, from_line(): return lax.ppermute(value, 'fsdp', [(i, (i + k) % F) for i in range(F)])  94.1 us
    ppermute x29, waiting for transfers between devices, from_part(): return lax.ppermute(value, 'seq', [(i, i ^ k * R) for i in range(S)])  79.8 us
    ppermute x24, starting transfers between devices, from_line(): return lax.ppermute(value, 'fsdp', [(i, (i + k) % F) for i in range(F)])  48.9 us
    ppermute x29, starting transfers between devices, from_part(): return lax.ppermute(value, 'seq', [(i, i ^ k * R) for i in range(S)])  36.5 us
    all_to_all x1, waiting for transfers between devices, spread(): return lax.all_to_all(copies, axis, 0, 0, tiled=True)  19 us
    pallas_call x4, Pallas kernels, by_line(): call(functools.partial(sum_kernel, F), F, [block] * len(arrays), [fixed(r...  18 us
    pallas_call x2, Pallas kernels, partial_sums(): call(functools.partial(partial_blocks_kernel, F, pairs), F, [fixed(TL, GW...  16.7 us
    ppermute x3, waiting for transfers between devices, line_chain(): down = lax.ppermute(down, 'fsdp', [(i, i - 1) for i in range(1, F - k + 1)])  16.2 us
  transfers between devices with their start and end apart: 74, of which 29 were waited for; matrix products, arithmetic and copies ran while one was open for 7% of the time, Pallas kernels for 20%

profile of v3, /device:TPU:0, one launch (start us, length us, event | category | flops | bytes accessed | tf_op | source)
XLA Modules:
  0.0 524.0 jit_solution(17520705221393178725)
XLA Ops:
  4.8 5.6 %collective-permute-start = (bf16[128,1536]{1,0:T(8,128)(2,1)S(1)}, bf16[128,1536]{1,0:T(8,128)(2,1)S(1)}, u32[]{:S(2)}, u32[]{:S(2)}) collective-permute-start(bf16[128,1536]{1,0:T(8,128)(2,1)S(1)} %fusion.2), channel_id=1, source_target_pairs={{0,1},{1,2},{2,3},{4,5},{5,6},{6,7},{8,9},{9,10},{10,11},{12,13},{... | collective-permute-start | bytes 1179656 | tf_op jit(solution)/shard_map/ppermute | solution.py:823
  22.3 17.2 %collective-permute-done.9 = bf16[168,384]{1,0:T(8,128)(2,1)S(1)} collective-permute-done((bf16[168,384]{1,0:T(8,128)(2,1)}, bf16[168,384]{1,0:T(8,128)(2,1)S(1)}, u32[]{:S(2)}, u32[]{:S(2)}) %collective-permute-start.9) | collective-permute-done | bytes 129056 | tf_op jit(solution)/shard_map/ppermute | solution.py:815
  39.5 11.6 %collective-permute-start.10 = (bf16[168,384]{1,0:T(8,128)(2,1)}, bf16[168,384]{1,0:T(8,128)(2,1)S(1)}, u32[]{:S(2)}, u32[]{:S(2)}) collective-permute-start(bf16[168,384]{1,0:T(8,128)(2,1)} %get-tuple-element.111), channel_id=1, source_target_pairs={{0,2},{1,3},{2,0},{3,1},{4,6},{5,7},{6,4},{7,5},{8,10},{9,11},{10,... | collective-permute-start | bytes 387080 | tf_op jit(solution)/shard_map/ppermute | solution.py:815
  51.0 5.1 collective-permute-done.10
  63.4 6.9 %collective-permute-start.22 = (bf16[192,384]{1,0:T(8,128)(2,1)}, bf16[192,384]{1,0:T(8,128)(2,1)S(1)}, u32[]{:S(2)}, u32[]{:S(2)}) collective-permute-start(bf16[192,384]{1,0:T(8,128)(2,1)} %get-tuple-element.128), channel_id=1, source_target_pairs={{0,1},{1,2},{2,3},{3,0},{4,5},{5,6},{6,7},{7,4},{8,9},{9,10},{10,1... | collective-permute-start | bytes 442376 | tf_op jit(solution)/shard_map/ppermute | solution.py:815
  84.6 11.9 %collective-permute-done.5 = bf16[128,1536]{1,0:T(8,128)(2,1)S(1)} collective-permute-done((bf16[128,1536]{1,0:T(8,128)(2,1)S(1)}, bf16[128,1536]{1,0:T(8,128)(2,1)S(1)}, u32[]{:S(2)}, u32[]{:S(2)}) %collective-permute-start.5) | collective-permute-done | bytes 393248 | tf_op jit(solution)/shard_map/ppermute | solution.py:824
  129.7 6.2 %all-to-all-start = ((f32[32,8,128]{2,1,0:T(8,128)}), f32[32,8,128]{2,1,0:T(8,128)}, u32[]{:S(2)}, u32[]{:S(2)}) async-start(f32[32,8,128]{2,1,0:T(8,128)} %broadcast_in_dim.27), calls=%async_computation | async-start | bytes 262144 | tf_op jit(solution)/shard_map/all_to_all | solution.py:27
  137.4 19.0 %all-to-all-done = f32[32,8,128]{2,1,0:T(8,128)} async-done(((f32[32,8,128]{2,1,0:T(8,128)}), f32[32,8,128]{2,1,0:T(8,128)}, u32[]{:S(2)}, u32[]{:S(2)}) %all-to-all-start) | async-done | bytes 131104 | tf_op jit(solution)/shard_map/all_to_all | solution.py:27
  160.1 15.3 %shard_map.230 = (bf16[1024,1536]{1,0:T(8,128)(2,1)}, bf16[392,1536]{1,0:T(8,128)(2,1)}, bf16[256,1536]{1,0:T(8,128)(2,1)}, bf16[1024,384]{1,0:T(8,128)(2,1)}, b...) custom-call(s32[3]{0:T(128)} %pad_add_fusion.spot_ref, ...), custom_call_target="tpu_custom_call" | custom-call | tf_op jit(solution)/shard_map/pallas_call | solution.py:1015
  179.0 6.0 %shard_map.231.y_ref = f32[1024,384]{1,0:T(8,128)} custom-call(s32[3]{0:T(128)} %pad_add_fusion.spot_ref, bf16[1024,384]{1,0:T(8,128)(2,1)} %get-tuple-element.116.actx_ref, bf16[1024,256]{1,0:T(8,128)(2,1)} %get-tuple-element.117.actp_ref, f32[1024,8]{1,0:T(8,128)} %get-tuple-element.120.dt_ref, f32[1024,8]{1,0:T(8,128)} %get-tuple-element.118.cum_ref, ...), custom_call_target="tpu_custom_call" | custom-call | tf_op jit(solution)/shard_map/pallas_call | solution.py:1046
  185.1 9.3 %shard_map.232 = (bf16[1024,1536]{1,0:T(8,128)(2,1)}, bf16[384,1536]{1,0:T(8,128)(2,1)}, bf16[384,1536]{1,0:T(8,128)(2,1)}, bf16[1024,384]{1,0:T(8,128)(2,1)}, bf16[1024,384]{1,0:T(8,128)(2,1)}) custom-call(s32[3]{0:T(128)} %pad_add_fusion.spot_ref, bf16[512,1536]{1,0:T(8,128)(2,1)} %copy-done.2, bf16[512,1536]{1,0:T(8,128)(2,1)} %collective-permute-done.21.other_ref, ...), custom_call_target="tpu_custom_call" | custom-call | tf_op jit(solution)/shard_map/pallas_call | solution.py:1053
  195.2 6.9 %shard_map.233 = (bf16[1024,384]{1,0:T(8,128)(2,1)}, bf16[4,128,384]{2,1,0:T(8,128)(2,1)}, f32[8,1024]{1,0:T(8,128)}) custom-call(s32[3]{0:T(128)} %pad_add_fusion.spot_ref, bf16[1024,384]{1,0:T(8,128)(2,1)} %get-tuple-element.116.actx_ref, bf16[1024,256]{1,0:T(8,128)(2,1)} %get-tuple-element.117.actp_ref, f32[1024,8]{1,0:T(8,128)} %get-tuple-element.118.cum_ref, ...), custom_call_target="tpu_custom_call" | custom-call | tf_op jit(solution)/shard_map/pallas_call | solution.py:1063
  212.4 12.3 %shard_map.234 = (bf16[1024,384]{1,0:T(8,128)(2,1)}, bf16[1024,384]{1,0:T(8,128)(2,1)}, bf16[1024,384]{1,0:T(8,128)(2,1)}, f32[4,128,384]{2,1,0:T(8,128)}, f32[1...) custom-call(s32[3]{0:T(128)} %pad_add_fusion.spot_ref, ...), custom_call_target="tpu_custom_call" | custom-call | tf_op jit(solution)/shard_map/pallas_call | solution.py:1078
  224.7 8.7 %shard_map.240 = (bf16[4,192,384]{2,1,0:T(8,128)(2,1)}, bf16[4,192,384]{2,1,0:T(8,128)(2,1)}, bf16[4,192,384]{2,1,0:T(8,128)(2,1)}, bf16[4,192,384]{2,1,0:T(8,128)(2,1)}) custom-call(s32[3]{0:T(128)} %pad_add_fusion.spot_ref, bf16[1024,384]{1,0:T(8,128)(2,1)} %get-tuple-element.169.refs_0_, bf16[1024,384]{1,0:T(8,128)(2,1)} %get-tuple-element.158.bgate_ref.refs_1_, ...), custom_call_target="tpu_custom_call" | custom-call | tf_op jit(solution)/shard_map/pallas_call | solution.py:1125
  239.3 26.4 %collective-permute-done.41.refs_5_ = f32[128,384]{1,0:T(8,128)S(1)} collective-permute-done((f32[128,384]{1,0:T(8,128)S(1)}, f32[128,384]{1,0:T(8,128)S(1)}, u32[]{:S(2)}, u32[]{:S(2)}) %collective-permute-start.41) | collective-permute-done | bytes 196640 | tf_op jit(solution)/shard_map/ppermute | solution.py:812
  268.1 8.7 %shard_map.236 = (f32[1024,384]{1,0:T(8,128)}, f32[1024,256]{1,0:T(8,128)}) custom-call(s32[3]{0:T(128)} %pad_add_fusion.spot_ref, bf16[1024,384]{1,0:T(8,128)(2,1)} %get-tuple-element.116.actx_ref, bf16[1024,256]{1,0:T(8,128)(2,1)} %get-tuple-element.117.actp_ref, f32[1024,8]{1,0:T(8,128)} %get-tuple-element.120.dt_ref, ...), custom_call_target="tpu_custom_call" | custom-call | tf_op jit(solution)/shard_map/pallas_call | solution.py:1159
  277.6 10.9 %shard_map.237 = (bf16[1024,384]{1,0:T(8,128)(2,1)}, bf16[1024,256]{1,0:T(8,128)(2,1)}, f32[1024,8]{1,0:T(8,128)}, f32[8,8]{1,0:T(8,128)}, f32[8,640]{1,0:T(8,128)}) custom-call(s32[3]{0:T(128)} %pad_add_fusion.spot_ref, bf16[1024,384]{1,0:T(8,128)(2,1)} %get-tuple-element.116.actx_ref, bf16[1024,256]{1,0:T(8,128)(2,1)} %get-tuple-element.117.actp_ref, ...), custom_call_target="tpu_custom_call" | custom-call | tf_op jit(solution)/shard_map/pallas_call | solution.py:1170
  295.0 13.3 %shard_map.238 = (bf16[1024,384]{1,0:T(8,128)(2,1)}, bf16[1024,256]{1,0:T(8,128)(2,1)}, f32[8,384]{1,0:T(8,128)}, f32[8,256]{1,0:T(8,128)}, bf16[512,1536]{1,0:T...) custom-call(s32[3]{0:T(128)} %pad_add_fusion.spot_ref, ...), custom_call_target="tpu_custom_call" | custom-call | tf_op jit(solution)/shard_map/pallas_call | solution.py:1200
  308.2 8.0 %shard_map.243 = (bf16[4,168,384]{2,1,0:T(8,128)(2,1)}, bf16[4,168,384]{2,1,0:T(8,128)(2,1)}, bf16[4,168,384]{2,1,0:T(8,128)(2,1)}, bf16[4,168,384]{2,1,0:T(8,128)(2,1)}) custom-call(s32[3]{0:T(128)} %pad_add_fusion.spot_ref, bf16[1024,384]{1,0:T(8,128)(2,1)} %get-tuple-element.185.refs_0_, bf16[1024,1536]{1,0:T(8,128)(2,1)} %get-tuple-element.126.x_ref.refs_3_.refs_1_, ...), custom_call_target="tpu_custom_call" | custom-call | tf_op jit(solution)/shard_map/pallas_call | solution.py:1125
  330.0 8.7 %collective-permute-done.57 = f32[64,128]{1,0:T(8,128)S(1)} collective-permute-done((f32[64,128]{1,0:T(8,128)}, f32[64,128]{1,0:T(8,128)S(1)}, u32[]{:S(2)}, u32[]{:S(2)}) %collective-permute-start.57) | collective-permute-done | bytes 32800 | tf_op jit(solution)/shard_map/ppermute | solution.py:812
  349.3 8.8 %collective-permute-done.58 = f32[64,128]{1,0:T(8,128)S(1)} collective-permute-done((f32[64,128]{1,0:T(8,128)S(1)}, f32[64,128]{1,0:T(8,128)S(1)}, u32[]{:S(2)}, u32[]{:S(2)}) %collective-permute-start.58) | collective-permute-done | bytes 32800 | tf_op jit(solution)/shard_map/ppermute | solution.py:812
  369.0 8.1 %collective-permute-done.61 = f32[32,128]{1,0:T(8,128)S(1)} collective-permute-done((f32[32,128]{1,0:T(8,128)S(1)}, f32[32,128]{1,0:T(8,128)S(1)}, u32[]{:S(2)}, u32[]{:S(2)}) %collective-permute-start.61) | collective-permute-done | bytes 16416 | tf_op jit(solution)/shard_map/ppermute | solution.py:1240
  383.0 9.8 %collective-permute-done.54.refs_2_ = bf16[4,192,384]{2,1,0:T(8,128)(2,1)S(1)} collective-permute-done((bf16[4,192,384]{2,1,0:T(8,128)(2,1)S(1)}, bf16[4,192,384]{2,1,0:T(8,128)(2,1)S(1)}, u32[]{:S(2)}, u32[]{:S(2)}) %collective-permute-start.54) | collective-permute-done | bytes 589856 | tf_op jit(solution)/shard_map/ppermute | solution.py:812
  398.3 8.0 %collective-permute-done.71.refs_3_ = bf16[4,168,384]{2,1,0:T(8,128)(2,1)S(1)} collective-permute-done((bf16[4,168,384]{2,1,0:T(8,128)(2,1)}, bf16[4,168,384]{2,1,0:T(8,128)(2,1)S(1)}, u32[]{:S(2)}, u32[]{:S(2)}) %collective-permute-start.71) | collective-permute-done | bytes 516128 | tf_op jit(solution)/shard_map/ppermute | solution.py:812
  406.3 9.7 %collective-permute-done.70.refs_2_ = bf16[4,168,384]{2,1,0:T(8,128)(2,1)} collective-permute-done((bf16[4,168,384]{2,1,0:T(8,128)(2,1)}, bf16[4,168,384]{2,1,0:T(8,128)(2,1)}, u32[]{:S(2)}, u32[]{:S(2)}) %collective-permute-start.70) | collective-permute-done | bytes 516128 | tf_op jit(solution)/shard_map/ppermute | solution.py:812
  416.8 5.3 %collective-permute-start.62 = (f32[32,128]{1,0:T(8,128)S(1)}, f32[32,128]{1,0:T(8,128)S(1)}, u32[]{:S(2)}, u32[]{:S(2)}) collective-permute-start(f32[32,128]{1,0:T(8,128)S(1)} %add.123), channel_id=1, source_target_pairs={{0,2},{1,3},{2,0},{3,1},{4,6},{5,7},{6,4},{7,5},{8,10},{9,11},{10,... | collective-permute-start | bytes 49160 | tf_op jit(solution)/shard_map/ppermute | solution.py:1240
  444.7 16.8 %collective-permute-done.45 = bf16[128,1536]{1,0:T(8,128)(2,1)} collective-permute-done((bf16[128,1536]{1,0:T(8,128)(2,1)}, bf16[128,1536]{1,0:T(8,128)(2,1)}, u32[]{:S(2)}, u32[]{:S(2)}) %collective-permute-start.45) | collective-permute-done | bytes 393248 | tf_op jit(solution)/shard_map/ppermute | solution.py:815
  461.5 9.4 %collective-permute-start.38 = (bf16[128,1536]{1,0:T(8,128)(2,1)}, bf16[128,1536]{1,0:T(8,128)(2,1)S(1)}, u32[]{:S(2)}, u32[]{:S(2)}) collective-permute-start(bf16[128,1536]{1,0:T(8,128)(2,1)} %get-tuple-element.143), channel_id=1, source_target_pairs={{0,3},{1,0},{2,1},{3,2},{4,7},{5,4},{6,5},{7,6},{8,11},{9,8},{10,9... | collective-permute-start | bytes 1179656 | tf_op jit(solution)/shard_map/ppermute | solution.py:815
  472.7 21.7 %collective-permute-done.37 = bf16[128,1536]{1,0:T(8,128)(2,1)S(1)} collective-permute-done((bf16[128,1536]{1,0:T(8,128)(2,1)}, bf16[128,1536]{1,0:T(8,128)(2,1)S(1)}, u32[]{:S(2)}, u32[]{:S(2)}) %collective-permute-start.37) | collective-permute-done | bytes 393248 | tf_op jit(solution)/shard_map/ppermute | solution.py:815
  494.3 8.3 %collective-permute-done.38 = bf16[128,1536]{1,0:T(8,128)(2,1)S(1)} collective-permute-done((bf16[128,1536]{1,0:T(8,128)(2,1)}, bf16[128,1536]{1,0:T(8,128)(2,1)S(1)}, u32[]{:S(2)}, u32[]{:S(2)}) %collective-permute-start.38) | collective-permute-done | bytes 393248 | tf_op jit(solution)/shard_map/ppermute | solution.py:815
  507.4 7.9 %shard_map.245 = (f32[6448,384]{1,0:T(8,128)}, f32[3072,384]{1,0:T(8,128)}) custom-call(s32[3]{0:T(128)} %pad_add_fusion.spot_ref, bf16[4,192,384]{2,1,0:T(8,128)(2,1)} %copy-done.6, bf16[4,192,384]{2,1,0:T(8,128)(2,1)} %copy-done.5, bf16[4,192,384]{2,1,0:T(8,128)(2,1)} %copy-done.4, bf16[4,192,384]{2,1,0:T(8,128)(2,1)} %copy-done.3, ...), custom_call_target="tpu_custom_call" | custom-call | tf_op jit(solution)/shard_map/pallas_call | solution.py:1267
  516.5 7.4 %shard_map.246 = f32[6448,384]{1,0:T(8,128)} custom-call(s32[3]{0:T(128)} %pad_add_fusion.spot_ref, bf16[4,168,384]{2,1,0:T(8,128)(2,1)} %get-tuple-element.242.refs_0_, bf16[4,168,384]{2,1,0:T(8,128)(2,1)} %collective-permute-done.69.refs_1_, bf16[4,168,384]{2,1,0:T(8,128)(2,1)} %collective-permute-done.70.refs_2_, ...), custom_call_target="tpu_custom_call", output_to_operand_aliasing={{}: (6, {})} | custom-call | tf_op jit(solution)/shard_map/pallas_call | solution.py:1274
  (280 shorter events, 183.4 us)
Async XLA Ops:
  3.5 57.9 %collective-permute-start.3 = (bf16[128,1536]{1,0:T(8,128)(2,1)S(1)}, bf16[128,1536]{1,0:T(8,128)(2,1)S(1)}, u32[]{:S(2)}, u32[]{:S(2)}) collective-permute-start(bf16[128,1536]{1,0:T(8,128)(2,1)S(1)} %fusion.2), channel_id=1, source_target_pairs={{1,0},{2,1},{3,2},{5,4},{6,5},{7,6},{9,8},{10,9},{11,10},{13,12},{... | collective-permute-start | bytes 1179656 | tf_op jit(solution)/shard_map/ppermute | solution.py:824
  4.8 57.9 %collective-permute-start = (bf16[128,1536]{1,0:T(8,128)(2,1)S(1)}, bf16[128,1536]{1,0:T(8,128)(2,1)S(1)}, u32[]{:S(2)}, u32[]{:S(2)}) collective-permute-start(bf16[128,1536]{1,0:T(8,128)(2,1)S(1)} %fusion.2), channel_id=1, source_target_pairs={{0,1},{1,2},{2,3},{4,5},{5,6},{6,7},{8,9},{9,10},{10,11},{12,13},{... | collective-permute-start | bytes 1179656 | tf_op jit(solution)/shard_map/ppermute | solution.py:823
  10.4 53.0 %collective-permute-start.20 = (bf16[128,1536]{1,0:T(8,128)(2,1)}, bf16[128,1536]{1,0:T(8,128)(2,1)S(1)}, u32[]{:S(2)}, u32[]{:S(2)}) collective-permute-start(bf16[128,1536]{1,0:T(8,128)(2,1)} %param.25), channel_id=1, source_target_pairs={{0,3},{1,0},{2,1},{3,2},{4,7},{5,4},{6,5},{7,6},{8,11},{9,8},{10,9... | collective-permute-start | bytes 1179656 | tf_op jit(solution)/shard_map/ppermute | solution.py:815
  12.3 58.0 %collective-permute-start.19 = (bf16[128,1536]{1,0:T(8,128)(2,1)}, bf16[128,1536]{1,0:T(8,128)(2,1)S(1)}, u32[]{:S(2)}, u32[]{:S(2)}) collective-permute-start(bf16[128,1536]{1,0:T(8,128)(2,1)} %param.25), channel_id=1, source_target_pairs={{0,2},{1,3},{2,0},{3,1},{4,6},{5,7},{6,4},{7,5},{8,10},{9,11},{10,... | collective-permute-start | bytes 1179656 | tf_op jit(solution)/shard_map/ppermute | solution.py:815
  63.4 34.4 %collective-permute-start.22 = (bf16[192,384]{1,0:T(8,128)(2,1)}, bf16[192,384]{1,0:T(8,128)(2,1)S(1)}, u32[]{:S(2)}, u32[]{:S(2)}) collective-permute-start(bf16[192,384]{1,0:T(8,128)(2,1)} %get-tuple-element.128), channel_id=1, source_target_pairs={{0,1},{1,2},{2,3},{3,0},{4,5},{5,6},{6,7},{7,4},{8,9},{9,10},{10,1... | collective-permute-start | bytes 442376 | tf_op jit(solution)/shard_map/ppermute | solution.py:815
  70.3 29.8 %collective-permute-start.23 = (bf16[192,384]{1,0:T(8,128)(2,1)}, bf16[192,384]{1,0:T(8,128)(2,1)S(1)}, u32[]{:S(2)}, u32[]{:S(2)}) collective-permute-start(bf16[192,384]{1,0:T(8,128)(2,1)} %get-tuple-element.129), channel_id=1, source_target_pairs={{0,2},{1,3},{2,0},{3,1},{4,6},{5,7},{6,4},{7,5},{8,10},{9,11},{10,... | collective-permute-start | bytes 442376 | tf_op jit(solution)/shard_map/ppermute | solution.py:815
  75.1 25.6 %collective-permute-start.24 = (bf16[192,384]{1,0:T(8,128)(2,1)}, bf16[192,384]{1,0:T(8,128)(2,1)S(1)}, u32[]{:S(2)}, u32[]{:S(2)}) collective-permute-start(bf16[192,384]{1,0:T(8,128)(2,1)} %get-tuple-element.130), channel_id=1, source_target_pairs={{0,3},{1,0},{2,1},{3,2},{4,7},{5,4},{6,5},{7,6},{8,11},{9,8},{10,9... | collective-permute-start | bytes 442376 | tf_op jit(solution)/shard_map/ppermute | solution.py:815
  96.9 63.2 %collective-permute-start.6 = (bf16[512,1536]{1,0:T(8,128)(2,1)S(1)}, bf16[512,1536]{1,0:T(8,128)(2,1)}, u32[]{:S(2)}, u32[]{:S(2)}) collective-permute-start(bf16[512,1536]{1,0:T(8,128)(2,1)S(1)} %pad_maximum_fusion.2.mine_ref), channel_id=1, source_target_pairs={{0,4},{4,0},{8,12},{12,8},{16,20},{20,16},{24,28},{28,24},{1,5},{5... | collective-permute-start | bytes 4718600 | tf_op jit(solution)/shard_map/ppermute | solution.py:809
  97.6 87.5 %collective-permute-start.21 = (bf16[512,1536]{1,0:T(8,128)(2,1)S(1)}, bf16[512,1536]{1,0:T(8,128)(2,1)}, u32[]{:S(2)}, u32[]{:S(2)}) collective-permute-start(bf16[512,1536]{1,0:T(8,128)(2,1)S(1)} %pad_maximum_fusion.3.mine_ref), channel_id=1, source_target_pairs={{0,4},{4,0},{8,12},{12,8},{16,20},{20,16},{24,28},{28,24},{1,5},{5... | collective-permute-start | bytes 4718600 | tf_op jit(solution)/shard_map/ppermute | solution.py:809
  124.8 52.7 %collective-permute-start.27 = (bf16[4,192,384]{2,1,0:T(8,128)(2,1)}, bf16[4,192,384]{2,1,0:T(8,128)(2,1)}, u32[]{:S(2)}, u32[]{:S(2)}) collective-permute-start(bf16[4,192,384]{2,1,0:T(8,128)(2,1)} %pad_maximum_fusion.4.refs_0_), channel_id=1, source_target_pairs={{0,24},{4,28},{8,16},{12,20},{16,8},{20,12},{24,0},{28,4},{1,25},{... | collective-permute-start | bytes 1769480 | tf_op jit(solution)/shard_map/ppermute | solution.py:812
  126.3 51.7 %collective-permute-start.26 = (bf16[4,192,384]{2,1,0:T(8,128)(2,1)}, bf16[4,192,384]{2,1,0:T(8,128)(2,1)}, u32[]{:S(2)}, u32[]{:S(2)}) collective-permute-start(bf16[4,192,384]{2,1,0:T(8,128)(2,1)} %pad_maximum_fusion.4.refs_0_), channel_id=1, source_target_pairs={{0,16},{4,20},{8,24},{12,28},{16,0},{20,4},{24,8},{28,12},{1,17},{... | collective-permute-start | bytes 1769480 | tf_op jit(solution)/shard_map/ppermute | solution.py:812
  128.1 56.9 %collective-permute-start.25 = (bf16[4,192,384]{2,1,0:T(8,128)(2,1)}, bf16[4,192,384]{2,1,0:T(8,128)(2,1)}, u32[]{:S(2)}, u32[]{:S(2)}) collective-permute-start(bf16[4,192,384]{2,1,0:T(8,128)(2,1)} %pad_maximum_fusion.4.refs_0_), channel_id=1, source_target_pairs={{0,8},{4,12},{8,0},{12,4},{16,24},{20,28},{24,16},{28,20},{1,9},{5... | collective-permute-start | bytes 1769480 | tf_op jit(solution)/shard_map/ppermute | solution.py:812
  129.7 26.7 %all-to-all-start = ((f32[32,8,128]{2,1,0:T(8,128)}), f32[32,8,128]{2,1,0:T(8,128)}, u32[]{:S(2)}, u32[]{:S(2)}) async-start(f32[32,8,128]{2,1,0:T(8,128)} %broadcast_in_dim.27), calls=%async_computation | async-start | bytes 262144 | tf_op jit(solution)/shard_map/all_to_all | solution.py:27
  233.4 84.6 %collective-permute-start.47 = (bf16[4,192,384]{2,1,0:T(8,128)(2,1)}, bf16[4,192,384]{2,1,0:T(8,128)(2,1)S(1)}, u32[]{:S(2)}, u32[]{:S(2)}) collective-permute-start(bf16[4,192,384]{2,1,0:T(8,128)(2,1)} %get-tuple-element.172), channel_id=1, source_target_pairs={{0,8},{4,12},{8,0},{12,4},{16,24},{20,28},{24,16},{28,20},{1,9},{5... | collective-permute-start | bytes 1769480 | tf_op jit(solution)/shard_map/ppermute | solution.py:812
  234.4 85.3 %collective-permute-start.48 = (bf16[4,192,384]{2,1,0:T(8,128)(2,1)}, bf16[4,192,384]{2,1,0:T(8,128)(2,1)S(1)}, u32[]{:S(2)}, u32[]{:S(2)}) collective-permute-start(bf16[4,192,384]{2,1,0:T(8,128)(2,1)} %get-tuple-element.173), channel_id=1, source_target_pairs={{0,16},{4,20},{8,24},{12,28},{16,0},{20,4},{24,8},{28,12},{1,17},{... | collective-permute-start | bytes 1769480 | tf_op jit(solution)/shard_map/ppermute | solution.py:812
  235.9 83.8 %collective-permute-start.49 = (bf16[4,192,384]{2,1,0:T(8,128)(2,1)}, bf16[4,192,384]{2,1,0:T(8,128)(2,1)S(1)}, u32[]{:S(2)}, u32[]{:S(2)}) collective-permute-start(bf16[4,192,384]{2,1,0:T(8,128)(2,1)} %get-tuple-element.174), channel_id=1, source_target_pairs={{0,24},{4,28},{8,16},{12,20},{16,8},{20,12},{24,0},{28,4},{1,25},{... | collective-permute-start | bytes 1769480 | tf_op jit(solution)/shard_map/ppermute | solution.py:812
  236.9 28.8 %collective-permute-start.41 = (f32[128,384]{1,0:T(8,128)S(1)}, f32[128,384]{1,0:T(8,128)S(1)}, u32[]{:S(2)}, u32[]{:S(2)}) collective-permute-start(f32[128,384]{1,0:T(8,128)S(1)} %copy-done.41), channel_id=1, source_target_pairs={{0,24},{4,28},{8,16},{12,20},{16,8},{20,12},{24,0},{28,4},{1,25},{... | collective-permute-start | bytes 589832 | tf_op jit(solution)/shard_map/ppermute | solution.py:812
  238.8 38.0 %collective-permute-start.40 = (f32[128,384]{1,0:T(8,128)S(1)}, f32[128,384]{1,0:T(8,128)S(1)}, u32[]{:S(2)}, u32[]{:S(2)}) collective-permute-start(f32[128,384]{1,0:T(8,128)S(1)} %copy-done.41), channel_id=1, source_target_pairs={{0,16},{4,20},{8,24},{12,28},{16,0},{20,4},{24,8},{28,12},{1,17},{... | collective-permute-start | bytes 589832 | tf_op jit(solution)/shard_map/ppermute | solution.py:812
  316.2 42.0 %collective-permute-start.63 = (bf16[4,168,384]{2,1,0:T(8,128)(2,1)}, bf16[4,168,384]{2,1,0:T(8,128)(2,1)S(1)}, u32[]{:S(2)}, u32[]{:S(2)}) collective-permute-start(bf16[4,168,384]{2,1,0:T(8,128)(2,1)} %get-tuple-element.188), channel_id=1, source_target_pairs={{0,8},{4,12},{8,0},{12,4},{16,24},{20,28},{24,16},{28,20},{1,9},{5... | collective-permute-start | bytes 1548296 | tf_op jit(solution)/shard_map/ppermute | solution.py:812
  318.1 40.2 %collective-permute-start.64 = (bf16[4,168,384]{2,1,0:T(8,128)(2,1)}, bf16[4,168,384]{2,1,0:T(8,128)(2,1)S(1)}, u32[]{:S(2)}, u32[]{:S(2)}) collective-permute-start(bf16[4,168,384]{2,1,0:T(8,128)(2,1)} %get-tuple-element.189), channel_id=1, source_target_pairs={{0,16},{4,20},{8,24},{12,28},{16,0},{20,4},{24,8},{28,12},{1,17},{... | collective-permute-start | bytes 1548296 | tf_op jit(solution)/shard_map/ppermute | solution.py:812
  318.1 40.2 %collective-permute-start.65 = (bf16[4,168,384]{2,1,0:T(8,128)(2,1)}, bf16[4,168,384]{2,1,0:T(8,128)(2,1)}, u32[]{:S(2)}, u32[]{:S(2)}) collective-permute-start(bf16[4,168,384]{2,1,0:T(8,128)(2,1)} %get-tuple-element.190), channel_id=1, source_target_pairs={{0,24},{4,28},{8,16},{12,20},{16,8},{20,12},{24,0},{28,4},{1,25},{... | collective-permute-start | bytes 1548296 | tf_op jit(solution)/shard_map/ppermute | solution.py:812
  347.2 35.1 %collective-permute-start.55 = (bf16[4,192,384]{2,1,0:T(8,128)(2,1)S(1)}, bf16[4,192,384]{2,1,0:T(8,128)(2,1)S(1)}, u32[]{:S(2)}, u32[]{:S(2)}) collective-permute-start(bf16[4,192,384]{2,1,0:T(8,128)(2,1)S(1)} %get-tuple-element.195.refs_0_), channel_id=1, source_target_pairs={{0,24},{4,28},{8,16},{12,20},{16,8},{20,12},{24,0},{28,4},{1,25},{... | collective-permute-start | bytes 1769480 | tf_op jit(solution)/shard_map/ppermute | solution.py:812
  377.0 48.6 %collective-permute-start.43 = (bf16[512,1536]{1,0:T(8,128)(2,1)}, bf16[512,1536]{1,0:T(8,128)(2,1)}, u32[]{:S(2)}, u32[]{:S(2)}) collective-permute-start(bf16[512,1536]{1,0:T(8,128)(2,1)} %get-tuple-element.164), channel_id=1, source_target_pairs={{0,4},{4,0},{8,12},{12,8},{16,20},{20,16},{24,28},{28,24},{1,5},{5... | collective-permute-start | bytes 4718600 | tf_op jit(solution)/shard_map/ppermute | solution.py:809
  377.1 57.1 %collective-permute-start.35 = (bf16[512,1536]{1,0:T(8,128)(2,1)}, bf16[512,1536]{1,0:T(8,128)(2,1)}, u32[]{:S(2)}, u32[]{:S(2)}) collective-permute-start(bf16[512,1536]{1,0:T(8,128)(2,1)} %get-tuple-element.139), channel_id=1, source_target_pairs={{0,4},{4,0},{8,12},{12,8},{16,20},{20,16},{24,28},{28,24},{1,5},{5... | collective-permute-start | bytes 4718600 | tf_op jit(solution)/shard_map/ppermute | solution.py:809
  382.3 24.0 %collective-permute-start.71 = (bf16[4,168,384]{2,1,0:T(8,128)(2,1)}, bf16[4,168,384]{2,1,0:T(8,128)(2,1)S(1)}, u32[]{:S(2)}, u32[]{:S(2)}) collective-permute-start(bf16[4,168,384]{2,1,0:T(8,128)(2,1)} %get-tuple-element.242.refs_0_), channel_id=1, source_target_pairs={{0,24},{4,28},{8,16},{12,20},{16,8},{20,12},{24,0},{28,4},{1,25},{... | collective-permute-start | bytes 1548296 | tf_op jit(solution)/shard_map/ppermute | solution.py:812
  406.3 99.1 %collective-permute-start.56 = (bf16[4,4,192,384]{3,2,1,0:T(8,128)(2,1)}, bf16[4,4,192,384]{3,2,1,0:T(8,128)(2,1)S(1)}, u32[]{:S(2)}, u32[]{:S(2)}) collective-permute-start(bf16[4,4,192,384]{3,2,1,0:T(8,128)(2,1)} %pad_maximum_fusion), channel_id=1, source_target_pairs={{0,4},{4,0},{8,12},{12,8},{16,20},{20,16},{24,28},{28,24},{1,5},{5... | collective-permute-start | bytes 7077896 | tf_op jit(solution)/shard_map/ppermute | solution.py:809
  425.1 91.4 %collective-permute-start.72 = (bf16[4,4,168,384]{3,2,1,0:T(8,128)(2,1)}, bf16[4,4,168,384]{3,2,1,0:T(8,128)(2,1)}, u32[]{:S(2)}, u32[]{:S(2)}) collective-permute-start(bf16[4,4,168,384]{3,2,1,0:T(8,128)(2,1)} %pad_maximum_fusion.1), channel_id=1, source_target_pairs={{0,4},{4,0},{8,12},{12,8},{16,20},{20,16},{24,28},{28,24},{1,5},{5... | collective-permute-start | bytes 6193160 | tf_op jit(solution)/shard_map/ppermute | solution.py:809
  431.4 30.1 %collective-permute-start.45 = (bf16[128,1536]{1,0:T(8,128)(2,1)}, bf16[128,1536]{1,0:T(8,128)(2,1)}, u32[]{:S(2)}, u32[]{:S(2)}) collective-permute-start(bf16[128,1536]{1,0:T(8,128)(2,1)} %get-tuple-element.167), channel_id=1, source_target_pairs={{0,2},{1,3},{2,0},{3,1},{4,6},{5,7},{6,4},{7,5},{8,10},{9,11},{10,... | collective-permute-start | bytes 1179656 | tf_op jit(solution)/shard_map/ppermute | solution.py:815
  434.2 27.3 %collective-permute-start.46 = (bf16[128,1536]{1,0:T(8,128)(2,1)}, bf16[128,1536]{1,0:T(8,128)(2,1)}, u32[]{:S(2)}, u32[]{:S(2)}) collective-permute-start(bf16[128,1536]{1,0:T(8,128)(2,1)} %get-tuple-element.168), channel_id=1, source_target_pairs={{0,3},{1,0},{2,1},{3,2},{4,7},{5,4},{6,5},{7,6},{8,11},{9,8},{10,9... | collective-permute-start | bytes 1179656 | tf_op jit(solution)/shard_map/ppermute | solution.py:815
  444.7 28.0 %collective-permute-start.36 = (bf16[128,1536]{1,0:T(8,128)(2,1)}, bf16[128,1536]{1,0:T(8,128)(2,1)S(1)}, u32[]{:S(2)}, u32[]{:S(2)}) collective-permute-start(bf16[128,1536]{1,0:T(8,128)(2,1)} %get-tuple-element.141), channel_id=1, source_target_pairs={{0,1},{1,2},{2,3},{3,0},{4,5},{5,6},{6,7},{7,4},{8,9},{9,10},{10,1... | collective-permute-start | bytes 1179656 | tf_op jit(solution)/shard_map/ppermute | solution.py:815
  461.5 32.8 %collective-permute-start.37 = (bf16[128,1536]{1,0:T(8,128)(2,1)}, bf16[128,1536]{1,0:T(8,128)(2,1)S(1)}, u32[]{:S(2)}, u32[]{:S(2)}) collective-permute-start(bf16[128,1536]{1,0:T(8,128)(2,1)} %get-tuple-element.142), channel_id=1, source_target_pairs={{0,2},{1,3},{2,0},{3,1},{4,6},{5,7},{6,4},{7,5},{8,10},{9,11},{10,... | collective-permute-start | bytes 1179656 | tf_op jit(solution)/shard_map/ppermute | solution.py:815
  461.5 41.2 %collective-permute-start.38 = (bf16[128,1536]{1,0:T(8,128)(2,1)}, bf16[128,1536]{1,0:T(8,128)(2,1)S(1)}, u32[]{:S(2)}, u32[]{:S(2)}) collective-permute-start(bf16[128,1536]{1,0:T(8,128)(2,1)} %get-tuple-element.143), channel_id=1, source_target_pairs={{0,3},{1,0},{2,1},{3,2},{4,7},{5,4},{6,5},{7,6},{8,11},{9,8},{10,9... | collective-permute-start | bytes 1179656 | tf_op jit(solution)/shard_map/ppermute | solution.py:815
  (84 other events, 1344.1 us)
